TPU v7x, 256 devices: a whole 4x4x8 slice. The times are simulated.
256 devices in a mesh: grp: 8 (over y, x_hi), tp: 32 (over z, x_lo, core).
Axes of the slice: x: 4 (x_hi: 2, x_lo: 2; x = x_hi * 2 + x_lo), y: 4, z: 8, core: 2. Of those that a mesh axis runs over, the one named last changes fastest.
Arguments:
- key_cache: bfloat16 [8, 32, 768, 512], P('grp', 'tp'), may hold values from -6 to 6
- value_cache: bfloat16 [8, 32, 768, 512], P('grp', 'tp'), may hold values from -12 to 12
- lengths: int32 [8, 32], P('grp', 'tp'), may hold values from 256 to 768, as said below
- queries: bfloat16 [8, 1, 32, 8192], P('grp', None, 'tp'), may hold values from -12 to 12
- new_keys: bfloat16 [8, 1, 32, 512], P('grp', None, 'tp'), may hold values from -18 to 18
- new_values: bfloat16 [8, 1, 32, 512], P('grp', None, 'tp'), may hold values from -12 to 12
- residual: bfloat16 [8, 1, 32, 8192], P('grp', None, 'tp'), may hold values from -4 to 4
- norm_gain: float32 [8192], replicated, may hold values from 0.25 to 1.75
- gate_weight: bfloat16 [8, 6656, 8192], P('grp', 'tp'), may hold values from -0.0625 to 0.0625
- up_weight: bfloat16 [8, 6656, 8192], P('grp', 'tp'), may hold values from -0.0625 to 0.0625
- down_weight: bfloat16 [8, 6656, 8192], P('grp', 'tp'), may hold values from -0.0390625 to 0.0390625
Outputs:
- mixed: bfloat16 [8, 1, 32, 8192], P('grp', None, 'tp')
Inputs may be any that keep to these rules, and one draw needn't show every extreme that they name: `lengths`: some row has exactly 768 valid positions.
All inputs are finite; a program needn't handle non-finite values.
Results may differ from a plain program's by a relative error of at most 0.005.
Values may be sent and summed in bfloat16 or wider, within the bound.
No kernel may reach another device: no remote copies, remote signals or barrier semaphores. Data moves between devices by JAX's collectives and lax.ppermute only.
A program may use at most 64 MiB of HBM per device.

v0:
```python
import jax
import jax.numpy as jnp
from jax import lax
from jax.sharding import Mesh
from jax.sharding import PartitionSpec as P

HEADS = 64
HD = 128
KVH = 4
TP = ("tp_0", "tp_1", "tp_2")


masked_score = -1e30


def in_order(pieces, dim):
    pieces = jnp.moveaxis(pieces, 0, dim)
    dims = pieces.shape
    return pieces.reshape(*dims[:dim], dims[dim] * dims[dim + 1], *dims[dim + 2 :])


def sent_to_all(value, axis):
    copies = jnp.broadcast_to(value, (lax.axis_size(axis), *value.shape))
    return lax.all_to_all(copies, axis, split_axis=0, concat_axis=0, tiled=True)


def collect(value, axis, dim):
    return in_order(sent_to_all(value, axis), dim)


def split_up(value, dim, size):
    before, after = (value.shape[:dim], value.shape[dim + 1 :])
    return jnp.moveaxis(value.reshape(*before, size, -1, *after), dim, 0)


def sum_at_owner(value, axis, dim):
    pieces = split_up(value, dim, lax.axis_size(axis))
    arrived = lax.all_to_all(pieces, axis, split_axis=0, concat_axis=0, tiled=True)
    return arrived.sum(axis=0)


def summed_rows(value, axes, dim):
    far, near = axes
    own = sum_at_owner(split_up(value, dim, lax.axis_size(far)), near, dim + 1)
    return jnp.sum(lax.all_to_all(own, far, 0, 0, tiled=True), axis=0)


def feed_rows(normed_rows, gate_weight, up_weight, down_weight):
    numbers = (((1,), (1,)), ((), ()))
    gate_part = lax.dot_general(
        normed_rows, gate_weight[0], numbers, preferred_element_type=jnp.float32
    )
    up_part = lax.dot_general(
        normed_rows, up_weight[0], numbers, preferred_element_type=jnp.float32
    )
    product = (jax.nn.silu(gate_part) * up_part).astype(jnp.bfloat16)
    return jnp.dot(product, down_weight[0], preferred_element_type=jnp.float32)


def local(
    key_cache,
    value_cache,
    lengths,
    queries,
    new_keys,
    new_values,
    residual,
    norm_gain,
    gate_weight,
    up_weight,
    down_weight,
):
    groups = lax.axis_size("grp")
    members = lax.axis_size(TP)
    serving = lax.axis_index("grp") < groups // 2
    step_count = queries.shape[1]
    own_rows = queries.shape[2]
    model_width = queries.shape[3]
    head_share = HEADS // KVH
    slot_count = key_cache.shape[2]
    score_scale = HD ** (-0.5)
    own_heads = queries[0].reshape(step_count, own_rows, KVH, head_share, HD)
    cache_keys = key_cache[0].reshape(own_rows, slot_count, KVH, HD)
    cache_values = value_cache[0].reshape(own_rows, slot_count, KVH, HD)
    positions = jnp.arange(slot_count)
    usable = positions[None, :] < lengths[0][:, None]
    usable_mask = usable[None, :, None, None, :]
    cache_scores = (
        jnp.einsum("srjgd,rpjd->srjgp", own_heads, cache_keys, preferred_element_type=jnp.float32)
        * score_scale
    )
    cache_scores = jnp.where(usable_mask, cache_scores, masked_score)
    fresh_keys = new_keys[0].reshape(step_count, own_rows, KVH, HD)
    fresh_values = new_values[0].reshape(step_count, own_rows, KVH, HD)
    fresh_scores = (
        jnp.einsum("srjgd,trjd->srjgt", own_heads, fresh_keys, preferred_element_type=jnp.float32)
        * score_scale
    )
    causal = jnp.arange(step_count)[:, None] >= jnp.arange(step_count)[None, :]
    causal_mask = causal[:, None, None, None, :]
    fresh_scores = jnp.where(causal_mask, fresh_scores, masked_score)
    ceiling = jnp.maximum(jnp.max(cache_scores, axis=-1), jnp.max(fresh_scores, axis=-1))
    cache_exp = jnp.where(usable_mask, jnp.exp(cache_scores - ceiling[..., None]), 0.0)
    fresh_exp = jnp.where(causal_mask, jnp.exp(fresh_scores - ceiling[..., None]), 0.0)
    denominator = jnp.sum(cache_exp, axis=-1) + jnp.sum(fresh_exp, axis=-1)
    cache_weighted = jnp.einsum(
        "srjgp,rpjd->srjgd",
        cache_exp.astype(jnp.bfloat16),
        cache_values,
        preferred_element_type=jnp.float32,
    )
    fresh_weighted = jnp.einsum(
        "srjgt,trjd->srjgd",
        fresh_exp.astype(jnp.bfloat16),
        fresh_values,
        preferred_element_type=jnp.float32,
    )
    attended = (cache_weighted + fresh_weighted) / denominator[..., None]
    attended = attended.reshape(step_count, own_rows, model_width)
    hidden = residual[0].astype(jnp.float32) + attended
    spread_sq = jnp.mean(hidden * hidden, axis=-1, keepdims=True)
    normed = (hidden * lax.rsqrt(spread_sq + 1e-05) * norm_gain).astype(jnp.bfloat16)
    block_rows = step_count * own_rows
    flat_rows = normed.reshape(block_rows, model_width)
    ffn_first = groups // 2
    group_block = collect(flat_rows, TP, 0).reshape(members, block_rows, model_width)
    all_rows = lax.all_gather(group_block, "grp", axis=1, tiled=True)
    real_rows = all_rows[:, : ffn_first * block_rows].reshape(
        members * ffn_first * block_rows, model_width
    )
    within = summed_rows(
        lax.cond(
            serving,
            lambda operand: jnp.zeros(
                (ffn_first * block_rows * lax.axis_size(TP), model_width), jnp.float32
            ),
            lambda operand: feed_rows(operand, gate_weight, up_weight, down_weight),
            real_rows,
        ),
        (("tp_0", "tp_1"), "tp_2"),
        0,
    )
    padded = jnp.concatenate(
        [within, jnp.zeros(((groups - ffn_first) * block_rows, model_width), jnp.float32)], 0
    )
    summed = sum_at_owner(padded, "grp", 0)
    mixed = (hidden + summed.reshape(step_count, own_rows, model_width)).astype(jnp.bfloat16)
    mixed = jnp.where(serving, mixed, jnp.zeros_like(mixed))
    return mixed[None]


def solution(mesh):
    finer = Mesh(mesh.devices.reshape(mesh.shape["grp"], 8, 2, 2), ("grp", "tp_0", "tp_1", "tp_2"))
    in_specs = (
        P("grp", TP, None, None),
        P("grp", TP, None, None),
        P("grp", TP),
        P("grp", None, TP, None),
        P("grp", None, TP, None),
        P("grp", None, TP, None),
        P("grp", None, TP, None),
        P(),
        P("grp", TP, None),
        P("grp", TP, None),
        P("grp", TP, None),
    )
    out_specs = P("grp", None, TP, None)
    return jax.shard_map(local, mesh=finer, in_specs=in_specs, out_specs=out_specs, check_vma=False)
```

profile of v0, /device:TPU:24, one launch (start us, length us, event | category | flops | bytes accessed | tf_op | source)
XLA Modules:
  0.0 241.5 jit_solution(11971909050703647324)
XLA Ops:
  6.5 0.0 copy-start
  6.5 0.0 copy-start.1
  6.5 0.0 copy-start.3
  6.5 0.0 all-gather.2.cloned.1.call-start
  7.3 0.7 convert.12
  8.0 0.8 convert_element_type.47
  8.8 1.8 reshape.147
  10.5 0.0 copy-done
  10.5 0.1 reduce.5
  10.6 0.8 fusion.37
  11.4 0.4 fusion.41
  11.8 0.2 fusion.28
  12.1 0.0 copy-done.1
  12.1 0.2 reshape.151
  12.2 0.9 fusion.36
  13.8 0.0 copy-done.3
  13.9 0.9 broadcast_in_dim.51
  14.8 0.5 broadcast.47
  15.3 3.8 %reduce.6 = bf16[32,8192]{1,0:T(8,128)(2,1)S(1)} reduce(bf16[32,1,8192]{2,1,0:T(2,128)(2,1)S(1)} %broadcast_in_dim.51, bf16[]{:T(256)} %broadcast.47), dimensions={1}, to_apply=%broadcast_in_dim.51.reduce_sub_computation | reduce | bytes 1048578 | tf_op jit(solution)/shard_map/broadcast_in_dim | solution.py:23
  19.1 0.4 reshape.166
  19.5 27.6 %all_to_all.20 = bf16[32,2,4096]{2,1,0:T(2,128)(2,1)S(1)} all-to-all(bf16[32,2,4096]{2,1,0:T(2,128)(2,1)S(1)} %reshape.166), channel_id=1, replica_groups=mesh['grp'=8,'tp_0'=8,'tp_1'=2,'tp_2'=2] {'tp_0','tp_1','tp_2'}, dimensions={0} | all-to-all | bytes 1048576 | tf_op jit(solution)/shard_map/all_to_all | solution.py:24
  47.1 0.5 reshape.167
  47.7 1.4 copy.37
  49.0 0.0 all-gather.2.cloned.1.call-update
  49.1 70.9 %all-gather.2.cloned.1.call-done = bf16[32,8,8192]{2,0,1:T(8,128)(2,1)} async-done(((bf16[32,1,8192]{2,0,1:T(8,128)(2,1)}), bf16[32,8,8192]{2,0,1:T(8,128)(2,1)}) %all-gather.2.cloned.1.call-update) | async-done | bytes 4194320 | tf_op jit(solution)/shard_map/all_gather | solution.py:127
  120.0 20.2 %conditional.1 = (f32[128,8192]{1,0:T(8,128)}) conditional(s32[]{:T(128)} %convert_element_type.50, (bf16[1,208,8192]{2,1,0:T(8,128)(2,1)}, bf16[32,8,8192]{2,0,1:T(8,128)(2,1)}, bf16[1,208,8192]{2,1,0:T(8,128)(2,1)}, bf16[1,208,8192]{2,1,0:T(8,128)(2,1)}) %tuple.11, () %tuple.12), branch_computations={%region_3.4_spmd, %region_4.5_spmd} | conditional | flops 1308782592 | bytes 35602440 | solution.py:132
  120.0 4.5 %copy.38 = bf16[32,8,8192]{2,1,0:T(8,128)(2,1)S(1)} copy(bf16[32,8,8192]{2,0,1:T(8,128)(2,1)} %get-tuple-element.45) | data formatting | bytes 8388608 | tf_op jit(solution)/shard_map
  124.5 2.4 slice.5
  126.8 2.5 %reshape.158 = bf16[128,8192]{1,0:T(8,128)(2,1)S(1)} reshape(bf16[32,4,8192]{2,1,0:T(4,128)(2,1)} %slice.5) | data formatting | bytes 4194304 | tf_op jit(solution)/shard_map/reshape | solution.py:128
  129.4 3.0 %fusion.4 = f32[128,208]{0,1:T(8,128)S(1)} fusion(bf16[128,8192]{1,0:T(8,128)(2,1)S(1)} %reshape.158, bf16[1,208,8192]{2,1,0:T(8,128)(2,1)} %get-tuple-element.24), kind=kOutput, calls=%fused_computation.4 | convolution fusion | flops 436207616 | bytes 5611520 | tf_op jit(solution)/shard_map/cond/branch_0_fun/dot_general | solution.py:50
  132.4 7.8 %fusion = f32[128,8192]{1,0:T(8,128)} fusion(bf16[1,208,8192]{2,1,0:T(8,128)(2,1)} %get-tuple-element.27, bf16[128,8192]{1,0:T(8,128)(2,1)S(1)} %reshape.158, bf16[1,208,8192]{2,1,0:T(8,128)(2,1)} %get-tuple-element.26, f32[128,208]{0,1:T(8,128)S(1)} %fusion.4), kind=kOutput, calls=%fused_computation | convolution fusion | flops 872574976 | bytes 13213696 | tf_op jit(solution)/shard_map/cond/branch_0_fun/dot_general | solution.py:57
  140.2 5.2 %reshape_reshape.3 = f32[16,2,4,8192]{3,2,1,0:T(4,128)} reshape(f32[128,8192]{1,0:T(8,128)} %get-tuple-element.54) | data formatting | bytes 8388608 | tf_op jit(solution)/shard_map/reshape;reshape | solution.py:33
  145.4 2.5 %copy.39 = f32[2,16,4,8192]{3,2,1,0:T(4,128)S(1)} copy(f32[2,16,4,8192]{3,2,0,1:T(4,128)} %bitcast.67) | data formatting | bytes 8388608 | tf_op jit(solution)/shard_map/transpose | solution.py:33
  147.9 8.2 %all_to_all.21 = f32[2,16,4,8192]{3,2,1,0:T(4,128)} all-to-all(f32[2,16,4,8192]{3,2,1,0:T(4,128)S(1)} %copy.39), channel_id=1, replica_groups=mesh['grp'=8,'tp_0'=8,'tp_1'=2,'tp_2'=2] {'tp_2'}, dimensions={0} | all-to-all | bytes 8388608 | tf_op jit(solution)/shard_map/all_to_all | solution.py:38
  156.0 4.0 %reduce_sum.51 = f32[16,4,8192]{2,1,0:T(4,128)S(1)} reduce(f32[2,16,4,8192]{3,2,1,0:T(4,128)} %all_to_all.21, f32[]{:T(128)} %constant.30.clone.1), dimensions={0}, to_apply=%region_5.6 | reduce | flops 524288 | bytes 6291460 | tf_op jit(solution)/shard_map/reduce_sum | solution.py:39
  160.0 0.0 copy-start.2
  160.0 58.7 %all_to_all.22 = f32[16,4,8192]{2,1,0:T(4,128)} all-to-all(f32[16,4,8192]{2,1,0:T(4,128)S(1)} %reduce_sum.51), channel_id=1, replica_groups=mesh['grp'=8,'tp_0'=8,'tp_1'=2,'tp_2'=2] {'tp_0','tp_1'}, dimensions={0} | all-to-all | bytes 4194304 | tf_op jit(solution)/shard_map/all_to_all | solution.py:45
  218.7 1.9 reduce_sum.52
  220.6 0.3 copy.41
  220.9 12.8 %all_to_all.23 = f32[8,1,8192]{2,1,0:T(1,128)S(1)} all-to-all(f32[8,1,8192]{2,1,0:T(1,128)S(1)} %copy.41), channel_id=1, replica_groups=mesh['grp'=8,'tp_0'=8,'tp_1'=2,'tp_2'=2] {'grp'}, dimensions={0} | all-to-all | bytes 524288 | tf_op jit(solution)/shard_map/all_to_all | solution.py:38
  233.8 0.2 reduce_sum.53
  234.0 0.0 copy-done.2
  234.0 0.7 broadcast_select_fusion
  (5 shorter events, 0.1 us)
Async XLA Ops:
  6.5 4.0 %copy-start = (bf16[1,1,1,8192]{3,2,1,0:T(2,128)(2,1)S(1)}, bf16[1,1,1,8192]{3,2,1,0:T(2,128)(2,1)}, u32[]{:S(2)}) copy-start(bf16[1,1,1,8192]{3,2,1,0:T(2,128)(2,1)} %param.16) | copy-start | bytes 49156
  6.5 5.5 %copy-start.1 = (bf16[1,1,768,512]{3,2,1,0:T(8,128)(2,1)S(1)}, bf16[1,1,768,512]{3,2,1,0:T(8,128)(2,1)}, u32[]{:S(2)}) copy-start(bf16[1,1,768,512]{3,2,1,0:T(8,128)(2,1)} %param.14) | copy-start | bytes 2359300
  6.5 7.3 %copy-start.3 = (f32[8192]{0:T(1024)S(1)}, f32[8192]{0:T(1024)}, u32[]{:S(2)}) copy-start(f32[8192]{0:T(1024)} %param.20) | copy-start | bytes 98308
  6.5 113.5 %all-gather.2.cloned.1.call-start = ((), (), s32[]{:S(2)}) async-start(), calls=%async_computation.4 | async-start | bytes 4718592 | tf_op jit(solution)/shard_map/all_gather | solution.py:127
  160.0 73.9 %copy-start.2 = (bf16[1,1,1,8192]{3,2,1,0:T(2,128)(2,1)S(1)}, bf16[1,1,1,8192]{3,2,1,0:T(2,128)(2,1)}, u32[]{:S(2)}) copy-start(bf16[1,1,1,8192]{3,2,1,0:T(2,128)(2,1)} %param.19) | copy-start | bytes 49156
Sparse Core Ops, SparseCore 0:
  49.2 70.7 all-gather.1
where the time goes:
time: 243 us; the launch traced here: 241 us
  blocking collectives  107 us (44%)
  waiting for transfers between devices  70.9 us (29%)
  local copies, waits for them, and re-layouts  23 us (9%)
  between operations  15 us (6%)
  matrix products  12.9 us (5%)
  other arithmetic  12.4 us (5%)
    all_gather x1, waiting for transfers between devices, local(): all_rows = lax.all_gather(group_block, 'grp', axis=1, tiled=True)  70.9 us
    all_to_all x1, blocking collectives, summed_rows(): return jnp.sum(lax.all_to_all(own, far, 0, 0, tiled=True), axis=0)  58.7 us
    all_to_all x1, blocking collectives, sent_to_all(): return lax.all_to_all(copies, axis, split_axis=0, concat_axis=0, tiled=True)  27.6 us
    all_to_all x2, blocking collectives, sum_at_owner(): lax.all_to_all(pieces, axis, split_axis=0, concat_axis=0, tiled=True)  21 us
    dot_general x1, matrix products, feed_rows(): return jnp.dot(product, down_weight[0], preferred_element_type=jnp.float32)  7.81 us
    another operation x3, local copies, waits for them, and re-layouts  6.41 us
    another operation x1, local copies, waits for them, and re-layouts, split_up(): return jnp.moveaxis(value.reshape(*before, size, -1, *after), dim, 0)  5.17 us
  transfers between devices with their start and end apart: 1, of which 1 were waited for; matrix products, arithmetic and copies ran while one was open for 0% of the time, Pallas kernels for 0%

commit v1 on v0

v1 whole, which is shorter than its diff:
```python
import jax
import jax.numpy as jnp
from jax import lax
from jax.sharding import Mesh
from jax.sharding import PartitionSpec as P

HEADS = 64
HD = 128
KVH = 4
X = ("xh", "xl")
GRP = ("y", "xh")
TP = ("z", "xl", "c")


masked_score = -1e30


def shifted(value, axes, hops):
    size = lax.axis_size(axes)
    return lax.ppermute(value, axes, [(i, (i + hops) % size) for i in range(size)])


def mirrored(value):
    return lax.ppermute(value, "y", [(i, 3 - i) for i in range(4)])


def opposite(value):
    return lax.ppermute(value, "y", [(i, (i + 2) % 4) for i in range(4)])


def gathered_rows(row):
    pair = jnp.concatenate([mirrored(row), opposite(row)], 0)
    planes, width = pair.shape
    depth = lax.axis_size("z")
    along_z = lax.all_to_all(
        jnp.broadcast_to(pair[None], (depth, planes, width)), "z", 0, 0, tiled=True
    ).reshape(depth * planes, width)
    near = [along_z] + [shifted(along_z, X, k) for k in (1, 2, 3)]
    half = jnp.concatenate(near, 0)
    return jnp.concatenate([half, shifted(half, "c", 1)], 0)


def returned_rows(partial):
    rows, width = partial.shape
    half = rows // 2
    other = shifted(partial[half:].astype(jnp.bfloat16), "c", 1)
    half_sum = partial[:half] + other.astype(jnp.float32)
    quarter = half // 4
    own = half_sum[:quarter]
    for k in (1, 2, 3):
        piece = half_sum[k * quarter : (k + 1) * quarter].astype(jnp.bfloat16)
        own = own + shifted(piece, X, -k).astype(jnp.float32)
    depth = lax.axis_size("z")
    pieces = own.astype(jnp.bfloat16).reshape(depth, quarter // depth, width)
    arrived = lax.all_to_all(pieces, "z", 0, 0, tiled=True)
    pair = jnp.sum(arrived.astype(jnp.float32), axis=0)
    return mirrored(pair[:1]) + opposite(pair[1:])


def feed_rows(normed_rows, gate_weight, up_weight, down_weight):
    numbers = (((1,), (1,)), ((), ()))
    gate_part = lax.dot_general(
        normed_rows, gate_weight[0], numbers, preferred_element_type=jnp.float32
    )
    up_part = lax.dot_general(
        normed_rows, up_weight[0], numbers, preferred_element_type=jnp.float32
    )
    product = (jax.nn.silu(gate_part) * up_part).astype(jnp.bfloat16)
    return jnp.dot(product, down_weight[0], preferred_element_type=jnp.float32)


def local(
    key_cache,
    value_cache,
    lengths,
    queries,
    new_keys,
    new_values,
    residual,
    norm_gain,
    gate_weight,
    up_weight,
    down_weight,
):
    serving = lax.axis_index("y") < lax.axis_size("y") // 2
    step_count = queries.shape[1]
    own_rows = queries.shape[2]
    model_width = queries.shape[3]
    head_share = HEADS // KVH
    slot_count = key_cache.shape[2]
    score_scale = HD ** (-0.5)
    own_heads = queries[0].reshape(step_count, own_rows, KVH, head_share, HD)
    cache_keys = key_cache[0].reshape(own_rows, slot_count, KVH, HD)
    cache_values = value_cache[0].reshape(own_rows, slot_count, KVH, HD)
    positions = jnp.arange(slot_count)
    usable = positions[None, :] < lengths[0][:, None]
    usable_mask = usable[None, :, None, None, :]
    cache_scores = (
        jnp.einsum("srjgd,rpjd->srjgp", own_heads, cache_keys, preferred_element_type=jnp.float32)
        * score_scale
    )
    cache_scores = jnp.where(usable_mask, cache_scores, masked_score)
    fresh_keys = new_keys[0].reshape(step_count, own_rows, KVH, HD)
    fresh_values = new_values[0].reshape(step_count, own_rows, KVH, HD)
    fresh_scores = (
        jnp.einsum("srjgd,trjd->srjgt", own_heads, fresh_keys, preferred_element_type=jnp.float32)
        * score_scale
    )
    causal = jnp.arange(step_count)[:, None] >= jnp.arange(step_count)[None, :]
    causal_mask = causal[:, None, None, None, :]
    fresh_scores = jnp.where(causal_mask, fresh_scores, masked_score)
    ceiling = jnp.maximum(jnp.max(cache_scores, axis=-1), jnp.max(fresh_scores, axis=-1))
    cache_exp = jnp.where(usable_mask, jnp.exp(cache_scores - ceiling[..., None]), 0.0)
    fresh_exp = jnp.where(causal_mask, jnp.exp(fresh_scores - ceiling[..., None]), 0.0)
    denominator = jnp.sum(cache_exp, axis=-1) + jnp.sum(fresh_exp, axis=-1)
    cache_weighted = jnp.einsum(
        "srjgp,rpjd->srjgd",
        cache_exp.astype(jnp.bfloat16),
        cache_values,
        preferred_element_type=jnp.float32,
    )
    fresh_weighted = jnp.einsum(
        "srjgt,trjd->srjgd",
        fresh_exp.astype(jnp.bfloat16),
        fresh_values,
        preferred_element_type=jnp.float32,
    )
    attended = (cache_weighted + fresh_weighted) / denominator[..., None]
    attended = attended.reshape(step_count, own_rows, model_width)
    hidden = residual[0].astype(jnp.float32) + attended
    spread_sq = jnp.mean(hidden * hidden, axis=-1, keepdims=True)
    normed = (hidden * lax.rsqrt(spread_sq + 1e-05) * norm_gain).astype(jnp.bfloat16)
    flat_rows = normed.reshape(step_count * own_rows, model_width)
    all_rows = gathered_rows(flat_rows)
    summed = returned_rows(feed_rows(all_rows, gate_weight, up_weight, down_weight))
    mixed = (hidden + summed.reshape(step_count, own_rows, model_width)).astype(jnp.bfloat16)
    mixed = jnp.where(serving, mixed, jnp.zeros_like(mixed))
    return mixed[None]


def solution(mesh):
    finer = Mesh(mesh.devices.reshape(4, 2, 8, 2, 2), ("y", "xh", "z", "xl", "c"))
    in_specs = (
        P(GRP, TP, None, None),
        P(GRP, TP, None, None),
        P(GRP, TP),
        P(GRP, None, TP, None),
        P(GRP, None, TP, None),
        P(GRP, None, TP, None),
        P(GRP, None, TP, None),
        P(),
        P(GRP, TP, None),
        P(GRP, TP, None),
        P(GRP, TP, None),
    )
    out_specs = P(GRP, None, TP, None)
    return jax.shard_map(local, mesh=finer, in_specs=in_specs, out_specs=out_specs, check_vma=False)
```

time: 243 us -> 120 us (0.49)
  blocking collectives: 107 us -> 32.9 us
  waiting for transfers between devices: 70.9 us -> 35.3 us
  starting transfers between devices: 0.01 us -> 15.9 us
  between operations: 15 us -> 1.69 us
  local copies, waits for them, and re-layouts: 23 us -> 14.4 us
  other arithmetic: 12.4 us -> 6.59 us
    all_to_all x4 -> x2, blocking collectives: 107 us -> 32.9 us  [the longest x1 17.2 us: gathered_rows(): lax.all_to_all(jnp.broadcast_to(pair[None], (depth, planes, width)), 'z',...]
    all_gather x1 -> x0, waiting for transfers between devices: 70.9 us -> none  [local(): all_rows = lax.all_gather(group_block, 'grp', axis=1, tiled=True)]
    ppermute x0 -> x12, waiting for transfers between devices: none -> 35.3 us  [the longest x8 25.2 us: shifted(): lax.ppermute(value, axes, [(i, (i + hops) % size) for i in range(size)])]
    ppermute x0 -> x12, starting transfers between devices: none -> 15.9 us  [the longest x8 10.2 us: shifted(): lax.ppermute(value, axes, [(i, (i + hops) % size) for i in range(size)])]
    another operation x4 -> x2, local copies, waits for them, and re-layouts: 11.6 us -> 5.03 us
    reduce_sum x3 -> x1, other arithmetic: 6.11 us -> 0.22 us  [returned_rows(): pair = jnp.sum(arrived.astype(jnp.float32), axis=0)]
    broadcast_in_dim x1 -> x0, other arithmetic: 3.81 us -> none  [sent_to_all(): copies = jnp.broadcast_to(value, (lax.axis_size(axis), *value.shape))]
    transpose x1 -> x0, local copies, waits for them, and re-layouts: 2.47 us -> none  [split_up(): return jnp.moveaxis(value.reshape(*before, size, -1, *after), dim, 0)]
  transfers between devices with their start and end apart: 1 -> 12, of which waited for: 1 -> 10; matrix products, arithmetic and copies ran while one was open for 0% -> 1% of each run, Pallas kernels for 0% -> 0%
where the time goes in v1:
time: 120 us
  waiting for transfers between devices  35.3 us (29%)
  blocking collectives  32.9 us (27%)
  starting transfers between devices  15.9 us (13%)
  local copies, waits for them, and re-layouts  14.4 us (12%)
  matrix products  12.9 us (11%)
  other arithmetic  6.59 us (5%)
  between operations  1.69 us (1%)
    ppermute x8, waiting for transfers between devices, shifted(): lax.ppermute(value, axes, [(i, (i + hops) % size) for i in range(size)])  25.2 us
    all_to_all x1, blocking collectives, gathered_rows(): lax.all_to_all(jnp.broadcast_to(pair[None], (depth, planes, width)), 'z',...  17.2 us
    all_to_all x1, blocking collectives, returned_rows(): arrived = lax.all_to_all(pieces, 'z', 0, 0, tiled=True)  15.6 us
    ppermute x8, starting transfers between devices, shifted(): lax.ppermute(value, axes, [(i, (i + hops) % size) for i in range(size)])  10.2 us
    dot_general x1, matrix products, feed_rows(): return jnp.dot(product, down_weight[0], preferred_element_type=jnp.float32)  7.39 us
    ppermute x2, waiting for transfers between devices, opposite(): return lax.ppermute(value, 'y', [(i, (i + 2) % 4) for i in range(4)])  5.35 us
    another operation x2, local copies, waits for them, and re-layouts  5.03 us
    ppermute x2, starting transfers between devices, mirrored(): return lax.ppermute(value, 'y', [(i, 3 - i) for i in range(4)])  4.84 us
  transfers between devices with their start and end apart: 12, of which 10 were waited for; matrix products, arithmetic and copies ran while one was open for 1% of the time, Pallas kernels for 0%

profile of v1, /device:TPU:24, one launch (start us, length us, event | category | flops | bytes accessed | tf_op | source)
XLA Modules:
  0.0 119.7 jit_solution(14308502603401596878)
XLA Ops:
  0.8 2.6 %reshape.146 = bf16[768,4,128]{2,1,0:T(4,128)(2,1)} reshape(bf16[1,1,768,512]{3,2,1,0:T(8,128)(2,1)} %param.11) | data formatting | bytes 1572864 | tf_op jit(solution)/shard_map/reshape.3
  3.4 0.8 reduce.4
  4.3 0.8 fusion.31
  5.1 1.5 %fusion.39 = (f32[4,16]{1,0:T(4,128)S(1)}, f32[1,1,4,16,768]{4,3,2,0,1:T(8,128)S(1)}) fusion(bf16[4,16,128]{2,1,0:T(8,128)(2,1)S(1)} %bitcast.72, bf16[768,4,128]{2,1,0:T(4,128)(2,1)} %reshape.146, pred[768]{0:T(1024)(128)(4,1)S(1)} %iota_compare_fusion), kind=kOutput, calls=%fused_computation.57 | convolution fusion | flops 12730304 | bytes 1000448 | tf_op jit(solution)/shard_map/srjgd,rpjd->srjgp/dot_general | solution.py:99
  6.6 0.7 copy-done.3
  7.3 0.2 fusion.16
  7.6 2.4 %reshape.150 = bf16[768,4,128]{2,1,0:T(4,128)(2,1)} reshape(bf16[1,1,768,512]{3,2,1,0:T(8,128)(2,1)} %param.12) | data formatting | bytes 1572864 | tf_op jit(solution)/shard_map/reshape.18
  10.0 2.1 %fusion.30 = (f32[]{:T(128)}, f32[1,4,128,1,16]{2,4,1,3,0:T(8,128)S(1)}) fusion(f32[1,1,4,16,128]{4,3,2,0,1:T(8,128)S(1)} %bitcast.69, f32[4,16]{1,0:T(4,128)S(1)} %get-tuple-element.13, f32[4,128]{1,0:T(4,128)S(1)} %bitcast.75, f32[4,16]{1,0:T(4,128)S(1)} %get-tuple-element.12, bf16[768,4,128]{2,1,0:T(4,128)(2,1)} %reshape.150, ...), kind=kOutput, calls=%fused_computation.38 | convolution fusion | flops 12779519 | bytes 1052164 | tf_op jit(solution)/shard_map/srjgp,rpjd->srjgd/dot_general | solution.py:116
  12.8 0.8 multiply_convert_fusion.2
  13.6 2.0 %collective-permute-start = (bf16[1,8192]{1,0:T(2,128)(2,1)S(1)}, bf16[1,8192]{1,0:T(2,128)(2,1)S(1)}, u32[]{:S(2)}, u32[]{:S(2)}) collective-permute-start(bf16[1,8192]{1,0:T(2,128)(2,1)S(1)} %reshape.154), channel_id=1, source_target_pairs={{0,192},{64,128},{128,64},{192,0},{1,193},{65,129},{129,65},{193,1... | collective-permute-start | bytes 49160 | tf_op jit(solution)/shard_map/ppermute | solution.py:24
  15.7 0.9 collective-permute-start.1
  16.5 2.3 %collective-permute-done = bf16[1,8192]{1,0:T(2,128)(2,1)S(1)} collective-permute-done((bf16[1,8192]{1,0:T(2,128)(2,1)S(1)}, bf16[1,8192]{1,0:T(2,128)(2,1)S(1)}, u32[]{:S(2)}, u32[]{:S(2)}) %collective-permute-start) | collective-permute-done | bytes 16416 | tf_op jit(solution)/shard_map/ppermute | solution.py:24
  18.8 2.3 %collective-permute-done.1 = bf16[1,8192]{1,0:T(2,128)(2,1)S(1)} collective-permute-done((bf16[1,8192]{1,0:T(2,128)(2,1)S(1)}, bf16[1,8192]{1,0:T(2,128)(2,1)S(1)}, u32[]{:S(2)}, u32[]{:S(2)}) %collective-permute-start.1) | collective-permute-done | bytes 16416 | tf_op jit(solution)/shard_map/ppermute | solution.py:28
  21.1 0.1 pad_maximum_fusion.1
  21.2 0.1 broadcast_in_dim.53
  21.3 17.2 %all_to_all.10 = bf16[8,2,8192]{2,1,0:T(2,128)(2,1)} all-to-all(bf16[8,2,8192]{2,1,0:T(2,128)(2,1)S(1)} %broadcast_in_dim.53), channel_id=1, replica_groups=mesh['y'=4,'xh'=2,'z'=8,'xl'=2,'c'=2] {'z'}, dimensions={0} | all-to-all | bytes 524288 | tf_op jit(solution)/shard_map/all_to_all | solution.py:35
  38.6 1.8 %reshape.155 = bf16[16,8192]{1,0:T(8,128)(2,1)} reshape(bf16[8,2,8192]{2,1,0:T(2,128)(2,1)} %all_to_all.10) | data formatting | bytes 524288 | tf_op jit(solution)/shard_map/reshape | solution.py:37
  40.3 1.5 %collective-permute-start.2 = (bf16[16,8192]{1,0:T(8,128)(2,1)}, bf16[16,8192]{1,0:T(8,128)(2,1)S(1)}, u32[]{:S(2)}, u32[]{:S(2)}) collective-permute-start(bf16[16,8192]{1,0:T(8,128)(2,1)} %reshape.155), channel_id=1, source_target_pairs={{0,2},{2,32},{32,34},{34,0},{1,3},{3,33},{33,35},{35,1},{4,6},{6,3... | collective-permute-start | bytes 786440 | tf_op jit(solution)/shard_map/ppermute | solution.py:20
  41.8 2.7 %collective-permute-start.3 = (bf16[16,8192]{1,0:T(8,128)(2,1)}, bf16[16,8192]{1,0:T(8,128)(2,1)S(1)}, u32[]{:S(2)}, u32[]{:S(2)}) collective-permute-start(bf16[16,8192]{1,0:T(8,128)(2,1)} %reshape.155), channel_id=1, source_target_pairs={{0,32},{2,34},{32,0},{34,2},{1,33},{3,35},{33,1},{35,3},{4,36},{6,... | collective-permute-start | bytes 786440 | tf_op jit(solution)/shard_map/ppermute | solution.py:20
  44.5 1.4 %collective-permute-start.4 = (bf16[16,8192]{1,0:T(8,128)(2,1)}, bf16[16,8192]{1,0:T(8,128)(2,1)S(1)}, u32[]{:S(2)}, u32[]{:S(2)}) collective-permute-start(bf16[16,8192]{1,0:T(8,128)(2,1)} %reshape.155), channel_id=1, source_target_pairs={{0,34},{2,0},{32,2},{34,32},{1,35},{3,1},{33,3},{35,33},{4,38},{6,... | collective-permute-start | bytes 786440 | tf_op jit(solution)/shard_map/ppermute | solution.py:20
  46.0 1.0 constant_dynamic-update-slice_fusion.4
  47.0 3.9 %collective-permute-done.2 = bf16[16,8192]{1,0:T(8,128)(2,1)S(1)} collective-permute-done((bf16[16,8192]{1,0:T(8,128)(2,1)}, bf16[16,8192]{1,0:T(8,128)(2,1)S(1)}, u32[]{:S(2)}, u32[]{:S(2)}) %collective-permute-start.2) | collective-permute-done | bytes 262176 | tf_op jit(solution)/shard_map/ppermute | solution.py:20
  50.9 2.8 %collective-permute-done.3 = bf16[16,8192]{1,0:T(8,128)(2,1)S(1)} collective-permute-done((bf16[16,8192]{1,0:T(8,128)(2,1)}, bf16[16,8192]{1,0:T(8,128)(2,1)S(1)}, u32[]{:S(2)}, u32[]{:S(2)}) %collective-permute-start.3) | collective-permute-done | bytes 262176 | tf_op jit(solution)/shard_map/ppermute | solution.py:20
  53.7 1.0 pad_maximum_fusion
  54.8 0.1 collective-permute-start.5
  54.9 2.6 %collective-permute-done.5 = bf16[64,8192]{1,0:T(8,128)(2,1)S(1)} collective-permute-done((bf16[64,8192]{1,0:T(8,128)(2,1)S(1)}, bf16[64,8192]{1,0:T(8,128)(2,1)S(1)}, u32[]{:S(2)}, u32[]{:S(2)}) %collective-permute-start.5) | collective-permute-done | bytes 1048608 | tf_op jit(solution)/shard_map/ppermute | solution.py:20
  57.5 0.1 constant_dynamic-update-slice_fusion
  57.6 1.3 %copy-done.1 = bf16[128,8192]{1,0:T(8,128)(2,1)} copy-done((bf16[128,8192]{1,0:T(8,128)(2,1)}, bf16[128,8192]{1,0:T(8,128)(2,1)S(1)}, u32[]{:S(2)}) %copy-start.1) | copy-done | bytes 2097176
  58.9 1.0 fusion.2
  60.0 7.4 %fusion = f32[128,8192]{1,0:T(8,128)} fusion(bf16[1,208,8192]{2,1,0:T(8,128)(2,1)S(1)} %copy-done, f32[128,208]{0,1:T(8,128)S(1)} %fusion.2, bf16[128,8192]{1,0:T(8,128)(2,1)} %copy-done.1, bf16[1,208,8192]{2,1,0:T(8,128)(2,1)} %param.19), kind=kOutput, calls=%fused_computation | convolution fusion | flops 872574976 | bytes 13213696 | tf_op jit(solution)/shard_map/dot_general | solution.py:69
  67.4 1.7 %slice.53 = bf16[64,8192]{1,0:T(8,128)(2,1)S(1)} slice(f32[128,8192]{1,0:T(8,128)} %fusion), slice={[64:128], [0:8192]} | slice | bytes 2097152 | tf_op jit(solution)/shard_map/slice | solution.py:46
  69.1 0.2 collective-permute-start.6
  69.3 2.5 %collective-permute-done.6 = bf16[64,8192]{1,0:T(8,128)(2,1)S(1)} collective-permute-done((bf16[64,8192]{1,0:T(8,128)(2,1)S(1)}, bf16[64,8192]{1,0:T(8,128)(2,1)S(1)}, u32[]{:S(2)}, u32[]{:S(2)}) %collective-permute-start.6) | collective-permute-done | bytes 1048608 | tf_op jit(solution)/shard_map/ppermute | solution.py:20
  71.8 1.9 %fusion.36 = (bf16[64,8192]{1,0:T(8,128)(2,1)S(1)}, f32[64,8192]{1,0:T(8,128)S(1)}) fusion(bf16[64,8192]{1,0:T(8,128)(2,1)S(1)} %collective-permute-done.6, f32[128,8192]{1,0:T(8,128)} %fusion), kind=kLoop, calls=%fused_computation.54 | loop fusion | flops 1572864 | bytes 6291456 | tf_op jit(solution)/shard_map/convert.8
  73.8 2.3 %collective-permute-start.7 = (bf16[16,8192]{1,0:T(8,128)(2,1)S(1)}, bf16[16,8192]{1,0:T(8,128)(2,1)S(1)}, u32[]{:S(2)}, u32[]{:S(2)}) collective-permute-start(bf16[16,8192]{1,0:T(8,128)(2,1)S(1)} %get-tuple-element.7), channel_id=1, source_target_pairs={{0,34},{2,0},{32,2},{34,32},{1,35},{3,1},{33,3},{35,33},{4,38},{6,... | collective-permute-start | bytes 786440 | tf_op jit(solution)/shard_map/ppermute | solution.py:20
  76.1 1.1 collective-permute-start.8
  77.2 0.7 collective-permute-start.9
  78.0 9.7 %collective-permute-done.7 = bf16[16,8192]{1,0:T(8,128)(2,1)S(1)} collective-permute-done((bf16[16,8192]{1,0:T(8,128)(2,1)S(1)}, bf16[16,8192]{1,0:T(8,128)(2,1)S(1)}, u32[]{:S(2)}, u32[]{:S(2)}) %collective-permute-start.7) | collective-permute-done | bytes 262176 | tf_op jit(solution)/shard_map/ppermute | solution.py:20
  87.6 3.7 %collective-permute-done.9 = bf16[16,8192]{1,0:T(8,128)(2,1)S(1)} collective-permute-done((bf16[16,8192]{1,0:T(8,128)(2,1)S(1)}, bf16[16,8192]{1,0:T(8,128)(2,1)S(1)}, u32[]{:S(2)}, u32[]{:S(2)}) %collective-permute-start.9) | collective-permute-done | bytes 262176 | tf_op jit(solution)/shard_map/ppermute | solution.py:20
  91.3 0.9 fusion.15
  92.1 1.8 %reshape.156 = bf16[8,2,8192]{2,1,0:T(2,128)(2,1)} reshape(bf16[16,8192]{1,0:T(8,128)(2,1)} %fusion.15) | data formatting | bytes 524288 | tf_op jit(solution)/shard_map/reshape | solution.py:54
  94.0 15.6 %all_to_all.11 = bf16[8,2,8192]{2,1,0:T(2,128)(2,1)S(1)} all-to-all(bf16[8,2,8192]{2,1,0:T(2,128)(2,1)} %reshape.156), channel_id=1, replica_groups=mesh['y'=4,'xh'=2,'z'=8,'xl'=2,'c'=2] {'z'}, dimensions={0} | all-to-all | bytes 524288 | tf_op jit(solution)/shard_map/all_to_all | solution.py:55
  109.6 0.2 convert_reduce_fusion
  109.9 0.7 fusion.38
  110.5 2.8 %collective-permute-start.10 = (f32[1,8192]{1,0:T(1,128)}, f32[1,8192]{1,0:T(1,128)S(1)}, u32[]{:S(2)}, u32[]{:S(2)}) collective-permute-start(f32[1,8192]{1,0:T(1,128)} %get-tuple-element.11), channel_id=1, source_target_pairs={{0,192},{64,128},{128,64},{192,0},{1,193},{65,129},{129,65},{193,1... | collective-permute-start | bytes 98312 | tf_op jit(solution)/shard_map/ppermute | solution.py:24
  113.4 2.5 %collective-permute-done.10 = f32[1,8192]{1,0:T(1,128)S(1)} collective-permute-done((f32[1,8192]{1,0:T(1,128)}, f32[1,8192]{1,0:T(1,128)S(1)}, u32[]{:S(2)}, u32[]{:S(2)}) %collective-permute-start.10) | collective-permute-done | bytes 32800 | tf_op jit(solution)/shard_map/ppermute | solution.py:24
  115.9 3.1 %collective-permute-done.11 = f32[1,8192]{1,0:T(1,128)S(1)} collective-permute-done((f32[1,8192]{1,0:T(1,128)}, f32[1,8192]{1,0:T(1,128)S(1)}, u32[]{:S(2)}, u32[]{:S(2)}) %collective-permute-start.11) | collective-permute-done | bytes 32800 | tf_op jit(solution)/shard_map/ppermute | solution.py:28
  119.0 0.7 broadcast_select_fusion
  (25 shorter events, 0.2 us)
Async XLA Ops:
  0.0 60.0 %copy-start = (bf16[1,208,8192]{2,1,0:T(8,128)(2,1)S(1)}, bf16[1,208,8192]{2,1,0:T(8,128)(2,1)}, u32[]{:S(2)}) copy-start(bf16[1,208,8192]{2,1,0:T(8,128)(2,1)} %param.21) | copy-start | bytes 10223620
  0.0 7.5 %copy-start.4 = (bf16[1,1,1,8192]{3,2,1,0:T(2,128)(2,1)S(1)}, bf16[1,1,1,8192]{3,2,1,0:T(2,128)(2,1)}, u32[]{:S(2)}) copy-start(bf16[1,1,1,8192]{3,2,1,0:T(2,128)(2,1)} %param.17) | copy-start | bytes 49156
  0.8 9.2 %copy-start.6 = (bf16[1,1,1,512]{3,2,1,0:T(2,128)(2,1)S(1)}, bf16[1,1,1,512]{3,2,1,0:T(2,128)(2,1)}, u32[]{:S(2)}) copy-start(bf16[1,1,1,512]{3,2,1,0:T(2,128)(2,1)} %param.16) | copy-start | bytes 3076
  6.6 0.7 copy-start.3
  13.6 5.2 %collective-permute-start = (bf16[1,8192]{1,0:T(2,128)(2,1)S(1)}, bf16[1,8192]{1,0:T(2,128)(2,1)S(1)}, u32[]{:S(2)}, u32[]{:S(2)}) collective-permute-start(bf16[1,8192]{1,0:T(2,128)(2,1)S(1)} %reshape.154), channel_id=1, source_target_pairs={{0,192},{64,128},{128,64},{192,0},{1,193},{65,129},{129,65},{193,1... | collective-permute-start | bytes 49160 | tf_op jit(solution)/shard_map/ppermute | solution.py:24
  15.7 5.4 %collective-permute-start.1 = (bf16[1,8192]{1,0:T(2,128)(2,1)S(1)}, bf16[1,8192]{1,0:T(2,128)(2,1)S(1)}, u32[]{:S(2)}, u32[]{:S(2)}) collective-permute-start(bf16[1,8192]{1,0:T(2,128)(2,1)S(1)} %reshape.154), channel_id=1, source_target_pairs={{0,128},{64,192},{128,0},{192,64},{1,129},{65,193},{129,1},{193,65... | collective-permute-start | bytes 49160 | tf_op jit(solution)/shard_map/ppermute | solution.py:28
  40.3 10.6 %collective-permute-start.2 = (bf16[16,8192]{1,0:T(8,128)(2,1)}, bf16[16,8192]{1,0:T(8,128)(2,1)S(1)}, u32[]{:S(2)}, u32[]{:S(2)}) collective-permute-start(bf16[16,8192]{1,0:T(8,128)(2,1)} %reshape.155), channel_id=1, source_target_pairs={{0,2},{2,32},{32,34},{34,0},{1,3},{3,33},{33,35},{35,1},{4,6},{6,3... | collective-permute-start | bytes 786440 | tf_op jit(solution)/shard_map/ppermute | solution.py:20
  41.8 11.9 %collective-permute-start.3 = (bf16[16,8192]{1,0:T(8,128)(2,1)}, bf16[16,8192]{1,0:T(8,128)(2,1)S(1)}, u32[]{:S(2)}, u32[]{:S(2)}) collective-permute-start(bf16[16,8192]{1,0:T(8,128)(2,1)} %reshape.155), channel_id=1, source_target_pairs={{0,32},{2,34},{32,0},{34,2},{1,33},{3,35},{33,1},{35,3},{4,36},{6,... | collective-permute-start | bytes 786440 | tf_op jit(solution)/shard_map/ppermute | solution.py:20
  44.5 9.2 %collective-permute-start.4 = (bf16[16,8192]{1,0:T(8,128)(2,1)}, bf16[16,8192]{1,0:T(8,128)(2,1)S(1)}, u32[]{:S(2)}, u32[]{:S(2)}) collective-permute-start(bf16[16,8192]{1,0:T(8,128)(2,1)} %reshape.155), channel_id=1, source_target_pairs={{0,34},{2,0},{32,2},{34,32},{1,35},{3,1},{33,3},{35,33},{4,38},{6,... | collective-permute-start | bytes 786440 | tf_op jit(solution)/shard_map/ppermute | solution.py:20
  54.8 4.2 %copy-start.2 = (bf16[1,208,8192]{2,1,0:T(8,128)(2,1)S(1)}, bf16[1,208,8192]{2,1,0:T(8,128)(2,1)}, u32[]{:S(2)}) copy-start(bf16[1,208,8192]{2,1,0:T(8,128)(2,1)} %param.20) | copy-start | bytes 10223620
  54.8 2.7 %collective-permute-start.5 = (bf16[64,8192]{1,0:T(8,128)(2,1)S(1)}, bf16[64,8192]{1,0:T(8,128)(2,1)S(1)}, u32[]{:S(2)}, u32[]{:S(2)}) collective-permute-start(bf16[64,8192]{1,0:T(8,128)(2,1)S(1)} %pad_maximum_fusion), channel_id=1, source_target_pairs={{0,1},{1,0},{2,3},{3,2},{4,5},{5,4},{6,7},{7,6},{8,9},{9,8},{10,11... | collective-permute-start | bytes 3145736 | tf_op jit(solution)/shard_map/ppermute | solution.py:20
  57.6 1.3 %copy-start.1 = (bf16[128,8192]{1,0:T(8,128)(2,1)}, bf16[128,8192]{1,0:T(8,128)(2,1)S(1)}, u32[]{:S(2)}) copy-start(bf16[128,8192]{1,0:T(8,128)(2,1)S(1)} %constant_dynamic-update-slice_fusion) | copy-start | bytes 6291460
  69.1 2.7 %collective-permute-start.6 = (bf16[64,8192]{1,0:T(8,128)(2,1)S(1)}, bf16[64,8192]{1,0:T(8,128)(2,1)S(1)}, u32[]{:S(2)}, u32[]{:S(2)}) collective-permute-start(bf16[64,8192]{1,0:T(8,128)(2,1)S(1)} %slice.53), channel_id=1, source_target_pairs={{0,1},{1,0},{2,3},{3,2},{4,5},{5,4},{6,7},{7,6},{8,9},{9,8},{10,11... | collective-permute-start | bytes 3145736 | tf_op jit(solution)/shard_map/ppermute | solution.py:20
  73.7 45.3 %copy-start.5 = (bf16[1,1,1,8192]{3,2,1,0:T(2,128)(2,1)S(1)}, bf16[1,1,1,8192]{3,2,1,0:T(2,128)(2,1)}, u32[]{:S(2)}) copy-start(bf16[1,1,1,8192]{3,2,1,0:T(2,128)(2,1)} %param.17) | copy-start | bytes 49156
  73.8 13.9 %collective-permute-start.7 = (bf16[16,8192]{1,0:T(8,128)(2,1)S(1)}, bf16[16,8192]{1,0:T(8,128)(2,1)S(1)}, u32[]{:S(2)}, u32[]{:S(2)}) collective-permute-start(bf16[16,8192]{1,0:T(8,128)(2,1)S(1)} %get-tuple-element.7), channel_id=1, source_target_pairs={{0,34},{2,0},{32,2},{34,32},{1,35},{3,1},{33,3},{35,33},{4,38},{6,... | collective-permute-start | bytes 786440 | tf_op jit(solution)/shard_map/ppermute | solution.py:20
  76.1 11.5 %collective-permute-start.8 = (bf16[16,8192]{1,0:T(8,128)(2,1)S(1)}, bf16[16,8192]{1,0:T(8,128)(2,1)S(1)}, u32[]{:S(2)}, u32[]{:S(2)}) collective-permute-start(bf16[16,8192]{1,0:T(8,128)(2,1)S(1)} %get-tuple-element.9), channel_id=1, source_target_pairs={{0,32},{2,34},{32,0},{34,2},{1,33},{3,35},{33,1},{35,3},{4,36},{6,... | collective-permute-start | bytes 786440 | tf_op jit(solution)/shard_map/ppermute | solution.py:20
  77.2 14.0 %collective-permute-start.9 = (bf16[16,8192]{1,0:T(8,128)(2,1)S(1)}, bf16[16,8192]{1,0:T(8,128)(2,1)S(1)}, u32[]{:S(2)}, u32[]{:S(2)}) collective-permute-start(bf16[16,8192]{1,0:T(8,128)(2,1)S(1)} %get-tuple-element.8), channel_id=1, source_target_pairs={{0,2},{2,32},{32,34},{34,0},{1,3},{3,33},{33,35},{35,1},{4,6},{6,3... | collective-permute-start | bytes 786440 | tf_op jit(solution)/shard_map/ppermute | solution.py:20
  110.5 5.3 %collective-permute-start.10 = (f32[1,8192]{1,0:T(1,128)}, f32[1,8192]{1,0:T(1,128)S(1)}, u32[]{:S(2)}, u32[]{:S(2)}) collective-permute-start(f32[1,8192]{1,0:T(1,128)} %get-tuple-element.11), channel_id=1, source_target_pairs={{0,192},{64,128},{128,64},{192,0},{1,193},{65,129},{129,65},{193,1... | collective-permute-start | bytes 98312 | tf_op jit(solution)/shard_map/ppermute | solution.py:24
  113.3 5.6 %collective-permute-start.11 = (f32[1,8192]{1,0:T(1,128)}, f32[1,8192]{1,0:T(1,128)S(1)}, u32[]{:S(2)}, u32[]{:S(2)}) collective-permute-start(f32[1,8192]{1,0:T(1,128)} %get-tuple-element.10), channel_id=1, source_target_pairs={{0,128},{64,192},{128,0},{192,64},{1,129},{65,193},{129,1},{193,65... | collective-permute-start | bytes 98312 | tf_op jit(solution)/shard_map/ppermute | solution.py:28

commit v2 on v1

v2 whole, which is shorter than its diff:
```python
import jax
import jax.numpy as jnp
from jax import lax
from jax.experimental import pallas as pl
from jax.experimental.pallas import tpu as pltpu
from jax.sharding import Mesh
from jax.sharding import PartitionSpec as P

HEADS = 64
HD = 128
KVH = 4
X = ("xh", "xl")
GRP = ("y", "xh")
TP = ("z", "xl", "c")


masked_score = -1e30


def shifted(value, axes, hops):
    size = lax.axis_size(axes)
    return lax.ppermute(value, axes, [(i, (i + hops) % size) for i in range(size)])


def swapped(value):
    return shifted(value, "c", 1)


def mirrored(value):
    return lax.ppermute(value, "y", [(i, 3 - i) for i in range(4)])


def opposite(value):
    return lax.ppermute(value, "y", [(i, (i + 2) % 4) for i in range(4)])


def in_hbm(value):
    return pltpu.with_memory_space_constraint(value, pltpu.HBM)


def wide(value):
    return value.astype(jnp.float32)


def narrow(value):
    return value.astype(jnp.bfloat16)


def pairs_kernel(pairs_ref, first_ref, second_ref):
    for i in range(4):
        first_ref[pl.ds(2 * i, 2), :] = pairs_ref[i]
        second_ref[pl.ds(2 * i, 2), :] = pairs_ref[4 + i]


def rows_of_pairs(pairs):
    half = pltpu.VMEM((8, pairs.shape[-1]), pairs.dtype)
    in_vmem = pl.BlockSpec(memory_space=pltpu.VMEM)
    return pl.pallas_call(
        pairs_kernel, out_shape=(half, half), in_specs=[in_vmem], out_specs=(in_vmem, in_vmem)
    )(pairs)


def gathered_blocks(row):
    pair = jnp.concatenate([mirrored(row), opposite(row)], 0)
    planes, width = pair.shape
    depth = lax.axis_size("z")
    pairs = lax.all_to_all(
        jnp.broadcast_to(pair[None], (depth, planes, width)), "z", 0, 0, tiled=True
    )
    first, second = rows_of_pairs(pairs)
    low = shifted(first, X, 1)
    high = shifted(second, X, -1)
    low_rest = shifted(second, X, 1)
    high_rest = shifted(first, X, -1)
    low_far = shifted(low, X, 1)
    high_far = shifted(high, X, -1)
    blocks = [first, second, low, low_rest, high_rest, high, low_far, high_far]
    return blocks + [swapped(b) for b in blocks]


def returned_rows(keep, send):
    total = keep + wide(swapped(send))
    own = total[:16]
    near_low, near_high, far = total[16:32], total[32:48], total[48:]
    far_low = shifted(narrow(far[:8]), X, -1)
    far_high = shifted(narrow(far[8:]), X, 1)
    low_rest = shifted(narrow(near_low[8:]), X, -1)
    high_rest = shifted(narrow(near_high[:8]), X, 1)
    low = shifted(narrow(near_low[:8] + wide(far_low)), X, -1)
    high = shifted(narrow(near_high[8:] + wide(far_high)), X, 1)
    first = own[:8] + wide(high_rest) + wide(low)
    second = own[8:] + wide(low_rest) + wide(high)
    own = jnp.concatenate([narrow(first), narrow(second)], 0)
    depth = lax.axis_size("z")
    pieces = own.reshape(depth, 2, own.shape[-1])
    arrived = lax.all_to_all(pieces, "z", 0, 0, tiled=True)
    pair = jnp.sum(arrived.astype(jnp.float32), axis=0)
    return mirrored(pair[:1]) + opposite(pair[1:])


CHUNKS = 4


def feed_kernel(*refs):
    blocks, rest = refs[:16], refs[16:]
    gate_hbm, up_hbm, down_hbm, keep_ref, send_ref, rows_ref, gate_ref, up_ref, down_ref, row_sems, sems = rest
    width = rows_ref.shape[1]
    part = width // CHUNKS
    row_copies = []
    for i, block in enumerate(blocks):
        size = block.shape[0]
        row_copies.append(
            pltpu.make_async_copy(block, rows_ref.at[pl.ds(i * size, size)], row_sems.at[i])
        )
    weight_copies = []
    for k in range(CHUNKS):
        for w, (hbm, vmem) in enumerate(((gate_hbm, gate_ref), (up_hbm, up_ref))):
            columns = pl.ds(k * part, part)
            weight_copies.append(
                pltpu.make_async_copy(hbm.at[:, columns], vmem.at[:, columns], sems.at[2 * k + w])
            )
    down_copy = pltpu.make_async_copy(down_hbm, down_ref, sems.at[2 * CHUNKS])
    for copy in row_copies + weight_copies + [down_copy]:
        copy.start()
    for copy in row_copies:
        copy.wait()
    numbers = (((1,), (1,)), ((), ()))
    gate = jnp.zeros((rows_ref.shape[0], gate_ref.shape[0]), jnp.float32)
    up = gate
    for k in range(CHUNKS):
        columns = pl.ds(k * part, part)
        rows = rows_ref[:, columns]
        weight_copies[2 * k].wait()
        gate = gate + lax.dot_general(rows, gate_ref[:, columns], numbers, preferred_element_type=jnp.float32)
        weight_copies[2 * k + 1].wait()
        up = up + lax.dot_general(rows, up_ref[:, columns], numbers, preferred_element_type=jnp.float32)
    act = (gate / (1.0 + jnp.exp(-gate)) * up).astype(jnp.bfloat16)
    down_copy.wait()
    half = rows_ref.shape[0] // 2
    send_ref[...] = jnp.dot(act[half:], down_ref[...], preferred_element_type=jnp.float32).astype(jnp.bfloat16)
    keep_ref[...] = jnp.dot(act[:half], down_ref[...], preferred_element_type=jnp.float32)


def feed_rows(blocks, gate_weight, up_weight, down_weight):
    units, width = gate_weight.shape[1:]
    anywhere = pl.BlockSpec(memory_space=pl.ANY)
    in_vmem = pl.BlockSpec(memory_space=pltpu.VMEM)
    held = pltpu.VMEM((units, width), jnp.bfloat16)
    return pl.pallas_call(
        feed_kernel,
        out_shape=(
            jax.ShapeDtypeStruct((64, width), jnp.float32),
            jax.ShapeDtypeStruct((64, width), jnp.bfloat16),
        ),
        in_specs=[anywhere] * len(blocks) + [pl.BlockSpec(memory_space=pltpu.HBM)] * 3,
        out_specs=(in_vmem, in_vmem),
        scratch_shapes=[
            pltpu.VMEM((128, width), jnp.bfloat16),
            held,
            held,
            held,
            pltpu.SemaphoreType.DMA((16,)),
            pltpu.SemaphoreType.DMA((2 * CHUNKS + 1,)),
        ],
        compiler_params=pltpu.CompilerParams(vmem_limit_bytes=28 << 20),
    )(*blocks, *(in_hbm(w[0]) for w in (gate_weight, up_weight, down_weight)))


def attend_kernel(
    length_ref,
    key_hbm,
    value_hbm,
    query_hbm,
    fresh_key_hbm,
    fresh_value_hbm,
    residual_hbm,
    gain_hbm,
    hidden_ref,
    normed_ref,
    keys,
    values,
    query,
    fresh_key,
    fresh_value,
    residual,
    gain,
    query_rows,
    residual_rows,
    sems,
):
    sources = (query_hbm, key_hbm, fresh_key_hbm, value_hbm, fresh_value_hbm, residual_hbm, gain_hbm)
    targets = (query, keys, fresh_key, values, fresh_value, residual, gain)
    copies = [pltpu.make_async_copy(s, t, sems.at[i]) for i, (s, t) in enumerate(zip(sources, targets))]
    for copy in copies:
        copy.start()
    copies[0].wait()
    for h in range(HEADS):
        query_rows[pl.ds(h, 1), :] = query[:, pl.ds(h * HD, HD)].astype(jnp.float32)
    slots = keys.shape[0]
    share = HEADS // KVH
    scale = HD ** (-0.5)
    usable = lax.broadcasted_iota(jnp.int32, (share, slots), 1) < length_ref[0, 0]
    copies[1].wait()
    copies[2].wait()
    weights = []
    for j in range(KVH):
        wide_query = query_rows[pl.ds(j * share, share), :]
        lanes = pl.ds(j * HD, HD)
        scores = lax.dot_general(
            wide_query.astype(jnp.bfloat16),
            keys[:, lanes],
            (((1,), (1,)), ((), ())),
            preferred_element_type=jnp.float32,
        )
        scores = jnp.where(usable, scores * scale, masked_score)
        fresh = jnp.sum(wide_query * fresh_key[:, lanes].astype(jnp.float32), axis=-1, keepdims=True) * scale
        ceiling = jnp.maximum(jnp.max(scores, axis=-1, keepdims=True), fresh)
        expo = jnp.where(usable, jnp.exp(scores - ceiling), 0.0)
        fresh_expo = jnp.exp(fresh - ceiling)
        denominator = jnp.sum(expo, axis=-1, keepdims=True) + fresh_expo
        weights.append((expo.astype(jnp.bfloat16), fresh_expo.astype(jnp.bfloat16), denominator))
    for copy in copies[3:]:
        copy.wait()
    for h in range(HEADS):
        residual_rows[pl.ds(h, 1), :] = residual[:, pl.ds(h * HD, HD)].astype(jnp.float32)
    square = jnp.zeros((1, 1), jnp.float32)
    for j in range(KVH):
        lanes = pl.ds(j * HD, HD)
        rows = pl.ds(j * share, share)
        expo, fresh_expo, denominator = weights[j]
        weighted = jnp.dot(expo, values[:, lanes], preferred_element_type=jnp.float32)
        weighted = weighted + fresh_expo.astype(jnp.float32) * fresh_value[:, lanes].astype(jnp.float32)
        hidden = residual_rows[rows, :] + weighted / denominator
        residual_rows[rows, :] = hidden
        square = square + jnp.sum(jnp.sum(hidden * hidden, axis=-1, keepdims=True), axis=0, keepdims=True)
    factor = lax.rsqrt(square / (HEADS * HD) + 1e-05)
    query_rows[...] = residual_rows[...] * factor * gain[...]
    for h in range(HEADS):
        lanes = pl.ds(h * HD, HD)
        hidden_ref[:, lanes] = residual_rows[pl.ds(h, 1), :]
        normed_ref[:, lanes] = query_rows[pl.ds(h, 1), :].astype(jnp.bfloat16)


def attend(lengths, key_cache, value_cache, queries, new_keys, new_values, residual, norm_gain):
    slots, columns = key_cache.shape[2:]
    width = queries.shape[-1]
    cache = (slots, columns)
    args = (
        lengths,
        key_cache.reshape(cache),
        value_cache.reshape(cache),
        queries.reshape(1, width),
        new_keys.reshape(1, columns),
        new_values.reshape(1, columns),
        residual.reshape(1, width),
        norm_gain.reshape(HEADS, HD),
    )
    in_vmem = pl.BlockSpec(memory_space=pltpu.VMEM)
    rows = pltpu.VMEM((HEADS, HD), jnp.float32)
    return pl.pallas_call(
        attend_kernel,
        out_shape=(
            jax.ShapeDtypeStruct((1, width), jnp.float32),
            jax.ShapeDtypeStruct((1, width), jnp.bfloat16),
        ),
        in_specs=[pl.BlockSpec(memory_space=pltpu.SMEM)] + [pl.BlockSpec(memory_space=pltpu.HBM)] * 7,
        out_specs=(in_vmem, in_vmem),
        scratch_shapes=[
            pltpu.VMEM(cache, jnp.bfloat16),
            pltpu.VMEM(cache, jnp.bfloat16),
            pltpu.VMEM((1, width), jnp.bfloat16),
            pltpu.VMEM((1, columns), jnp.bfloat16),
            pltpu.VMEM((1, columns), jnp.bfloat16),
            pltpu.VMEM((1, width), jnp.bfloat16),
            rows,
            rows,
            rows,
            pltpu.SemaphoreType.DMA((7,)),
        ],
        compiler_params=pltpu.CompilerParams(vmem_limit_bytes=16 << 20),
    )(args[0], *(in_hbm(arg) for arg in args[1:]))


def local(
    key_cache,
    value_cache,
    lengths,
    queries,
    new_keys,
    new_values,
    residual,
    norm_gain,
    gate_weight,
    up_weight,
    down_weight,
):
    serving = lax.axis_index("y") < lax.axis_size("y") // 2
    hidden, flat_rows = attend(
        lengths, key_cache, value_cache, queries, new_keys, new_values, residual, norm_gain
    )
    keep, send = feed_rows(gathered_blocks(flat_rows), gate_weight, up_weight, down_weight)
    summed = returned_rows(keep, send)
    mixed = (hidden + summed).astype(jnp.bfloat16)
    mixed = jnp.where(serving, mixed, jnp.zeros_like(mixed))
    return mixed.reshape(residual.shape)


def solution(mesh):
    finer = Mesh(mesh.devices.reshape(4, 2, 8, 2, 2), ("y", "xh", "z", "xl", "c"))
    in_specs = (
        P(GRP, TP, None, None),
        P(GRP, TP, None, None),
        P(GRP, TP),
        P(GRP, None, TP, None),
        P(GRP, None, TP, None),
        P(GRP, None, TP, None),
        P(GRP, None, TP, None),
        P(),
        P(GRP, TP, None),
        P(GRP, TP, None),
        P(GRP, TP, None),
    )
    out_specs = P(GRP, None, TP, None)
    return jax.shard_map(local, mesh=finer, in_specs=in_specs, out_specs=out_specs, check_vma=False)
```

time: 120 us -> 97.3 us (0.81)
  local copies, waits for them, and re-layouts: 14.4 us -> 0.41 us
  Pallas kernels: 0 us -> 13.5 us
  matrix products: 12.9 us -> 0 us
  waiting for transfers between devices: 35.3 us -> 26.9 us
  starting transfers between devices: 15.9 us -> 24 us
  other arithmetic: 6.59 us -> 1.43 us
  blocking collectives: 32.9 us -> 30.1 us
    pallas_call x0 -> x3, Pallas kernels: none -> 13.5 us  [the longest x1 10.4 us: feed_rows(): pl.pallas_call(feed_kernel, out_shape=(jax.ShapeDtypeStruct((64, width),...]
    dot_general x5 -> x0, matrix products: 12.9 us -> none  [the longest x1 7.39 us: feed_rows(): return jnp.dot(product, down_weight[0], preferred_element_type=jnp.float32)]
    ppermute x8 -> x21, waiting for transfers between devices: 25.2 us -> 16.9 us  [shifted(): lax.ppermute(value, axes, [(i, (i + hops) % size) for i in range(size)])]
    ppermute x8 -> x21, starting transfers between devices: 10.2 us -> 18.1 us  [shifted(): lax.ppermute(value, axes, [(i, (i + hops) % size) for i in range(size)])]
    another operation x2 -> x0, local copies, waits for them, and re-layouts: 5.03 us -> none
    reshape x3 -> x1, local copies, waits for them, and re-layouts: 3.6 us -> 0.18 us  [returned_rows(): pieces = own.reshape(depth, 2, own.shape[-1])]
    unnamed x18 -> x0, local copies, waits for them, and re-layouts: 3.1 us -> none
    all_to_all x1, blocking collectives: 15.6 us -> 12.9 us  [returned_rows(): arrived = lax.all_to_all(pieces, 'z', 0, 0, tiled=True)]
  transfers between devices with their start and end apart: 12 -> 25, of which waited for: 10 -> 15; matrix products, arithmetic and copies ran while one was open for 1% -> 0% of each run, Pallas kernels for 0% -> 0%
where the time goes in v2:
time: 97.3 us; the launch traced here: 97.1 us
  blocking collectives  30.1 us (31%)
  waiting for transfers between devices  26.9 us (28%)
  starting transfers between devices  24 us (25%)
  Pallas kernels  13.5 us (14%)
  other arithmetic  1.43 us (1%)
    ppermute x21, starting transfers between devices, shifted(): lax.ppermute(value, axes, [(i, (i + hops) % size) for i in range(size)])  18.1 us
    all_to_all x1, blocking collectives, gathered_blocks(): lax.all_to_all(jnp.broadcast_to(pair[None], (depth, planes, width)), 'z',...  17.2 us
    ppermute x21, waiting for transfers between devices, shifted(): lax.ppermute(value, axes, [(i, (i + hops) % size) for i in range(size)])  16.9 us
    all_to_all x1, blocking collectives, returned_rows(): arrived = lax.all_to_all(pieces, 'z', 0, 0, tiled=True)  12.9 us
    pallas_call x1, Pallas kernels, feed_rows(): pl.pallas_call(feed_kernel, out_shape=(jax.ShapeDtypeStruct((64, width),...  10.4 us
    ppermute x2, waiting for transfers between devices, opposite(): return lax.ppermute(value, 'y', [(i, (i + 2) % 4) for i in range(4)])  5.43 us
    ppermute x2, starting transfers between devices, mirrored(): return lax.ppermute(value, 'y', [(i, 3 - i) for i in range(4)])  5.02 us
    ppermute x2, waiting for transfers between devices, mirrored(): return lax.ppermute(value, 'y', [(i, 3 - i) for i in range(4)])  4.53 us
  transfers between devices with their start and end apart: 25, of which 15 were waited for; matrix products, arithmetic and copies ran while one was open for 0% of the time, Pallas kernels for 0%

profile of v2, /device:TPU:24, one launch (start us, length us, event | category | flops | bytes accessed | tf_op | source)
XLA Modules:
  0.0 97.1 jit_solution(16219171142134857701)
XLA Ops:
  0.7 2.1 %shard_map.109 = (f32[1,8192]{1,0:T(1,128)S(1)}, bf16[1,8192]{1,0:T(2,128)(2,1)S(1)}) custom-call(s32[1,1]{1,0:T(1,128)S(6)} %copy.12.length_ref, bf16[768,512]{1,0:T(8,128)(2,1)} %bitcast.15, bf16[768,512]{1,0:T(8,128)(2,1)} %bitcast.16, bf16[1,8192]{1,0:T(2,128)(2,1)} %bitcast.17, bf16[1,512]{1,0:T(2,128)(2,1)} %bitcast.20, bf16[1,512]{1,0:T(2,128)(2,1)} %bitcast.21, ...), custom_call_target="tpu_custom_call" | custom-call | tf_op jit(solution)/shard_map/pallas_call | solution.py:260
  2.7 2.0 %collective-permute-start = (bf16[1,8192]{1,0:T(2,128)(2,1)S(1)}, bf16[1,8192]{1,0:T(2,128)(2,1)S(1)}, u32[]{:S(2)}, u32[]{:S(2)}) collective-permute-start(bf16[1,8192]{1,0:T(2,128)(2,1)S(1)} %get-tuple-element.12), channel_id=1, source_target_pairs={{0,192},{64,128},{128,64},{192,0},{1,193},{65,129},{129,65},{193,1... | collective-permute-start | bytes 49160 | tf_op jit(solution)/shard_map/ppermute | solution.py:30
  4.8 0.9 collective-permute-start.1
  5.6 2.3 %collective-permute-done = bf16[1,8192]{1,0:T(2,128)(2,1)S(1)} collective-permute-done((bf16[1,8192]{1,0:T(2,128)(2,1)S(1)}, bf16[1,8192]{1,0:T(2,128)(2,1)S(1)}, u32[]{:S(2)}, u32[]{:S(2)}) %collective-permute-start) | collective-permute-done | bytes 16416 | tf_op jit(solution)/shard_map/ppermute | solution.py:30
  7.9 2.3 %collective-permute-done.1 = bf16[1,8192]{1,0:T(2,128)(2,1)S(1)} collective-permute-done((bf16[1,8192]{1,0:T(2,128)(2,1)S(1)}, bf16[1,8192]{1,0:T(2,128)(2,1)S(1)}, u32[]{:S(2)}, u32[]{:S(2)}) %collective-permute-start.1) | collective-permute-done | bytes 16416 | tf_op jit(solution)/shard_map/ppermute | solution.py:34
  10.2 0.1 pad_maximum_fusion.1
  10.3 0.1 broadcast_in_dim.4
  10.4 17.2 %all_to_all.10.pairs_ref = bf16[8,2,8192]{2,1,0:T(2,128)(2,1)} all-to-all(bf16[8,2,8192]{2,1,0:T(2,128)(2,1)S(1)} %broadcast_in_dim.4), channel_id=1, replica_groups=mesh['y'=4,'xh'=2,'z'=8,'xl'=2,'c'=2] {'z'}, dimensions={0} | all-to-all | bytes 524288 | tf_op jit(solution)/shard_map/all_to_all | solution.py:67
  27.7 1.1 %shard_map.110 = (bf16[8,8192]{1,0:T(8,128)(2,1)S(1)}, bf16[8,8192]{1,0:T(8,128)(2,1)S(1)}) custom-call(bf16[8,2,8192]{2,1,0:T(2,128)(2,1)} %all_to_all.10.pairs_ref), custom_call_target="tpu_custom_call" | custom-call | tf_op jit(solution)/shard_map/pallas_call | solution.py:58
  28.8 1.6 %collective-permute-start.2 = (bf16[8,8192]{1,0:T(8,128)(2,1)S(1)}, bf16[8,8192]{1,0:T(8,128)(2,1)S(1)}, u32[]{:S(2)}, u32[]{:S(2)}) collective-permute-start(bf16[8,8192]{1,0:T(8,128)(2,1)S(1)} %get-tuple-element.13.refs_0_), channel_id=1, source_target_pairs={{0,2},{2,32},{32,34},{34,0},{1,3},{3,33},{33,35},{35,1},{4,6},{6,3... | collective-permute-start | bytes 393224 | tf_op jit(solution)/shard_map/ppermute | solution.py:22
  30.3 1.7 %collective-permute-start.5 = (bf16[8,8192]{1,0:T(8,128)(2,1)S(1)}, bf16[8,8192]{1,0:T(8,128)(2,1)S(1)}, u32[]{:S(2)}, u32[]{:S(2)}) collective-permute-start(bf16[8,8192]{1,0:T(8,128)(2,1)S(1)} %get-tuple-element.14.refs_1_), channel_id=1, source_target_pairs={{0,34},{2,0},{32,2},{34,32},{1,35},{3,1},{33,3},{35,33},{4,38},{6,... | collective-permute-start | bytes 393224 | tf_op jit(solution)/shard_map/ppermute | solution.py:22
  32.1 0.3 collective-permute-start.3
  32.3 3.0 %collective-permute-start.4 = (bf16[8,8192]{1,0:T(8,128)(2,1)S(1)}, bf16[8,8192]{1,0:T(8,128)(2,1)S(1)}, u32[]{:S(2)}, u32[]{:S(2)}) collective-permute-start(bf16[8,8192]{1,0:T(8,128)(2,1)S(1)} %get-tuple-element.13.refs_0_), channel_id=1, source_target_pairs={{0,34},{2,0},{32,2},{34,32},{1,35},{3,1},{33,3},{35,33},{4,38},{6,... | collective-permute-start | bytes 393224 | tf_op jit(solution)/shard_map/ppermute | solution.py:22
  35.3 0.5 collective-permute-start.9
  35.8 1.0 collective-permute-start.6
  36.8 1.5 %collective-permute-done.3.refs_3_ = bf16[8,8192]{1,0:T(8,128)(2,1)S(1)} collective-permute-done((bf16[8,8192]{1,0:T(8,128)(2,1)S(1)}, bf16[8,8192]{1,0:T(8,128)(2,1)S(1)}, u32[]{:S(2)}, u32[]{:S(2)}) %collective-permute-start.3) | collective-permute-done | bytes 131104 | tf_op jit(solution)/shard_map/ppermute | solution.py:22
  38.2 0.8 collective-permute-start.7
  39.1 0.5 collective-permute-start.13
  39.6 0.1 collective-permute-start.11
  39.7 2.8 %collective-permute-done.6.refs_6_ = bf16[8,8192]{1,0:T(8,128)(2,1)S(1)} collective-permute-done((bf16[8,8192]{1,0:T(8,128)(2,1)S(1)}, bf16[8,8192]{1,0:T(8,128)(2,1)S(1)}, u32[]{:S(2)}, u32[]{:S(2)}) %collective-permute-start.6) | collective-permute-done | bytes 131104 | tf_op jit(solution)/shard_map/ppermute | solution.py:22
  42.5 0.7 collective-permute-done.7.refs_7_
  43.2 0.5 collective-permute-start.15
  43.7 0.1 collective-permute-done.12.refs_12_
  43.9 0.7 collective-permute-done.14.refs_14_
  44.6 0.2 collective-permute-done.15.refs_15_
  44.7 10.4 %shard_map.111 = (f32[64,8192]{1,0:T(8,128)S(1)}, bf16[64,8192]{1,0:T(8,128)(2,1)S(1)}) custom-call(bf16[8,8192]{1,0:T(8,128)(2,1)S(1)} %get-tuple-element.13.refs_0_, bf16[8,8192]{1,0:T(8,128)(2,1)S(1)} %get-tuple-element.14.refs_1_, bf16[8,8192]{1,0:T(8,128)(2,1)S(1)} %collective-permute-done.2.refs_2_, ...), custom_call_target="tpu_custom_call" | custom-call | tf_op jit(solution)/shard_map/pallas_call | solution.py:149
  55.1 0.4 collective-permute-start.16
  55.5 2.3 %collective-permute-done.16 = bf16[64,8192]{1,0:T(8,128)(2,1)S(1)} collective-permute-done((bf16[64,8192]{1,0:T(8,128)(2,1)S(1)}, bf16[64,8192]{1,0:T(8,128)(2,1)S(1)}, u32[]{:S(2)}, u32[]{:S(2)}) %collective-permute-start.16) | collective-permute-done | bytes 1048608 | tf_op jit(solution)/shard_map/ppermute | solution.py:22
  57.9 0.3 fusion.7
  58.2 2.3 %collective-permute-start.18 = (bf16[8,8192]{1,0:T(8,128)(2,1)S(1)}, bf16[8,8192]{1,0:T(8,128)(2,1)S(1)}, u32[]{:S(2)}, u32[]{:S(2)}) collective-permute-start(bf16[8,8192]{1,0:T(8,128)(2,1)S(1)} %get-tuple-element.26), channel_id=1, source_target_pairs={{0,34},{2,0},{32,2},{34,32},{1,35},{3,1},{33,3},{35,33},{4,38},{6,... | collective-permute-start | bytes 393224 | tf_op jit(solution)/shard_map/ppermute | solution.py:22
  60.6 3.3 %collective-permute-start.20 = (bf16[8,8192]{1,0:T(8,128)(2,1)S(1)}, bf16[8,8192]{1,0:T(8,128)(2,1)S(1)}, u32[]{:S(2)}, u32[]{:S(2)}) collective-permute-start(bf16[8,8192]{1,0:T(8,128)(2,1)S(1)} %get-tuple-element.25), channel_id=1, source_target_pairs={{0,34},{2,0},{32,2},{34,32},{1,35},{3,1},{33,3},{35,33},{4,38},{6,... | collective-permute-start | bytes 393224 | tf_op jit(solution)/shard_map/ppermute | solution.py:22
  63.8 0.8 collective-permute-done.18
  64.6 3.5 %collective-permute-done.21 = bf16[8,8192]{1,0:T(8,128)(2,1)S(1)} collective-permute-done((bf16[8,8192]{1,0:T(8,128)(2,1)S(1)}, bf16[8,8192]{1,0:T(8,128)(2,1)S(1)}, u32[]{:S(2)}, u32[]{:S(2)}) %collective-permute-start.21) | collective-permute-done | bytes 131104 | tf_op jit(solution)/shard_map/ppermute | solution.py:22
  68.1 0.1 fusion.3
  68.2 0.1 collective-permute-start.19
  68.3 2.0 %collective-permute-start.22 = (bf16[8,8192]{1,0:T(8,128)(2,1)S(1)}, bf16[8,8192]{1,0:T(8,128)(2,1)S(1)}, u32[]{:S(2)}, u32[]{:S(2)}) collective-permute-start(bf16[8,8192]{1,0:T(8,128)(2,1)S(1)} %get-tuple-element.22), channel_id=1, source_target_pairs={{0,2},{2,32},{32,34},{34,0},{1,3},{3,33},{33,35},{35,1},{4,6},{6,3... | collective-permute-start | bytes 393224 | tf_op jit(solution)/shard_map/ppermute | solution.py:22
  70.3 2.9 %collective-permute-done.19 = bf16[8,8192]{1,0:T(8,128)(2,1)S(1)} collective-permute-done((bf16[8,8192]{1,0:T(8,128)(2,1)S(1)}, bf16[8,8192]{1,0:T(8,128)(2,1)S(1)}, u32[]{:S(2)}, u32[]{:S(2)}) %collective-permute-start.19) | collective-permute-done | bytes 131104 | tf_op jit(solution)/shard_map/ppermute | solution.py:22
  73.2 1.3 %collective-permute-done.22 = bf16[8,8192]{1,0:T(8,128)(2,1)S(1)} collective-permute-done((bf16[8,8192]{1,0:T(8,128)(2,1)S(1)}, bf16[8,8192]{1,0:T(8,128)(2,1)S(1)}, u32[]{:S(2)}, u32[]{:S(2)}) %collective-permute-start.22) | collective-permute-done | bytes 131104 | tf_op jit(solution)/shard_map/ppermute | solution.py:22
  74.5 0.1 fusion.5
  74.7 0.2 reshape.35
  74.8 12.9 %all_to_all.11 = bf16[8,2,8192]{2,1,0:T(2,128)(2,1)S(1)} all-to-all(bf16[8,2,8192]{2,1,0:T(2,128)(2,1)S(1)} %reshape.35), channel_id=1, replica_groups=mesh['y'=4,'xh'=2,'z'=8,'xl'=2,'c'=2] {'z'}, dimensions={0} | all-to-all | bytes 524288 | tf_op jit(solution)/shard_map/all_to_all | solution.py:96
  87.7 0.2 convert_reduce_fusion
  88.0 0.1 fusion.9
  88.0 3.0 %collective-permute-start.23 = (f32[1,8192]{1,0:T(1,128)S(1)}, f32[1,8192]{1,0:T(1,128)S(1)}, u32[]{:S(2)}, u32[]{:S(2)}) collective-permute-start(f32[1,8192]{1,0:T(1,128)S(1)} %get-tuple-element.28), channel_id=1, source_target_pairs={{0,192},{64,128},{128,64},{192,0},{1,193},{65,129},{129,65},{193,1... | collective-permute-start | bytes 98312 | tf_op jit(solution)/shard_map/ppermute | solution.py:30
  91.0 0.0 collective-permute-start.24
  91.0 2.2 %collective-permute-done.23 = f32[1,8192]{1,0:T(1,128)S(1)} collective-permute-done((f32[1,8192]{1,0:T(1,128)S(1)}, f32[1,8192]{1,0:T(1,128)S(1)}, u32[]{:S(2)}, u32[]{:S(2)}) %collective-permute-start.23) | collective-permute-done | bytes 32800 | tf_op jit(solution)/shard_map/ppermute | solution.py:30
  93.2 3.2 %collective-permute-done.24 = f32[1,8192]{1,0:T(1,128)S(1)} collective-permute-done((f32[1,8192]{1,0:T(1,128)S(1)}, f32[1,8192]{1,0:T(1,128)S(1)}, u32[]{:S(2)}, u32[]{:S(2)}) %collective-permute-start.24) | collective-permute-done | bytes 32800 | tf_op jit(solution)/shard_map/ppermute | solution.py:34
  96.4 0.7 fusion.6
  (18 shorter events, 0.1 us)
Async XLA Ops:
  2.7 5.2 %collective-permute-start = (bf16[1,8192]{1,0:T(2,128)(2,1)S(1)}, bf16[1,8192]{1,0:T(2,128)(2,1)S(1)}, u32[]{:S(2)}, u32[]{:S(2)}) collective-permute-start(bf16[1,8192]{1,0:T(2,128)(2,1)S(1)} %get-tuple-element.12), channel_id=1, source_target_pairs={{0,192},{64,128},{128,64},{192,0},{1,193},{65,129},{129,65},{193,1... | collective-permute-start | bytes 49160 | tf_op jit(solution)/shard_map/ppermute | solution.py:30
  4.8 5.4 %collective-permute-start.1 = (bf16[1,8192]{1,0:T(2,128)(2,1)S(1)}, bf16[1,8192]{1,0:T(2,128)(2,1)S(1)}, u32[]{:S(2)}, u32[]{:S(2)}) collective-permute-start(bf16[1,8192]{1,0:T(2,128)(2,1)S(1)} %get-tuple-element.12), channel_id=1, source_target_pairs={{0,128},{64,192},{128,0},{192,64},{1,129},{65,193},{129,1},{193,65... | collective-permute-start | bytes 49160 | tf_op jit(solution)/shard_map/ppermute | solution.py:34
  28.8 6.6 %collective-permute-start.2 = (bf16[8,8192]{1,0:T(8,128)(2,1)S(1)}, bf16[8,8192]{1,0:T(8,128)(2,1)S(1)}, u32[]{:S(2)}, u32[]{:S(2)}) collective-permute-start(bf16[8,8192]{1,0:T(8,128)(2,1)S(1)} %get-tuple-element.13.refs_0_), channel_id=1, source_target_pairs={{0,2},{2,32},{32,34},{34,0},{1,3},{3,33},{33,35},{35,1},{4,6},{6,3... | collective-permute-start | bytes 393224 | tf_op jit(solution)/shard_map/ppermute | solution.py:22
  30.3 5.5 %collective-permute-start.5 = (bf16[8,8192]{1,0:T(8,128)(2,1)S(1)}, bf16[8,8192]{1,0:T(8,128)(2,1)S(1)}, u32[]{:S(2)}, u32[]{:S(2)}) collective-permute-start(bf16[8,8192]{1,0:T(8,128)(2,1)S(1)} %get-tuple-element.14.refs_1_), channel_id=1, source_target_pairs={{0,34},{2,0},{32,2},{34,32},{1,35},{3,1},{33,3},{35,33},{4,38},{6,... | collective-permute-start | bytes 393224 | tf_op jit(solution)/shard_map/ppermute | solution.py:22
  32.1 6.2 %collective-permute-start.3 = (bf16[8,8192]{1,0:T(8,128)(2,1)S(1)}, bf16[8,8192]{1,0:T(8,128)(2,1)S(1)}, u32[]{:S(2)}, u32[]{:S(2)}) collective-permute-start(bf16[8,8192]{1,0:T(8,128)(2,1)S(1)} %get-tuple-element.14.refs_1_), channel_id=1, source_target_pairs={{0,2},{2,32},{32,34},{34,0},{1,3},{3,33},{33,35},{35,1},{4,6},{6,3... | collective-permute-start | bytes 393224 | tf_op jit(solution)/shard_map/ppermute | solution.py:22
  32.3 6.7 %collective-permute-start.4 = (bf16[8,8192]{1,0:T(8,128)(2,1)S(1)}, bf16[8,8192]{1,0:T(8,128)(2,1)S(1)}, u32[]{:S(2)}, u32[]{:S(2)}) collective-permute-start(bf16[8,8192]{1,0:T(8,128)(2,1)S(1)} %get-tuple-element.13.refs_0_), channel_id=1, source_target_pairs={{0,34},{2,0},{32,2},{34,32},{1,35},{3,1},{33,3},{35,33},{4,38},{6,... | collective-permute-start | bytes 393224 | tf_op jit(solution)/shard_map/ppermute | solution.py:22
  35.3 3.8 %collective-permute-start.8 = (bf16[8,8192]{1,0:T(8,128)(2,1)S(1)}, bf16[8,8192]{1,0:T(8,128)(2,1)S(1)}, u32[]{:S(2)}, u32[]{:S(2)}) collective-permute-start(bf16[8,8192]{1,0:T(8,128)(2,1)S(1)} %get-tuple-element.13.refs_0_), channel_id=1, source_target_pairs={{0,1},{1,0},{2,3},{3,2},{4,5},{5,4},{6,7},{7,6},{8,9},{9,8},{10,11... | collective-permute-start | bytes 393224 | tf_op jit(solution)/shard_map/ppermute | solution.py:22
  35.3 4.3 %collective-permute-start.9 = (bf16[8,8192]{1,0:T(8,128)(2,1)S(1)}, bf16[8,8192]{1,0:T(8,128)(2,1)S(1)}, u32[]{:S(2)}, u32[]{:S(2)}) collective-permute-start(bf16[8,8192]{1,0:T(8,128)(2,1)S(1)} %get-tuple-element.14.refs_1_), channel_id=1, source_target_pairs={{0,1},{1,0},{2,3},{3,2},{4,5},{5,4},{6,7},{7,6},{8,9},{9,8},{10,11... | collective-permute-start | bytes 393224 | tf_op jit(solution)/shard_map/ppermute | solution.py:22
  35.8 6.7 %collective-permute-start.6 = (bf16[8,8192]{1,0:T(8,128)(2,1)S(1)}, bf16[8,8192]{1,0:T(8,128)(2,1)S(1)}, u32[]{:S(2)}, u32[]{:S(2)}) collective-permute-start(bf16[8,8192]{1,0:T(8,128)(2,1)S(1)} %collective-permute-done.2.refs_2_), channel_id=1, source_target_pairs={{0,2},{2,32},{32,34},{34,0},{1,3},{3,33},{33,35},{35,1},{4,6},{6,3... | collective-permute-start | bytes 393224 | tf_op jit(solution)/shard_map/ppermute | solution.py:22
  38.2 5.0 %collective-permute-start.7 = (bf16[8,8192]{1,0:T(8,128)(2,1)S(1)}, bf16[8,8192]{1,0:T(8,128)(2,1)S(1)}, u32[]{:S(2)}, u32[]{:S(2)}) collective-permute-start(bf16[8,8192]{1,0:T(8,128)(2,1)S(1)} %collective-permute-done.5.refs_5_), channel_id=1, source_target_pairs={{0,34},{2,0},{32,2},{34,32},{1,35},{3,1},{33,3},{35,33},{4,38},{6,... | collective-permute-start | bytes 393224 | tf_op jit(solution)/shard_map/ppermute | solution.py:22
  39.1 4.2 %collective-permute-start.10 = (bf16[8,8192]{1,0:T(8,128)(2,1)S(1)}, bf16[8,8192]{1,0:T(8,128)(2,1)S(1)}, u32[]{:S(2)}, u32[]{:S(2)}) collective-permute-start(bf16[8,8192]{1,0:T(8,128)(2,1)S(1)} %collective-permute-done.2.refs_2_), channel_id=1, source_target_pairs={{0,1},{1,0},{2,3},{3,2},{4,5},{5,4},{6,7},{7,6},{8,9},{9,8},{10,11... | collective-permute-start | bytes 393224 | tf_op jit(solution)/shard_map/ppermute | solution.py:22
  39.1 4.7 %collective-permute-start.13 = (bf16[8,8192]{1,0:T(8,128)(2,1)S(1)}, bf16[8,8192]{1,0:T(8,128)(2,1)S(1)}, u32[]{:S(2)}, u32[]{:S(2)}) collective-permute-start(bf16[8,8192]{1,0:T(8,128)(2,1)S(1)} %collective-permute-done.5.refs_5_), channel_id=1, source_target_pairs={{0,1},{1,0},{2,3},{3,2},{4,5},{5,4},{6,7},{7,6},{8,9},{9,8},{10,11... | collective-permute-start | bytes 393224 | tf_op jit(solution)/shard_map/ppermute | solution.py:22
  39.6 4.2 %collective-permute-start.11 = (bf16[8,8192]{1,0:T(8,128)(2,1)S(1)}, bf16[8,8192]{1,0:T(8,128)(2,1)S(1)}, u32[]{:S(2)}, u32[]{:S(2)}) collective-permute-start(bf16[8,8192]{1,0:T(8,128)(2,1)S(1)} %collective-permute-done.3.refs_3_), channel_id=1, source_target_pairs={{0,1},{1,0},{2,3},{3,2},{4,5},{5,4},{6,7},{7,6},{8,9},{9,8},{10,11... | collective-permute-start | bytes 393224 | tf_op jit(solution)/shard_map/ppermute | solution.py:22
  42.5 1.3 %collective-permute-start.12 = (bf16[8,8192]{1,0:T(8,128)(2,1)S(1)}, bf16[8,8192]{1,0:T(8,128)(2,1)S(1)}, u32[]{:S(2)}, u32[]{:S(2)}) collective-permute-start(bf16[8,8192]{1,0:T(8,128)(2,1)S(1)} %collective-permute-done.4.refs_4_), channel_id=1, source_target_pairs={{0,1},{1,0},{2,3},{3,2},{4,5},{5,4},{6,7},{7,6},{8,9},{9,8},{10,11... | collective-permute-start | bytes 393224 | tf_op jit(solution)/shard_map/ppermute | solution.py:22
  43.2 1.3 %collective-permute-start.14 = (bf16[8,8192]{1,0:T(8,128)(2,1)S(1)}, bf16[8,8192]{1,0:T(8,128)(2,1)S(1)}, u32[]{:S(2)}, u32[]{:S(2)}) collective-permute-start(bf16[8,8192]{1,0:T(8,128)(2,1)S(1)} %collective-permute-done.6.refs_6_), channel_id=1, source_target_pairs={{0,1},{1,0},{2,3},{3,2},{4,5},{5,4},{6,7},{7,6},{8,9},{9,8},{10,11... | collective-permute-start | bytes 393224 | tf_op jit(solution)/shard_map/ppermute | solution.py:22
  43.2 1.5 %collective-permute-start.15 = (bf16[8,8192]{1,0:T(8,128)(2,1)S(1)}, bf16[8,8192]{1,0:T(8,128)(2,1)S(1)}, u32[]{:S(2)}, u32[]{:S(2)}) collective-permute-start(bf16[8,8192]{1,0:T(8,128)(2,1)S(1)} %collective-permute-done.7.refs_7_), channel_id=1, source_target_pairs={{0,1},{1,0},{2,3},{3,2},{4,5},{5,4},{6,7},{7,6},{8,9},{9,8},{10,11... | collective-permute-start | bytes 393224 | tf_op jit(solution)/shard_map/ppermute | solution.py:22
  55.1 2.7 %collective-permute-start.16 = (bf16[64,8192]{1,0:T(8,128)(2,1)S(1)}, bf16[64,8192]{1,0:T(8,128)(2,1)S(1)}, u32[]{:S(2)}, u32[]{:S(2)}) collective-permute-start(bf16[64,8192]{1,0:T(8,128)(2,1)S(1)} %get-tuple-element.16), channel_id=1, source_target_pairs={{0,1},{1,0},{2,3},{3,2},{4,5},{5,4},{6,7},{7,6},{8,9},{9,8},{10,11... | collective-permute-start | bytes 3145736 | tf_op jit(solution)/shard_map/ppermute | solution.py:22
  58.2 6.4 %collective-permute-start.18 = (bf16[8,8192]{1,0:T(8,128)(2,1)S(1)}, bf16[8,8192]{1,0:T(8,128)(2,1)S(1)}, u32[]{:S(2)}, u32[]{:S(2)}) collective-permute-start(bf16[8,8192]{1,0:T(8,128)(2,1)S(1)} %get-tuple-element.26), channel_id=1, source_target_pairs={{0,34},{2,0},{32,2},{34,32},{1,35},{3,1},{33,3},{35,33},{4,38},{6,... | collective-permute-start | bytes 393224 | tf_op jit(solution)/shard_map/ppermute | solution.py:22
  60.5 7.6 %collective-permute-start.21 = (bf16[8,8192]{1,0:T(8,128)(2,1)S(1)}, bf16[8,8192]{1,0:T(8,128)(2,1)S(1)}, u32[]{:S(2)}, u32[]{:S(2)}) collective-permute-start(bf16[8,8192]{1,0:T(8,128)(2,1)S(1)} %get-tuple-element.24), channel_id=1, source_target_pairs={{0,2},{2,32},{32,34},{34,0},{1,3},{3,33},{33,35},{35,1},{4,6},{6,3... | collective-permute-start | bytes 393224 | tf_op jit(solution)/shard_map/ppermute | solution.py:22
  60.5 9.7 %collective-permute-start.17 = (bf16[8,8192]{1,0:T(8,128)(2,1)S(1)}, bf16[8,8192]{1,0:T(8,128)(2,1)S(1)}, u32[]{:S(2)}, u32[]{:S(2)}) collective-permute-start(bf16[8,8192]{1,0:T(8,128)(2,1)S(1)} %get-tuple-element.23), channel_id=1, source_target_pairs={{0,2},{2,32},{32,34},{34,0},{1,3},{3,33},{33,35},{35,1},{4,6},{6,3... | collective-permute-start | bytes 393224 | tf_op jit(solution)/shard_map/ppermute | solution.py:22
  60.6 9.7 %collective-permute-start.20 = (bf16[8,8192]{1,0:T(8,128)(2,1)S(1)}, bf16[8,8192]{1,0:T(8,128)(2,1)S(1)}, u32[]{:S(2)}, u32[]{:S(2)}) collective-permute-start(bf16[8,8192]{1,0:T(8,128)(2,1)S(1)} %get-tuple-element.25), channel_id=1, source_target_pairs={{0,34},{2,0},{32,2},{34,32},{1,35},{3,1},{33,3},{35,33},{4,38},{6,... | collective-permute-start | bytes 393224 | tf_op jit(solution)/shard_map/ppermute | solution.py:22
  68.2 5.0 %collective-permute-start.19 = (bf16[8,8192]{1,0:T(8,128)(2,1)S(1)}, bf16[8,8192]{1,0:T(8,128)(2,1)S(1)}, u32[]{:S(2)}, u32[]{:S(2)}) collective-permute-start(bf16[8,8192]{1,0:T(8,128)(2,1)S(1)} %get-tuple-element.21), channel_id=1, source_target_pairs={{0,34},{2,0},{32,2},{34,32},{1,35},{3,1},{33,3},{35,33},{4,38},{6,... | collective-permute-start | bytes 393224 | tf_op jit(solution)/shard_map/ppermute | solution.py:22
  68.3 6.3 %collective-permute-start.22 = (bf16[8,8192]{1,0:T(8,128)(2,1)S(1)}, bf16[8,8192]{1,0:T(8,128)(2,1)S(1)}, u32[]{:S(2)}, u32[]{:S(2)}) collective-permute-start(bf16[8,8192]{1,0:T(8,128)(2,1)S(1)} %get-tuple-element.22), channel_id=1, source_target_pairs={{0,2},{2,32},{32,34},{34,0},{1,3},{3,33},{33,35},{35,1},{4,6},{6,3... | collective-permute-start | bytes 393224 | tf_op jit(solution)/shard_map/ppermute | solution.py:22
  88.0 5.2 %collective-permute-start.23 = (f32[1,8192]{1,0:T(1,128)S(1)}, f32[1,8192]{1,0:T(1,128)S(1)}, u32[]{:S(2)}, u32[]{:S(2)}) collective-permute-start(f32[1,8192]{1,0:T(1,128)S(1)} %get-tuple-element.28), channel_id=1, source_target_pairs={{0,192},{64,128},{128,64},{192,0},{1,193},{65,129},{129,65},{193,1... | collective-permute-start | bytes 98312 | tf_op jit(solution)/shard_map/ppermute | solution.py:30
  91.0 5.4 %collective-permute-start.24 = (f32[1,8192]{1,0:T(1,128)S(1)}, f32[1,8192]{1,0:T(1,128)S(1)}, u32[]{:S(2)}, u32[]{:S(2)}) collective-permute-start(f32[1,8192]{1,0:T(1,128)S(1)} %get-tuple-element.27), channel_id=1, source_target_pairs={{0,128},{64,192},{128,0},{192,64},{1,129},{65,193},{129,1},{193,65... | collective-permute-start | bytes 98312 | tf_op jit(solution)/shard_map/ppermute | solution.py:34

commit v3 on v2

--- a/solution.py
+++ b/solution.py
@@ -1,3 +1,5 @@
+import functools
+
 import jax
 import jax.numpy as jnp
 from jax import lax
@@ -46,36 +48,68 @@
     return value.astype(jnp.bfloat16)
 
 
-def pairs_kernel(pairs_ref, first_ref, second_ref):
-    for i in range(4):
-        first_ref[pl.ds(2 * i, 2), :] = pairs_ref[i]
-        second_ref[pl.ds(2 * i, 2), :] = pairs_ref[4 + i]
+def spread_kernel(near_ref, far_ref, copies_ref):
+    near, far = near_ref[...], far_ref[...]
+    for i in range(copies_ref.shape[0]):
+        copies_ref[i, pl.ds(0, 1), :] = near
+        copies_ref[i, pl.ds(1, 1), :] = far
+
+
+def spread(near, far):
+    in_vmem = pl.BlockSpec(memory_space=pltpu.VMEM)
+    return pl.pallas_call(
+        spread_kernel,
+        out_shape=pltpu.VMEM((8, 2, near.shape[-1]), near.dtype),
+        in_specs=[in_vmem, in_vmem],
+        out_specs=in_vmem,
+        compiler_params=pltpu.CompilerParams(vmem_limit_bytes=4 << 20),
+    )(near, far)
+
+
+def pairs_kernel(pairs_ref, rows_ref):
+    for i in range(pairs_ref.shape[0]):
+        rows_ref[pl.ds(2 * i, 2), :] = pairs_ref[i]
 
 
 def rows_of_pairs(pairs):
-    half = pltpu.VMEM((8, pairs.shape[-1]), pairs.dtype)
-    in_vmem = pl.BlockSpec(memory_space=pltpu.VMEM)
-    return pl.pallas_call(
-        pairs_kernel, out_shape=(half, half), in_specs=[in_vmem], out_specs=(in_vmem, in_vmem)
+    count, _, width = pairs.shape
+    in_vmem = pl.BlockSpec(memory_space=pltpu.VMEM)
+    return pl.pallas_call(
+        pairs_kernel,
+        out_shape=pltpu.VMEM((2 * count, width), pairs.dtype),
+        in_specs=[in_vmem],
+        out_specs=in_vmem,
+        compiler_params=pltpu.CompilerParams(vmem_limit_bytes=4 << 20),
     )(pairs)
 
 
-def gathered_blocks(row):
-    pair = jnp.concatenate([mirrored(row), opposite(row)], 0)
-    planes, width = pair.shape
-    depth = lax.axis_size("z")
-    pairs = lax.all_to_all(
-        jnp.broadcast_to(pair[None], (depth, planes, width)), "z", 0, 0, tiled=True
-    )
-    first, second = rows_of_pairs(pairs)
-    low = shifted(first, X, 1)
-    high = shifted(second, X, -1)
-    low_rest = shifted(second, X, 1)
-    high_rest = shifted(first, X, -1)
-    low_far = shifted(low, X, 1)
-    high_far = shifted(high, X, -1)
-    blocks = [first, second, low, low_rest, high_rest, high, low_far, high_far]
-    return blocks + [swapped(b) for b in blocks]
+def half_kernel(block_ref, token_ref, half_ref, *, start):
+    half_ref[...] = block_ref[pl.ds(start, half_ref.shape[0]), :]
+
+
+def half_of(block, start, token):
+    rows, width = block.shape
+    in_vmem = pl.BlockSpec(memory_space=pltpu.VMEM)
+    return pl.pallas_call(
+        functools.partial(half_kernel, start=start),
+        out_shape=pltpu.VMEM((rows // 2, width), block.dtype),
+        in_specs=[in_vmem, pl.BlockSpec(memory_space=pl.ANY)],
+        out_specs=in_vmem,
+        compiler_params=pltpu.CompilerParams(vmem_limit_bytes=4 << 20),
+    )(block, token)
+
+
+def gathered_blocks(row, weights):
+    copies = spread(mirrored(row), opposite(row))
+    pairs = lax.all_to_all(copies, "z", 0, 0, tiled=True)
+    block = rows_of_pairs(pairs)
+    *weights, token = loaded(weights, block)
+    low = shifted(block, X, 1)
+    high = shifted(block, X, -1)
+    low_far = shifted(half_of(low, 0, token), X, 1)
+    high_far = shifted(half_of(high, 8, token), X, -1)
+    blocks = [block, low, high, low_far, high_far]
+    return blocks + [swapped(b) for b in blocks], weights
 
 
 def returned_rows(keep, send):
@@ -98,72 +132,70 @@
     return mirrored(pair[:1]) + opposite(pair[1:])
 
 
-CHUNKS = 4
+def load_kernel(*refs):
+    sources, targets, token_ref, sems = refs[:3], refs[4:7], refs[7], refs[8]
+    copies = []
+    parts = 2
+    for w, (source, target) in enumerate(zip(sources, targets)):
+        size = source.shape[0] // parts
+        for i in range(parts):
+            rows = pl.ds(i * size, size)
+            copies.append(pltpu.make_async_copy(source.at[rows], target.at[rows], sems.at[w * parts + i]))
+    for copy in copies:
+        copy.start()
+    token_ref[...] = jnp.zeros_like(token_ref)
+    for copy in copies:
+        copy.wait()
+
+
+def loaded(weights, rows):
+    in_vmem = pl.BlockSpec(memory_space=pltpu.VMEM)
+    return pl.pallas_call(
+        load_kernel,
+        out_shape=tuple(pltpu.VMEM(w.shape, w.dtype) for w in weights) + (pltpu.VMEM((8, 128), jnp.float32),),
+        in_specs=[pl.BlockSpec(memory_space=pltpu.HBM)] * 3 + [pl.BlockSpec(memory_space=pl.ANY)],
+        out_specs=(in_vmem,) * 4,
+        scratch_shapes=[pltpu.SemaphoreType.DMA((6,))],
+        compiler_params=pltpu.CompilerParams(vmem_limit_bytes=12 << 20),
+    )(*(in_hbm(w) for w in weights), rows)
 
 
 def feed_kernel(*refs):
-    blocks, rest = refs[:16], refs[16:]
-    gate_hbm, up_hbm, down_hbm, keep_ref, send_ref, rows_ref, gate_ref, up_ref, down_ref, row_sems, sems = rest
-    width = rows_ref.shape[1]
-    part = width // CHUNKS
-    row_copies = []
-    for i, block in enumerate(blocks):
+    blocks, (gate_ref, up_ref, down_ref, keep_ref, send_ref, rows_ref) = refs[:-6], refs[-6:]
+    at = 0
+    for block in blocks:
         size = block.shape[0]
-        row_copies.append(
-            pltpu.make_async_copy(block, rows_ref.at[pl.ds(i * size, size)], row_sems.at[i])
-        )
-    weight_copies = []
-    for k in range(CHUNKS):
-        for w, (hbm, vmem) in enumerate(((gate_hbm, gate_ref), (up_hbm, up_ref))):
-            columns = pl.ds(k * part, part)
-            weight_copies.append(
-                pltpu.make_async_copy(hbm.at[:, columns], vmem.at[:, columns], sems.at[2 * k + w])
-            )
-    down_copy = pltpu.make_async_copy(down_hbm, down_ref, sems.at[2 * CHUNKS])
-    for copy in row_copies + weight_copies + [down_copy]:
-        copy.start()
-    for copy in row_copies:
-        copy.wait()
+        rows_ref[pl.ds(at, size), :] = block[...]
+        at += size
+    rows = rows_ref[...]
     numbers = (((1,), (1,)), ((), ()))
-    gate = jnp.zeros((rows_ref.shape[0], gate_ref.shape[0]), jnp.float32)
-    up = gate
-    for k in range(CHUNKS):
+    gate = lax.dot_general(gate_ref[...], rows, numbers, preferred_element_type=jnp.float32)
+    up = lax.dot_general(up_ref[...], rows, numbers, preferred_element_type=jnp.float32)
+    act = (gate / (1.0 + jnp.exp(-gate)) * up).T.astype(jnp.bfloat16)
+    half = at // 2
+    part = 1024
+    for k in range(rows_ref.shape[1] // part):
         columns = pl.ds(k * part, part)
-        rows = rows_ref[:, columns]
-        weight_copies[2 * k].wait()
-        gate = gate + lax.dot_general(rows, gate_ref[:, columns], numbers, preferred_element_type=jnp.float32)
-        weight_copies[2 * k + 1].wait()
-        up = up + lax.dot_general(rows, up_ref[:, columns], numbers, preferred_element_type=jnp.float32)
-    act = (gate / (1.0 + jnp.exp(-gate)) * up).astype(jnp.bfloat16)
-    down_copy.wait()
-    half = rows_ref.shape[0] // 2
-    send_ref[...] = jnp.dot(act[half:], down_ref[...], preferred_element_type=jnp.float32).astype(jnp.bfloat16)
-    keep_ref[...] = jnp.dot(act[:half], down_ref[...], preferred_element_type=jnp.float32)
-
-
-def feed_rows(blocks, gate_weight, up_weight, down_weight):
-    units, width = gate_weight.shape[1:]
-    anywhere = pl.BlockSpec(memory_space=pl.ANY)
-    in_vmem = pl.BlockSpec(memory_space=pltpu.VMEM)
-    held = pltpu.VMEM((units, width), jnp.bfloat16)
+        feed = jnp.dot(act, down_ref[:, columns], preferred_element_type=jnp.float32)
+        keep_ref[:, columns] = feed[:half]
+        send_ref[:, columns] = feed[half:].astype(jnp.bfloat16)
+
+
+def feed_rows(blocks, weights):
+    width = weights[0].shape[-1]
+    in_vmem = pl.BlockSpec(memory_space=pltpu.VMEM)
+    held = [pltpu.with_memory_space_constraint(w, pltpu.VMEM) for w in weights]
     return pl.pallas_call(
         feed_kernel,
         out_shape=(
-            jax.ShapeDtypeStruct((64, width), jnp.float32),
-            jax.ShapeDtypeStruct((64, width), jnp.bfloat16),
+            pltpu.VMEM((64, width), jnp.float32),
+            pltpu.VMEM((64, width), jnp.bfloat16),
         ),
-        in_specs=[anywhere] * len(blocks) + [pl.BlockSpec(memory_space=pltpu.HBM)] * 3,
+        in_specs=[in_vmem] * (len(blocks) + 3),
         out_specs=(in_vmem, in_vmem),
-        scratch_shapes=[
-            pltpu.VMEM((128, width), jnp.bfloat16),
-            held,
-            held,
-            held,
-            pltpu.SemaphoreType.DMA((16,)),
-            pltpu.SemaphoreType.DMA((2 * CHUNKS + 1,)),
-        ],
-        compiler_params=pltpu.CompilerParams(vmem_limit_bytes=28 << 20),
-    )(*blocks, *(in_hbm(w[0]) for w in (gate_weight, up_weight, down_weight)))
+        scratch_shapes=[pltpu.VMEM((128, width), jnp.bfloat16)],
+        compiler_params=pltpu.CompilerParams(vmem_limit_bytes=12 << 20),
+    )(*blocks, *held)
 
 
 def attend_kernel(
@@ -298,7 +330,8 @@
     hidden, flat_rows = attend(
         lengths, key_cache, value_cache, queries, new_keys, new_values, residual, norm_gain
     )
-    keep, send = feed_rows(gathered_blocks(flat_rows), gate_weight, up_weight, down_weight)
+    weights = gate_weight[0], up_weight[0], down_weight[0]
+    keep, send = feed_rows(*gathered_blocks(flat_rows, weights))
     summed = returned_rows(keep, send)
     mixed = (hidden + summed).astype(jnp.bfloat16)
     mixed = jnp.where(serving, mixed, jnp.zeros_like(mixed))

time: 97.3 us -> 88.9 us (0.914)
  Pallas kernels: 13.5 us -> 8.95 us
  starting transfers between devices: 24 us -> 20.7 us
    pallas_call x2 -> x6, Pallas kernels: 11.5 us -> 6.89 us  [the longest x1 4.02 us: loaded(): pl.pallas_call(load_kernel, out_shape=tuple((pltpu.VMEM(w.shape, w.dtype)...]
    ppermute x21 -> x16, starting transfers between devices: 18.1 us -> 14.8 us  [shifted(): lax.ppermute(value, axes, [(i, (i + hops) % size) for i in range(size)])]
    ppermute x21 -> x16, waiting for transfers between devices: 16.9 us -> 16.7 us  [shifted(): lax.ppermute(value, axes, [(i, (i + hops) % size) for i in range(size)])]
  transfers between devices with their start and end apart: 25 -> 20, of which waited for: 15 -> 12; matrix products, arithmetic and copies ran while one was open for 0% -> 0% of each run, Pallas kernels for 0% -> 5%
where the time goes in v3:
time: 88.9 us; the launch traced here: 88.8 us
  blocking collectives  30 us (34%)
  waiting for transfers between devices  26.7 us (30%)
  starting transfers between devices  20.7 us (23%)
  Pallas kernels  8.95 us (10%)
  other arithmetic  1.35 us (2%)
    all_to_all x1, blocking collectives, gathered_blocks(): pairs = lax.all_to_all(copies, 'z', 0, 0, tiled=True)  17.1 us
    ppermute x16, waiting for transfers between devices, shifted(): lax.ppermute(value, axes, [(i, (i + hops) % size) for i in range(size)])  16.7 us
    ppermute x16, starting transfers between devices, shifted(): lax.ppermute(value, axes, [(i, (i + hops) % size) for i in range(size)])  14.8 us
    all_to_all x1, blocking collectives, returned_rows(): arrived = lax.all_to_all(pieces, 'z', 0, 0, tiled=True)  12.9 us
    ppermute x2, waiting for transfers between devices, opposite(): return lax.ppermute(value, 'y', [(i, (i + 2) % 4) for i in range(4)])  5.45 us
    ppermute x2, starting transfers between devices, mirrored(): return lax.ppermute(value, 'y', [(i, 3 - i) for i in range(4)])  5.03 us
    ppermute x2, waiting for transfers between devices, mirrored(): return lax.ppermute(value, 'y', [(i, 3 - i) for i in range(4)])  4.52 us
    pallas_call x1, Pallas kernels, loaded(): pl.pallas_call(load_kernel, out_shape=tuple((pltpu.VMEM(w.shape, w.dtype)...  4.02 us
  transfers between devices with their start and end apart: 20, of which 12 were waited for; matrix products, arithmetic and copies ran while one was open for 0% of the time, Pallas kernels for 5%

profile of v3, /device:TPU:24, one launch (start us, length us, event | category | flops | bytes accessed | tf_op | source)
XLA Modules:
  0.0 88.8 jit_solution(11286313392594831192)
XLA Ops:
  0.7 2.1 %shard_map.109 = (f32[1,8192]{1,0:T(1,128)S(1)}, bf16[1,8192]{1,0:T(2,128)(2,1)S(1)}) custom-call(s32[1,1]{1,0:T(1,128)S(6)} %copy.12.length_ref, bf16[768,512]{1,0:T(8,128)(2,1)} %bitcast.15, bf16[768,512]{1,0:T(8,128)(2,1)} %bitcast.16, bf16[1,8192]{1,0:T(2,128)(2,1)} %bitcast.17, bf16[1,512]{1,0:T(2,128)(2,1)} %bitcast.20, bf16[1,512]{1,0:T(2,128)(2,1)} %bitcast.21, ...), custom_call_target="tpu_custom_call" | custom-call | tf_op jit(solution)/shard_map/pallas_call | solution.py:292
  2.7 2.0 %collective-permute-start = (bf16[1,8192]{1,0:T(2,128)(2,1)S(1)}, bf16[1,8192]{1,0:T(2,128)(2,1)S(1)}, u32[]{:S(2)}, u32[]{:S(2)}) collective-permute-start(bf16[1,8192]{1,0:T(2,128)(2,1)S(1)} %get-tuple-element.14), channel_id=1, source_target_pairs={{0,192},{64,128},{128,64},{192,0},{1,193},{65,129},{129,65},{193,1... | collective-permute-start | bytes 49160 | tf_op jit(solution)/shard_map/ppermute | solution.py:32
  4.8 0.9 collective-permute-start.1
  5.6 2.3 %collective-permute-done.near_ref = bf16[1,8192]{1,0:T(2,128)(2,1)S(1)} collective-permute-done((bf16[1,8192]{1,0:T(2,128)(2,1)S(1)}, bf16[1,8192]{1,0:T(2,128)(2,1)S(1)}, u32[]{:S(2)}, u32[]{:S(2)}) %collective-permute-start) | collective-permute-done | bytes 16416 | tf_op jit(solution)/shard_map/ppermute | solution.py:32
  7.9 2.3 %collective-permute-done.1.far_ref = bf16[1,8192]{1,0:T(2,128)(2,1)S(1)} collective-permute-done((bf16[1,8192]{1,0:T(2,128)(2,1)S(1)}, bf16[1,8192]{1,0:T(2,128)(2,1)S(1)}, u32[]{:S(2)}, u32[]{:S(2)}) %collective-permute-start.1) | collective-permute-done | bytes 16416 | tf_op jit(solution)/shard_map/ppermute | solution.py:36
  10.2 17.1 %all_to_all.10.pairs_ref = bf16[8,2,8192]{2,1,0:T(2,128)(2,1)S(1)} all-to-all(bf16[8,2,8192]{2,1,0:T(2,128)(2,1)S(1)} %shard_map.110), channel_id=1, replica_groups=mesh['y'=4,'xh'=2,'z'=8,'xl'=2,'c'=2] {'z'}, dimensions={0} | all-to-all | bytes 524288 | tf_op jit(solution)/shard_map/all_to_all | solution.py:104
  27.4 0.1 shard_map.111.refs_3_.refs_0_
  27.5 2.8 %collective-permute-start.3 = (bf16[16,8192]{1,0:T(8,128)(2,1)S(1)}, bf16[16,8192]{1,0:T(8,128)(2,1)S(1)}, u32[]{:S(2)}, u32[]{:S(2)}) collective-permute-start(bf16[16,8192]{1,0:T(8,128)(2,1)S(1)} %shard_map.111.refs_3_.refs_0_), channel_id=1, source_target_pairs={{0,34},{2,0},{32,2},{34,32},{1,35},{3,1},{33,3},{35,33},{4,38},{6,... | collective-permute-start | bytes 786440 | tf_op jit(solution)/shard_map/ppermute | solution.py:24
  30.3 0.0 collective-permute-start.2
  30.4 0.0 collective-permute-start.6
  30.4 4.0 %shard_map.112 = (bf16[208,8192]{1,0:T(8,128)(2,1)S(1)}, bf16[208,8192]{1,0:T(8,128)(2,1)S(1)}, bf16[208,8192]{1,0:T(8,128)(2,1)S(1)}, f32[8,128]{1,0:T(8,128)S(1)}) custom-call(bf16[208,8192]{1,0:T(8,128)(2,1)} %bitcast.12, bf16[208,8192]{1,0:T(8,128)(2,1)} %bitcast.13, bf16[208,8192]{1,0:T(8,128)(2,1)} %bitcast.14, ...), custom_call_target="tpu_custom_call" | custom-call | tf_op jit(solution)/shard_map/pallas_call | solution.py:153
  34.4 0.0 collective-permute-done.3.block_ref.refs_2_
  34.4 3.6 %collective-permute-start.5 = (bf16[8,8192]{1,0:T(8,128)(2,1)S(1)}, bf16[8,8192]{1,0:T(8,128)(2,1)S(1)}, u32[]{:S(2)}, u32[]{:S(2)}) collective-permute-start(bf16[8,8192]{1,0:T(8,128)(2,1)S(1)} %shard_map.114), channel_id=1, source_target_pairs={{0,34},{2,0},{32,2},{34,32},{1,35},{3,1},{33,3},{35,33},{4,38},{6,... | collective-permute-start | bytes 393224 | tf_op jit(solution)/shard_map/ppermute | solution.py:24
  38.0 0.0 collective-permute-done.2.block_ref.refs_1_
  38.0 0.1 collective-permute-start.4
  38.1 0.1 collective-permute-start.7
  38.2 0.5 collective-permute-start.8
  38.7 2.4 %collective-permute-done.5.refs_4_ = bf16[8,8192]{1,0:T(8,128)(2,1)S(1)} collective-permute-done((bf16[8,8192]{1,0:T(8,128)(2,1)S(1)}, bf16[8,8192]{1,0:T(8,128)(2,1)S(1)}, u32[]{:S(2)}, u32[]{:S(2)}) %collective-permute-start.5) | collective-permute-done | bytes 131104 | tf_op jit(solution)/shard_map/ppermute | solution.py:24
  41.2 3.5 %collective-permute-done.4.refs_3_ = bf16[8,8192]{1,0:T(8,128)(2,1)S(1)} collective-permute-done((bf16[8,8192]{1,0:T(8,128)(2,1)S(1)}, bf16[8,8192]{1,0:T(8,128)(2,1)S(1)}, u32[]{:S(2)}, u32[]{:S(2)}) %collective-permute-start.4) | collective-permute-done | bytes 131104 | tf_op jit(solution)/shard_map/ppermute | solution.py:24
  44.7 0.0 collective-permute-start.9
  44.7 0.0 collective-permute-done.6.refs_5_
  44.7 0.0 collective-permute-done.10.refs_9_
  44.7 1.3 %collective-permute-done.9.refs_8_ = bf16[8,8192]{1,0:T(8,128)(2,1)S(1)} collective-permute-done((bf16[8,8192]{1,0:T(8,128)(2,1)S(1)}, bf16[8,8192]{1,0:T(8,128)(2,1)S(1)}, u32[]{:S(2)}, u32[]{:S(2)}) %collective-permute-start.9) | collective-permute-done | bytes 131104 | tf_op jit(solution)/shard_map/ppermute | solution.py:24
  46.0 2.7 %shard_map.115 = (f32[64,8192]{1,0:T(8,128)S(1)}, bf16[64,8192]{1,0:T(8,128)(2,1)S(1)}) custom-call(bf16[16,8192]{1,0:T(8,128)(2,1)S(1)} %shard_map.111.refs_3_.refs_0_, bf16[16,8192]{1,0:T(8,128)(2,1)S(1)} %collective-permute-done.2.block_ref.refs_1_, bf16[16,8192]{1,0:T(8,128)(2,1)S(1)} %collective-permute-done.3.block_ref.refs_2_, ...), custom_call_target="tpu_custom_call" | custom-call | tf_op jit(solution)/shard_map/pallas_call | solution.py:188
  48.7 0.2 collective-permute-start.11
  48.9 2.5 %collective-permute-done.11 = bf16[64,8192]{1,0:T(8,128)(2,1)S(1)} collective-permute-done((bf16[64,8192]{1,0:T(8,128)(2,1)S(1)}, bf16[64,8192]{1,0:T(8,128)(2,1)S(1)}, u32[]{:S(2)}, u32[]{:S(2)}) %collective-permute-start.11) | collective-permute-done | bytes 1048608 | tf_op jit(solution)/shard_map/ppermute | solution.py:24
  51.4 0.3 fusion.7
  51.8 0.4 collective-permute-start.13
  52.2 1.7 %collective-permute-start.16 = (bf16[8,8192]{1,0:T(8,128)(2,1)S(1)}, bf16[8,8192]{1,0:T(8,128)(2,1)S(1)}, u32[]{:S(2)}, u32[]{:S(2)}) collective-permute-start(bf16[8,8192]{1,0:T(8,128)(2,1)S(1)} %get-tuple-element.28), channel_id=1, source_target_pairs={{0,2},{2,32},{32,34},{34,0},{1,3},{3,33},{33,35},{35,1},{4,6},{6,3... | collective-permute-start | bytes 393224 | tf_op jit(solution)/shard_map/ppermute | solution.py:24
  53.9 0.0 collective-permute-start.12
  53.9 3.2 %collective-permute-start.15 = (bf16[8,8192]{1,0:T(8,128)(2,1)S(1)}, bf16[8,8192]{1,0:T(8,128)(2,1)S(1)}, u32[]{:S(2)}, u32[]{:S(2)}) collective-permute-start(bf16[8,8192]{1,0:T(8,128)(2,1)S(1)} %get-tuple-element.29), channel_id=1, source_target_pairs={{0,34},{2,0},{32,2},{34,32},{1,35},{3,1},{33,3},{35,33},{4,38},{6,... | collective-permute-start | bytes 393224 | tf_op jit(solution)/shard_map/ppermute | solution.py:24
  57.1 1.1 %collective-permute-done.13 = bf16[8,8192]{1,0:T(8,128)(2,1)S(1)} collective-permute-done((bf16[8,8192]{1,0:T(8,128)(2,1)S(1)}, bf16[8,8192]{1,0:T(8,128)(2,1)S(1)}, u32[]{:S(2)}, u32[]{:S(2)}) %collective-permute-start.13) | collective-permute-done | bytes 131104 | tf_op jit(solution)/shard_map/ppermute | solution.py:24
  58.2 1.6 %collective-permute-done.16 = bf16[8,8192]{1,0:T(8,128)(2,1)S(1)} collective-permute-done((bf16[8,8192]{1,0:T(8,128)(2,1)S(1)}, bf16[8,8192]{1,0:T(8,128)(2,1)S(1)}, u32[]{:S(2)}, u32[]{:S(2)}) %collective-permute-start.16) | collective-permute-done | bytes 131104 | tf_op jit(solution)/shard_map/ppermute | solution.py:24
  59.8 0.1 fusion.3
  59.8 0.1 collective-permute-start.14
  59.9 2.0 %collective-permute-start.17 = (bf16[8,8192]{1,0:T(8,128)(2,1)S(1)}, bf16[8,8192]{1,0:T(8,128)(2,1)S(1)}, u32[]{:S(2)}, u32[]{:S(2)}) collective-permute-start(bf16[8,8192]{1,0:T(8,128)(2,1)S(1)} %get-tuple-element.26), channel_id=1, source_target_pairs={{0,2},{2,32},{32,34},{34,0},{1,3},{3,33},{33,35},{35,1},{4,6},{6,3... | collective-permute-start | bytes 393224 | tf_op jit(solution)/shard_map/ppermute | solution.py:24
  61.9 2.9 %collective-permute-done.14 = bf16[8,8192]{1,0:T(8,128)(2,1)S(1)} collective-permute-done((bf16[8,8192]{1,0:T(8,128)(2,1)S(1)}, bf16[8,8192]{1,0:T(8,128)(2,1)S(1)}, u32[]{:S(2)}, u32[]{:S(2)}) %collective-permute-start.14) | collective-permute-done | bytes 131104 | tf_op jit(solution)/shard_map/ppermute | solution.py:24
  64.9 1.3 %collective-permute-done.17 = bf16[8,8192]{1,0:T(8,128)(2,1)S(1)} collective-permute-done((bf16[8,8192]{1,0:T(8,128)(2,1)S(1)}, bf16[8,8192]{1,0:T(8,128)(2,1)S(1)}, u32[]{:S(2)}, u32[]{:S(2)}) %collective-permute-start.17) | collective-permute-done | bytes 131104 | tf_op jit(solution)/shard_map/ppermute | solution.py:24
  66.2 0.1 fusion.5
  66.3 0.2 reshape.34
  66.5 12.9 %all_to_all.11 = bf16[8,2,8192]{2,1,0:T(2,128)(2,1)S(1)} all-to-all(bf16[8,2,8192]{2,1,0:T(2,128)(2,1)S(1)} %reshape.34), channel_id=1, replica_groups=mesh['y'=4,'xh'=2,'z'=8,'xl'=2,'c'=2] {'z'}, dimensions={0} | all-to-all | bytes 524288 | tf_op jit(solution)/shard_map/all_to_all | solution.py:130
  79.4 0.2 convert_reduce_fusion
  79.6 0.1 fusion.9
  79.7 3.0 %collective-permute-start.18 = (f32[1,8192]{1,0:T(1,128)S(1)}, f32[1,8192]{1,0:T(1,128)S(1)}, u32[]{:S(2)}, u32[]{:S(2)}) collective-permute-start(f32[1,8192]{1,0:T(1,128)S(1)} %get-tuple-element.32), channel_id=1, source_target_pairs={{0,192},{64,128},{128,64},{192,0},{1,193},{65,129},{129,65},{193,1... | collective-permute-start | bytes 98312 | tf_op jit(solution)/shard_map/ppermute | solution.py:32
  82.7 0.0 collective-permute-start.19
  82.7 2.2 %collective-permute-done.18 = f32[1,8192]{1,0:T(1,128)S(1)} collective-permute-done((f32[1,8192]{1,0:T(1,128)S(1)}, f32[1,8192]{1,0:T(1,128)S(1)}, u32[]{:S(2)}, u32[]{:S(2)}) %collective-permute-start.18) | collective-permute-done | bytes 32800 | tf_op jit(solution)/shard_map/ppermute | solution.py:32
  84.9 3.2 %collective-permute-done.19 = f32[1,8192]{1,0:T(1,128)S(1)} collective-permute-done((f32[1,8192]{1,0:T(1,128)S(1)}, f32[1,8192]{1,0:T(1,128)S(1)}, u32[]{:S(2)}, u32[]{:S(2)}) %collective-permute-start.19) | collective-permute-done | bytes 32800 | tf_op jit(solution)/shard_map/ppermute | solution.py:36
  88.1 0.7 fusion.6
  (10 shorter events, 0.1 us)
Async XLA Ops:
  2.7 5.2 %collective-permute-start = (bf16[1,8192]{1,0:T(2,128)(2,1)S(1)}, bf16[1,8192]{1,0:T(2,128)(2,1)S(1)}, u32[]{:S(2)}, u32[]{:S(2)}) collective-permute-start(bf16[1,8192]{1,0:T(2,128)(2,1)S(1)} %get-tuple-element.14), channel_id=1, source_target_pairs={{0,192},{64,128},{128,64},{192,0},{1,193},{65,129},{129,65},{193,1... | collective-permute-start | bytes 49160 | tf_op jit(solution)/shard_map/ppermute | solution.py:32
  4.8 5.4 %collective-permute-start.1 = (bf16[1,8192]{1,0:T(2,128)(2,1)S(1)}, bf16[1,8192]{1,0:T(2,128)(2,1)S(1)}, u32[]{:S(2)}, u32[]{:S(2)}) collective-permute-start(bf16[1,8192]{1,0:T(2,128)(2,1)S(1)} %get-tuple-element.14), channel_id=1, source_target_pairs={{0,128},{64,192},{128,0},{192,64},{1,129},{65,193},{129,1},{193,65... | collective-permute-start | bytes 49160 | tf_op jit(solution)/shard_map/ppermute | solution.py:36
  27.5 6.9 %collective-permute-start.3 = (bf16[16,8192]{1,0:T(8,128)(2,1)S(1)}, bf16[16,8192]{1,0:T(8,128)(2,1)S(1)}, u32[]{:S(2)}, u32[]{:S(2)}) collective-permute-start(bf16[16,8192]{1,0:T(8,128)(2,1)S(1)} %shard_map.111.refs_3_.refs_0_), channel_id=1, source_target_pairs={{0,34},{2,0},{32,2},{34,32},{1,35},{3,1},{33,3},{35,33},{4,38},{6,... | collective-permute-start | bytes 786440 | tf_op jit(solution)/shard_map/ppermute | solution.py:24
  30.3 7.7 %collective-permute-start.2 = (bf16[16,8192]{1,0:T(8,128)(2,1)S(1)}, bf16[16,8192]{1,0:T(8,128)(2,1)S(1)}, u32[]{:S(2)}, u32[]{:S(2)}) collective-permute-start(bf16[16,8192]{1,0:T(8,128)(2,1)S(1)} %shard_map.111.refs_3_.refs_0_), channel_id=1, source_target_pairs={{0,2},{2,32},{32,34},{34,0},{1,3},{3,33},{33,35},{35,1},{4,6},{6,3... | collective-permute-start | bytes 786440 | tf_op jit(solution)/shard_map/ppermute | solution.py:24
  30.4 14.3 %collective-permute-start.6 = (bf16[16,8192]{1,0:T(8,128)(2,1)S(1)}, bf16[16,8192]{1,0:T(8,128)(2,1)S(1)}, u32[]{:S(2)}, u32[]{:S(2)}) collective-permute-start(bf16[16,8192]{1,0:T(8,128)(2,1)S(1)} %shard_map.111.refs_3_.refs_0_), channel_id=1, source_target_pairs={{0,1},{1,0},{2,3},{3,2},{4,5},{5,4},{6,7},{7,6},{8,9},{9,8},{10,11... | collective-permute-start | bytes 786440 | tf_op jit(solution)/shard_map/ppermute | solution.py:24
  34.4 6.7 %collective-permute-start.5 = (bf16[8,8192]{1,0:T(8,128)(2,1)S(1)}, bf16[8,8192]{1,0:T(8,128)(2,1)S(1)}, u32[]{:S(2)}, u32[]{:S(2)}) collective-permute-start(bf16[8,8192]{1,0:T(8,128)(2,1)S(1)} %shard_map.114), channel_id=1, source_target_pairs={{0,34},{2,0},{32,2},{34,32},{1,35},{3,1},{33,3},{35,33},{4,38},{6,... | collective-permute-start | bytes 393224 | tf_op jit(solution)/shard_map/ppermute | solution.py:24
  38.0 6.6 %collective-permute-start.4 = (bf16[8,8192]{1,0:T(8,128)(2,1)S(1)}, bf16[8,8192]{1,0:T(8,128)(2,1)S(1)}, u32[]{:S(2)}, u32[]{:S(2)}) collective-permute-start(bf16[8,8192]{1,0:T(8,128)(2,1)S(1)} %shard_map.113), channel_id=1, source_target_pairs={{0,2},{2,32},{32,34},{34,0},{1,3},{3,33},{33,35},{35,1},{4,6},{6,3... | collective-permute-start | bytes 393224 | tf_op jit(solution)/shard_map/ppermute | solution.py:24
  38.1 7.9 %collective-permute-start.7 = (bf16[16,8192]{1,0:T(8,128)(2,1)S(1)}, bf16[16,8192]{1,0:T(8,128)(2,1)S(1)}, u32[]{:S(2)}, u32[]{:S(2)}) collective-permute-start(bf16[16,8192]{1,0:T(8,128)(2,1)S(1)} %collective-permute-done.2.block_ref.refs_1_), channel_id=1, source_target_pairs={{0,1},{1,0},{2,3},{3,2},{4,5},{5,4},{6,7},{7,6},{8,9},{9,8},{10,11... | collective-permute-start | bytes 786440 | tf_op jit(solution)/shard_map/ppermute | solution.py:24
  38.2 7.8 %collective-permute-start.8 = (bf16[16,8192]{1,0:T(8,128)(2,1)S(1)}, bf16[16,8192]{1,0:T(8,128)(2,1)S(1)}, u32[]{:S(2)}, u32[]{:S(2)}) collective-permute-start(bf16[16,8192]{1,0:T(8,128)(2,1)S(1)} %collective-permute-done.3.block_ref.refs_2_), channel_id=1, source_target_pairs={{0,1},{1,0},{2,3},{3,2},{4,5},{5,4},{6,7},{7,6},{8,9},{9,8},{10,11... | collective-permute-start | bytes 786440 | tf_op jit(solution)/shard_map/ppermute | solution.py:24
  41.1 3.5 %collective-permute-start.10 = (bf16[8,8192]{1,0:T(8,128)(2,1)S(1)}, bf16[8,8192]{1,0:T(8,128)(2,1)S(1)}, u32[]{:S(2)}, u32[]{:S(2)}) collective-permute-start(bf16[8,8192]{1,0:T(8,128)(2,1)S(1)} %collective-permute-done.5.refs_4_), channel_id=1, source_target_pairs={{0,1},{1,0},{2,3},{3,2},{4,5},{5,4},{6,7},{7,6},{8,9},{9,8},{10,11... | collective-permute-start | bytes 393224 | tf_op jit(solution)/shard_map/ppermute | solution.py:24
  44.7 1.3 %collective-permute-start.9 = (bf16[8,8192]{1,0:T(8,128)(2,1)S(1)}, bf16[8,8192]{1,0:T(8,128)(2,1)S(1)}, u32[]{:S(2)}, u32[]{:S(2)}) collective-permute-start(bf16[8,8192]{1,0:T(8,128)(2,1)S(1)} %collective-permute-done.4.refs_3_), channel_id=1, source_target_pairs={{0,1},{1,0},{2,3},{3,2},{4,5},{5,4},{6,7},{7,6},{8,9},{9,8},{10,11... | collective-permute-start | bytes 393224 | tf_op jit(solution)/shard_map/ppermute | solution.py:24
  48.7 2.7 %collective-permute-start.11 = (bf16[64,8192]{1,0:T(8,128)(2,1)S(1)}, bf16[64,8192]{1,0:T(8,128)(2,1)S(1)}, u32[]{:S(2)}, u32[]{:S(2)}) collective-permute-start(bf16[64,8192]{1,0:T(8,128)(2,1)S(1)} %get-tuple-element.20), channel_id=1, source_target_pairs={{0,1},{1,0},{2,3},{3,2},{4,5},{5,4},{6,7},{7,6},{8,9},{9,8},{10,11... | collective-permute-start | bytes 3145736 | tf_op jit(solution)/shard_map/ppermute | solution.py:24
  51.8 6.4 %collective-permute-start.13 = (bf16[8,8192]{1,0:T(8,128)(2,1)S(1)}, bf16[8,8192]{1,0:T(8,128)(2,1)S(1)}, u32[]{:S(2)}, u32[]{:S(2)}) collective-permute-start(bf16[8,8192]{1,0:T(8,128)(2,1)S(1)} %get-tuple-element.30), channel_id=1, source_target_pairs={{0,34},{2,0},{32,2},{34,32},{1,35},{3,1},{33,3},{35,33},{4,38},{6,... | collective-permute-start | bytes 393224 | tf_op jit(solution)/shard_map/ppermute | solution.py:24
  52.2 7.6 %collective-permute-start.16 = (bf16[8,8192]{1,0:T(8,128)(2,1)S(1)}, bf16[8,8192]{1,0:T(8,128)(2,1)S(1)}, u32[]{:S(2)}, u32[]{:S(2)}) collective-permute-start(bf16[8,8192]{1,0:T(8,128)(2,1)S(1)} %get-tuple-element.28), channel_id=1, source_target_pairs={{0,2},{2,32},{32,34},{34,0},{1,3},{3,33},{33,35},{35,1},{4,6},{6,3... | collective-permute-start | bytes 393224 | tf_op jit(solution)/shard_map/ppermute | solution.py:24
  53.9 8.1 %collective-permute-start.12 = (bf16[8,8192]{1,0:T(8,128)(2,1)S(1)}, bf16[8,8192]{1,0:T(8,128)(2,1)S(1)}, u32[]{:S(2)}, u32[]{:S(2)}) collective-permute-start(bf16[8,8192]{1,0:T(8,128)(2,1)S(1)} %get-tuple-element.27), channel_id=1, source_target_pairs={{0,2},{2,32},{32,34},{34,0},{1,3},{3,33},{33,35},{35,1},{4,6},{6,3... | collective-permute-start | bytes 393224 | tf_op jit(solution)/shard_map/ppermute | solution.py:24
  53.9 8.0 %collective-permute-start.15 = (bf16[8,8192]{1,0:T(8,128)(2,1)S(1)}, bf16[8,8192]{1,0:T(8,128)(2,1)S(1)}, u32[]{:S(2)}, u32[]{:S(2)}) collective-permute-start(bf16[8,8192]{1,0:T(8,128)(2,1)S(1)} %get-tuple-element.29), channel_id=1, source_target_pairs={{0,34},{2,0},{32,2},{34,32},{1,35},{3,1},{33,3},{35,33},{4,38},{6,... | collective-permute-start | bytes 393224 | tf_op jit(solution)/shard_map/ppermute | solution.py:24
  59.8 5.0 %collective-permute-start.14 = (bf16[8,8192]{1,0:T(8,128)(2,1)S(1)}, bf16[8,8192]{1,0:T(8,128)(2,1)S(1)}, u32[]{:S(2)}, u32[]{:S(2)}) collective-permute-start(bf16[8,8192]{1,0:T(8,128)(2,1)S(1)} %get-tuple-element.25), channel_id=1, source_target_pairs={{0,34},{2,0},{32,2},{34,32},{1,35},{3,1},{33,3},{35,33},{4,38},{6,... | collective-permute-start | bytes 393224 | tf_op jit(solution)/shard_map/ppermute | solution.py:24
  59.9 6.3 %collective-permute-start.17 = (bf16[8,8192]{1,0:T(8,128)(2,1)S(1)}, bf16[8,8192]{1,0:T(8,128)(2,1)S(1)}, u32[]{:S(2)}, u32[]{:S(2)}) collective-permute-start(bf16[8,8192]{1,0:T(8,128)(2,1)S(1)} %get-tuple-element.26), channel_id=1, source_target_pairs={{0,2},{2,32},{32,34},{34,0},{1,3},{3,33},{33,35},{35,1},{4,6},{6,3... | collective-permute-start | bytes 393224 | tf_op jit(solution)/shard_map/ppermute | solution.py:24
  79.7 5.2 %collective-permute-start.18 = (f32[1,8192]{1,0:T(1,128)S(1)}, f32[1,8192]{1,0:T(1,128)S(1)}, u32[]{:S(2)}, u32[]{:S(2)}) collective-permute-start(f32[1,8192]{1,0:T(1,128)S(1)} %get-tuple-element.32), channel_id=1, source_target_pairs={{0,192},{64,128},{128,64},{192,0},{1,193},{65,129},{129,65},{193,1... | collective-permute-start | bytes 98312 | tf_op jit(solution)/shard_map/ppermute | solution.py:32
  82.7 5.4 %collective-permute-start.19 = (f32[1,8192]{1,0:T(1,128)S(1)}, f32[1,8192]{1,0:T(1,128)S(1)}, u32[]{:S(2)}, u32[]{:S(2)}) collective-permute-start(f32[1,8192]{1,0:T(1,128)S(1)} %get-tuple-element.31), channel_id=1, source_target_pairs={{0,128},{64,192},{128,0},{192,64},{1,129},{65,193},{129,1},{193,65... | collective-permute-start | bytes 98312 | tf_op jit(solution)/shard_map/ppermute | solution.py:36

commit v4 on v3

--- a/solution.py
+++ b/solution.py
@@ -99,32 +99,32 @@
     )(block, token)
 
 
+def along_x(value, hops):
+    pairs = [(x * 2 + c, (x + (1 - 2 * c) * hops) % 4 * 2 + c) for x in range(4) for c in range(2)]
+    return lax.ppermute(value, X + ("c",), pairs)
+
+
 def gathered_blocks(row, weights):
     copies = spread(mirrored(row), opposite(row))
     pairs = lax.all_to_all(copies, "z", 0, 0, tiled=True)
     block = rows_of_pairs(pairs)
     *weights, token = loaded(weights, block)
-    low = shifted(block, X, 1)
-    high = shifted(block, X, -1)
-    low_far = shifted(half_of(low, 0, token), X, 1)
-    high_far = shifted(half_of(high, 8, token), X, -1)
-    blocks = [block, low, high, low_far, high_far]
-    return blocks + [swapped(b) for b in blocks], weights
-
-
-def returned_rows(keep, send):
-    total = keep + wide(swapped(send))
-    own = total[:16]
-    near_low, near_high, far = total[16:32], total[32:48], total[48:]
-    far_low = shifted(narrow(far[:8]), X, -1)
-    far_high = shifted(narrow(far[8:]), X, 1)
-    low_rest = shifted(narrow(near_low[8:]), X, -1)
-    high_rest = shifted(narrow(near_high[:8]), X, 1)
-    low = shifted(narrow(near_low[:8] + wide(far_low)), X, -1)
-    high = shifted(narrow(near_high[8:] + wide(far_high)), X, 1)
-    first = own[:8] + wide(high_rest) + wide(low)
-    second = own[8:] + wide(low_rest) + wide(high)
-    own = jnp.concatenate([narrow(first), narrow(second)], 0)
+    near = along_x(block, 1)
+    back = along_x(block, -1)
+    far_low = along_x(half_of(near, 0, token), 1)
+    far_high = along_x(half_of(back, 8, token), -1)
+    kept = [block, near, swapped(back), far_low, far_high]
+    return kept + [swapped(block), swapped(near), back, swapped(far_low), swapped(far_high)], weights
+
+
+def returned_rows(keep, send, send_far):
+    far = keep[48:] + wide(swapped(send_far))
+    rest = keep[:48] + wide(swapped(send))
+    own, near, near_other = rest[:16], rest[16:32], rest[32:]
+    far_in = along_x(narrow(far), -1)
+    other_in = along_x(narrow(near_other), -1)
+    near_in = along_x(narrow(near + wide(far_in)), -1)
+    own = narrow(own + wide(swapped(other_in)) + wide(near_in))
     depth = lax.axis_size("z")
     pieces = own.reshape(depth, 2, own.shape[-1])
     arrived = lax.all_to_all(pieces, "z", 0, 0, tiled=True)
@@ -161,7 +161,7 @@
 
 
 def feed_kernel(*refs):
-    blocks, (gate_ref, up_ref, down_ref, keep_ref, send_ref, rows_ref) = refs[:-6], refs[-6:]
+    blocks, (gate_ref, up_ref, down_ref, keep_ref, send_ref, far_ref, rows_ref) = refs[:-7], refs[-7:]
     at = 0
     for block in blocks:
         size = block.shape[0]
@@ -178,7 +178,8 @@
         columns = pl.ds(k * part, part)
         feed = jnp.dot(act, down_ref[:, columns], preferred_element_type=jnp.float32)
         keep_ref[:, columns] = feed[:half]
-        send_ref[:, columns] = feed[half:].astype(jnp.bfloat16)
+        send_ref[:, columns] = feed[half : half + 48].astype(jnp.bfloat16)
+        far_ref[:, columns] = feed[half + 48 :].astype(jnp.bfloat16)
 
 
 def feed_rows(blocks, weights):
@@ -189,10 +190,11 @@
         feed_kernel,
         out_shape=(
             pltpu.VMEM((64, width), jnp.float32),
-            pltpu.VMEM((64, width), jnp.bfloat16),
+            pltpu.VMEM((48, width), jnp.bfloat16),
+            pltpu.VMEM((16, width), jnp.bfloat16),
         ),
         in_specs=[in_vmem] * (len(blocks) + 3),
-        out_specs=(in_vmem, in_vmem),
+        out_specs=(in_vmem,) * 3,
         scratch_shapes=[pltpu.VMEM((128, width), jnp.bfloat16)],
         compiler_params=pltpu.CompilerParams(vmem_limit_bytes=12 << 20),
     )(*blocks, *held)
@@ -331,8 +333,7 @@
         lengths, key_cache, value_cache, queries, new_keys, new_values, residual, norm_gain
     )
     weights = gate_weight[0], up_weight[0], down_weight[0]
-    keep, send = feed_rows(*gathered_blocks(flat_rows, weights))
-    summed = returned_rows(keep, send)
+    summed = returned_rows(*feed_rows(*gathered_blocks(flat_rows, weights)))
     mixed = (hidden + summed).astype(jnp.bfloat16)
     mixed = jnp.where(serving, mixed, jnp.zeros_like(mixed))
     return mixed.reshape(residual.shape)

time: 88.9 us -> 87.8 us (0.988)
  starting transfers between devices: 20.7 us -> 18 us
  blocking collectives: 30 us -> 32.1 us
    ppermute x16 -> x8, waiting for transfers between devices: 16.7 us -> 2.51 us  [shifted(): lax.ppermute(value, axes, [(i, (i + hops) % size) for i in range(size)])]
    ppermute x0 -> x7, waiting for transfers between devices: none -> 13.7 us  [along_x(): return lax.ppermute(value, X + ('c',), pairs)]
    ppermute x16 -> x8, starting transfers between devices: 14.8 us -> 1.4 us  [shifted(): lax.ppermute(value, axes, [(i, (i + hops) % size) for i in range(size)])]
    ppermute x0 -> x7, starting transfers between devices: none -> 10.7 us  [along_x(): return lax.ppermute(value, X + ('c',), pairs)]
    all_to_all x1, blocking collectives: 12.9 us -> 15 us  [returned_rows(): arrived = lax.all_to_all(pieces, 'z', 0, 0, tiled=True)]
  transfers between devices with their start and end apart: 20 -> 19, of which waited for: 12 -> 12; matrix products, arithmetic and copies ran while one was open for 0% -> 0% of each run, Pallas kernels for 5% -> 5%
where the time goes in v4:
time: 87.8 us; the launch traced here: 87.6 us
  blocking collectives  32.1 us (37%)
  waiting for transfers between devices  26.2 us (30%)
  starting transfers between devices  18 us (21%)
  Pallas kernels  8.96 us (10%)
  other arithmetic  1.28 us (1%)
    all_to_all x1, blocking collectives, gathered_blocks(): pairs = lax.all_to_all(copies, 'z', 0, 0, tiled=True)  17.1 us
    all_to_all x1, blocking collectives, returned_rows(): arrived = lax.all_to_all(pieces, 'z', 0, 0, tiled=True)  15 us
    ppermute x7, waiting for transfers between devices, along_x(): return lax.ppermute(value, X + ('c',), pairs)  13.7 us
    ppermute x7, starting transfers between devices, along_x(): return lax.ppermute(value, X + ('c',), pairs)  10.7 us
    ppermute x2, waiting for transfers between devices, opposite(): return lax.ppermute(value, 'y', [(i, (i + 2) % 4) for i in range(4)])  5.43 us
    ppermute x2, starting transfers between devices, mirrored(): return lax.ppermute(value, 'y', [(i, 3 - i) for i in range(4)])  5.02 us
    ppermute x2, waiting for transfers between devices, mirrored(): return lax.ppermute(value, 'y', [(i, 3 - i) for i in range(4)])  4.52 us
    pallas_call x1, Pallas kernels, loaded(): pl.pallas_call(load_kernel, out_shape=tuple((pltpu.VMEM(w.shape, w.dtype)...  4.02 us
  transfers between devices with their start and end apart: 19, of which 12 were waited for; matrix products, arithmetic and copies ran while one was open for 0% of the time, Pallas kernels for 5%

profile of v4, /device:TPU:24, one launch (start us, length us, event | category | flops | bytes accessed | tf_op | source)
XLA Modules:
  0.0 87.6 jit_solution(13840894602689041675)
XLA Ops:
  0.7 2.1 %shard_map.109 = (f32[1,8192]{1,0:T(1,128)S(1)}, bf16[1,8192]{1,0:T(2,128)(2,1)S(1)}) custom-call(s32[1,1]{1,0:T(1,128)S(6)} %copy.12.length_ref, bf16[768,512]{1,0:T(8,128)(2,1)} %bitcast.15, bf16[768,512]{1,0:T(8,128)(2,1)} %bitcast.16, bf16[1,8192]{1,0:T(2,128)(2,1)} %bitcast.17, bf16[1,512]{1,0:T(2,128)(2,1)} %bitcast.20, bf16[1,512]{1,0:T(2,128)(2,1)} %bitcast.21, ...), custom_call_target="tpu_custom_call" | custom-call | tf_op jit(solution)/shard_map/pallas_call | solution.py:294
  2.7 2.0 %collective-permute-start = (bf16[1,8192]{1,0:T(2,128)(2,1)S(1)}, bf16[1,8192]{1,0:T(2,128)(2,1)S(1)}, u32[]{:S(2)}, u32[]{:S(2)}) collective-permute-start(bf16[1,8192]{1,0:T(2,128)(2,1)S(1)} %get-tuple-element.15), channel_id=1, source_target_pairs={{0,192},{64,128},{128,64},{192,0},{1,193},{65,129},{129,65},{193,1... | collective-permute-start | bytes 49160 | tf_op jit(solution)/shard_map/ppermute | solution.py:32
  4.8 0.9 collective-permute-start.1
  5.6 2.3 %collective-permute-done.near_ref = bf16[1,8192]{1,0:T(2,128)(2,1)S(1)} collective-permute-done((bf16[1,8192]{1,0:T(2,128)(2,1)S(1)}, bf16[1,8192]{1,0:T(2,128)(2,1)S(1)}, u32[]{:S(2)}, u32[]{:S(2)}) %collective-permute-start) | collective-permute-done | bytes 16416 | tf_op jit(solution)/shard_map/ppermute | solution.py:32
  7.9 2.3 %collective-permute-done.1.far_ref = bf16[1,8192]{1,0:T(2,128)(2,1)S(1)} collective-permute-done((bf16[1,8192]{1,0:T(2,128)(2,1)S(1)}, bf16[1,8192]{1,0:T(2,128)(2,1)S(1)}, u32[]{:S(2)}, u32[]{:S(2)}) %collective-permute-start.1) | collective-permute-done | bytes 16416 | tf_op jit(solution)/shard_map/ppermute | solution.py:36
  10.2 17.1 %all_to_all.10.pairs_ref = bf16[8,2,8192]{2,1,0:T(2,128)(2,1)S(1)} all-to-all(bf16[8,2,8192]{2,1,0:T(2,128)(2,1)S(1)} %shard_map.110), channel_id=1, replica_groups=mesh['y'=4,'xh'=2,'z'=8,'xl'=2,'c'=2] {'z'}, dimensions={0} | all-to-all | bytes 524288 | tf_op jit(solution)/shard_map/all_to_all | solution.py:109
  27.4 0.1 shard_map.111.refs_3_.refs_0_
  27.5 2.8 %collective-permute-start.3 = (bf16[16,8192]{1,0:T(8,128)(2,1)S(1)}, bf16[16,8192]{1,0:T(8,128)(2,1)S(1)}, u32[]{:S(2)}, u32[]{:S(2)}) collective-permute-start(bf16[16,8192]{1,0:T(8,128)(2,1)S(1)} %shard_map.111.refs_3_.refs_0_), channel_id=1, source_target_pairs={{0,34},{1,3},{2,0},{3,33},{32,2},{33,35},{34,32},{35,1},{4,38},{5,... | collective-permute-start | bytes 786440 | tf_op jit(solution)/shard_map/ppermute | solution.py:104
  30.3 0.0 collective-permute-start.2
  30.4 0.0 collective-permute-start.7
  30.4 4.0 %shard_map.112 = (bf16[208,8192]{1,0:T(8,128)(2,1)S(1)}, bf16[208,8192]{1,0:T(8,128)(2,1)S(1)}, bf16[208,8192]{1,0:T(8,128)(2,1)S(1)}, f32[8,128]{1,0:T(8,128)S(1)}) custom-call(bf16[208,8192]{1,0:T(8,128)(2,1)} %bitcast.12, bf16[208,8192]{1,0:T(8,128)(2,1)} %bitcast.13, bf16[208,8192]{1,0:T(8,128)(2,1)} %bitcast.14, ...), custom_call_target="tpu_custom_call" | custom-call | tf_op jit(solution)/shard_map/pallas_call | solution.py:153
  34.4 0.0 collective-permute-done.3.block_ref.refs_7_
  34.4 3.6 %collective-permute-start.6 = (bf16[8,8192]{1,0:T(8,128)(2,1)S(1)}, bf16[8,8192]{1,0:T(8,128)(2,1)S(1)}, u32[]{:S(2)}, u32[]{:S(2)}) collective-permute-start(bf16[8,8192]{1,0:T(8,128)(2,1)S(1)} %shard_map.114), channel_id=1, source_target_pairs={{0,34},{1,3},{2,0},{3,33},{32,2},{33,35},{34,32},{35,1},{4,38},{5,... | collective-permute-start | bytes 393224 | tf_op jit(solution)/shard_map/ppermute | solution.py:104
  38.0 0.0 collective-permute-done.2.block_ref.refs_1_
  38.0 0.1 collective-permute-start.5
  38.1 0.1 collective-permute-start.4
  38.2 0.5 collective-permute-start.8
  38.7 2.5 %collective-permute-done.6.refs_4_ = bf16[8,8192]{1,0:T(8,128)(2,1)S(1)} collective-permute-done((bf16[8,8192]{1,0:T(8,128)(2,1)S(1)}, bf16[8,8192]{1,0:T(8,128)(2,1)S(1)}, u32[]{:S(2)}, u32[]{:S(2)}) %collective-permute-start.6) | collective-permute-done | bytes 131104 | tf_op jit(solution)/shard_map/ppermute | solution.py:104
  41.3 0.0 collective-permute-start.10
  41.3 3.0 %collective-permute-done.5.refs_3_ = bf16[8,8192]{1,0:T(8,128)(2,1)S(1)} collective-permute-done((bf16[8,8192]{1,0:T(8,128)(2,1)S(1)}, bf16[8,8192]{1,0:T(8,128)(2,1)S(1)}, u32[]{:S(2)}, u32[]{:S(2)}) %collective-permute-start.5) | collective-permute-done | bytes 131104 | tf_op jit(solution)/shard_map/ppermute | solution.py:104
  44.3 0.0 collective-permute-done.10.refs_9_
  44.3 1.3 %collective-permute-done.9.refs_8_ = bf16[8,8192]{1,0:T(8,128)(2,1)S(1)} collective-permute-done((bf16[8,8192]{1,0:T(8,128)(2,1)S(1)}, bf16[8,8192]{1,0:T(8,128)(2,1)S(1)}, u32[]{:S(2)}, u32[]{:S(2)}) %collective-permute-start.9) | collective-permute-done | bytes 131104 | tf_op jit(solution)/shard_map/ppermute | solution.py:24
  45.6 0.0 collective-permute-done.4.refs_2_
  45.7 2.7 %shard_map.115 = (f32[64,8192]{1,0:T(8,128)S(1)}, bf16[48,8192]{1,0:T(8,128)(2,1)S(1)}, bf16[16,8192]{1,0:T(8,128)(2,1)S(1)}) custom-call(bf16[16,8192]{1,0:T(8,128)(2,1)S(1)} %shard_map.111.refs_3_.refs_0_, bf16[16,8192]{1,0:T(8,128)(2,1)S(1)} %collective-permute-done.2.block_ref.refs_1_, bf16[16,8192]{1,0:T(8,128)(2,1)S(1)} %collective-permute-done.4.refs_2_, ...), custom_call_target="tpu_custom_call" | custom-call | tf_op jit(solution)/shard_map/pallas_call | solution.py:189
  48.3 0.2 collective-permute-start.14
  48.6 0.4 collective-permute-start.11
  48.9 1.0 %collective-permute-done.14 = bf16[16,8192]{1,0:T(8,128)(2,1)S(1)} collective-permute-done((bf16[16,8192]{1,0:T(8,128)(2,1)S(1)}, bf16[16,8192]{1,0:T(8,128)(2,1)S(1)}, u32[]{:S(2)}, u32[]{:S(2)}) %collective-permute-start.14) | collective-permute-done | bytes 262176 | tf_op jit(solution)/shard_map/ppermute | solution.py:24
  50.0 0.1 add_convert_fusion
  50.0 0.9 %collective-permute-start.15 = (bf16[16,8192]{1,0:T(8,128)(2,1)S(1)}, bf16[16,8192]{1,0:T(8,128)(2,1)S(1)}, u32[]{:S(2)}, u32[]{:S(2)}) collective-permute-start(bf16[16,8192]{1,0:T(8,128)(2,1)S(1)} %add_convert_fusion), channel_id=1, source_target_pairs={{0,34},{1,3},{2,0},{3,33},{32,2},{33,35},{34,32},{35,1},{4,38},{5,... | collective-permute-start | bytes 786440 | tf_op jit(solution)/shard_map/ppermute | solution.py:104
  50.9 0.1 collective-permute-done.11
  51.1 0.2 convert_add_fusion
  51.3 1.1 %collective-permute-start.12 = (bf16[16,8192]{1,0:T(8,128)(2,1)S(1)}, bf16[16,8192]{1,0:T(8,128)(2,1)S(1)}, u32[]{:S(2)}, u32[]{:S(2)}) collective-permute-start(bf16[16,8192]{1,0:T(8,128)(2,1)S(1)} %slice.45), channel_id=1, source_target_pairs={{0,34},{1,3},{2,0},{3,33},{32,2},{33,35},{34,32},{35,1},{4,38},{5,... | collective-permute-start | bytes 786440 | tf_op jit(solution)/shard_map/ppermute | solution.py:104
  52.4 4.1 %collective-permute-done.15 = bf16[16,8192]{1,0:T(8,128)(2,1)S(1)} collective-permute-done((bf16[16,8192]{1,0:T(8,128)(2,1)S(1)}, bf16[16,8192]{1,0:T(8,128)(2,1)S(1)}, u32[]{:S(2)}, u32[]{:S(2)}) %collective-permute-start.15) | collective-permute-done | bytes 262176 | tf_op jit(solution)/shard_map/ppermute | solution.py:104
  56.5 2.1 %collective-permute-start.16 = (bf16[16,8192]{1,0:T(8,128)(2,1)S(1)}, bf16[16,8192]{1,0:T(8,128)(2,1)S(1)}, u32[]{:S(2)}, u32[]{:S(2)}) collective-permute-start(bf16[16,8192]{1,0:T(8,128)(2,1)S(1)} %fusion), channel_id=1, source_target_pairs={{0,34},{1,3},{2,0},{3,33},{32,2},{33,35},{34,32},{35,1},{4,38},{5,... | collective-permute-start | bytes 786440 | tf_op jit(solution)/shard_map/ppermute | solution.py:104
  58.6 0.6 collective-permute-done.12
  59.3 0.2 collective-permute-start.13
  59.5 3.5 %collective-permute-done.16 = bf16[16,8192]{1,0:T(8,128)(2,1)S(1)} collective-permute-done((bf16[16,8192]{1,0:T(8,128)(2,1)S(1)}, bf16[16,8192]{1,0:T(8,128)(2,1)S(1)}, u32[]{:S(2)}, u32[]{:S(2)}) %collective-permute-start.16) | collective-permute-done | bytes 262176 | tf_op jit(solution)/shard_map/ppermute | solution.py:104
  63.0 0.0 collective-permute-done.13
  63.0 0.1 fusion.2
  63.1 0.2 reshape.34
  63.3 15.0 %all_to_all.11 = bf16[8,2,8192]{2,1,0:T(2,128)(2,1)S(1)} all-to-all(bf16[8,2,8192]{2,1,0:T(2,128)(2,1)S(1)} %reshape.34), channel_id=1, replica_groups=mesh['y'=4,'xh'=2,'z'=8,'xl'=2,'c'=2] {'z'}, dimensions={0} | all-to-all | bytes 524288 | tf_op jit(solution)/shard_map/all_to_all | solution.py:130
  78.3 0.2 convert_reduce_fusion
  78.5 0.1 fusion.4
  78.6 3.0 %collective-permute-start.17 = (f32[1,8192]{1,0:T(1,128)S(1)}, f32[1,8192]{1,0:T(1,128)S(1)}, u32[]{:S(2)}, u32[]{:S(2)}) collective-permute-start(f32[1,8192]{1,0:T(1,128)S(1)} %get-tuple-element.24), channel_id=1, source_target_pairs={{0,192},{64,128},{128,64},{192,0},{1,193},{65,129},{129,65},{193,1... | collective-permute-start | bytes 98312 | tf_op jit(solution)/shard_map/ppermute | solution.py:32
  81.5 0.0 collective-permute-start.18
  81.6 2.2 %collective-permute-done.17 = f32[1,8192]{1,0:T(1,128)S(1)} collective-permute-done((f32[1,8192]{1,0:T(1,128)S(1)}, f32[1,8192]{1,0:T(1,128)S(1)}, u32[]{:S(2)}, u32[]{:S(2)}) %collective-permute-start.17) | collective-permute-done | bytes 32800 | tf_op jit(solution)/shard_map/ppermute | solution.py:32
  83.8 3.2 %collective-permute-done.18 = f32[1,8192]{1,0:T(1,128)S(1)} collective-permute-done((f32[1,8192]{1,0:T(1,128)S(1)}, f32[1,8192]{1,0:T(1,128)S(1)}, u32[]{:S(2)}, u32[]{:S(2)}) %collective-permute-start.18) | collective-permute-done | bytes 32800 | tf_op jit(solution)/shard_map/ppermute | solution.py:36
  86.9 0.7 fusion.3
  (8 shorter events, 0.1 us)
Async XLA Ops:
  2.7 5.2 %collective-permute-start = (bf16[1,8192]{1,0:T(2,128)(2,1)S(1)}, bf16[1,8192]{1,0:T(2,128)(2,1)S(1)}, u32[]{:S(2)}, u32[]{:S(2)}) collective-permute-start(bf16[1,8192]{1,0:T(2,128)(2,1)S(1)} %get-tuple-element.15), channel_id=1, source_target_pairs={{0,192},{64,128},{128,64},{192,0},{1,193},{65,129},{129,65},{193,1... | collective-permute-start | bytes 49160 | tf_op jit(solution)/shard_map/ppermute | solution.py:32
  4.8 5.4 %collective-permute-start.1 = (bf16[1,8192]{1,0:T(2,128)(2,1)S(1)}, bf16[1,8192]{1,0:T(2,128)(2,1)S(1)}, u32[]{:S(2)}, u32[]{:S(2)}) collective-permute-start(bf16[1,8192]{1,0:T(2,128)(2,1)S(1)} %get-tuple-element.15), channel_id=1, source_target_pairs={{0,128},{64,192},{128,0},{192,64},{1,129},{65,193},{129,1},{193,65... | collective-permute-start | bytes 49160 | tf_op jit(solution)/shard_map/ppermute | solution.py:36
  27.5 6.9 %collective-permute-start.3 = (bf16[16,8192]{1,0:T(8,128)(2,1)S(1)}, bf16[16,8192]{1,0:T(8,128)(2,1)S(1)}, u32[]{:S(2)}, u32[]{:S(2)}) collective-permute-start(bf16[16,8192]{1,0:T(8,128)(2,1)S(1)} %shard_map.111.refs_3_.refs_0_), channel_id=1, source_target_pairs={{0,34},{1,3},{2,0},{3,33},{32,2},{33,35},{34,32},{35,1},{4,38},{5,... | collective-permute-start | bytes 786440 | tf_op jit(solution)/shard_map/ppermute | solution.py:104
  30.3 7.7 %collective-permute-start.2 = (bf16[16,8192]{1,0:T(8,128)(2,1)S(1)}, bf16[16,8192]{1,0:T(8,128)(2,1)S(1)}, u32[]{:S(2)}, u32[]{:S(2)}) collective-permute-start(bf16[16,8192]{1,0:T(8,128)(2,1)S(1)} %shard_map.111.refs_3_.refs_0_), channel_id=1, source_target_pairs={{0,2},{1,35},{2,32},{3,1},{32,34},{33,3},{34,0},{35,33},{4,6},{5,3... | collective-permute-start | bytes 786440 | tf_op jit(solution)/shard_map/ppermute | solution.py:104
  30.4 13.9 %collective-permute-start.7 = (bf16[16,8192]{1,0:T(8,128)(2,1)S(1)}, bf16[16,8192]{1,0:T(8,128)(2,1)S(1)}, u32[]{:S(2)}, u32[]{:S(2)}) collective-permute-start(bf16[16,8192]{1,0:T(8,128)(2,1)S(1)} %shard_map.111.refs_3_.refs_0_), channel_id=1, source_target_pairs={{0,1},{1,0},{2,3},{3,2},{4,5},{5,4},{6,7},{7,6},{8,9},{9,8},{10,11... | collective-permute-start | bytes 786440 | tf_op jit(solution)/shard_map/ppermute | solution.py:24
  34.4 6.9 %collective-permute-start.6 = (bf16[8,8192]{1,0:T(8,128)(2,1)S(1)}, bf16[8,8192]{1,0:T(8,128)(2,1)S(1)}, u32[]{:S(2)}, u32[]{:S(2)}) collective-permute-start(bf16[8,8192]{1,0:T(8,128)(2,1)S(1)} %shard_map.114), channel_id=1, source_target_pairs={{0,34},{1,3},{2,0},{3,33},{32,2},{33,35},{34,32},{35,1},{4,38},{5,... | collective-permute-start | bytes 393224 | tf_op jit(solution)/shard_map/ppermute | solution.py:104
  38.0 6.3 %collective-permute-start.5 = (bf16[8,8192]{1,0:T(8,128)(2,1)S(1)}, bf16[8,8192]{1,0:T(8,128)(2,1)S(1)}, u32[]{:S(2)}, u32[]{:S(2)}) collective-permute-start(bf16[8,8192]{1,0:T(8,128)(2,1)S(1)} %shard_map.113), channel_id=1, source_target_pairs={{0,2},{1,35},{2,32},{3,1},{32,34},{33,3},{34,0},{35,33},{4,6},{5,3... | collective-permute-start | bytes 393224 | tf_op jit(solution)/shard_map/ppermute | solution.py:104
  38.1 7.5 %collective-permute-start.4 = (bf16[16,8192]{1,0:T(8,128)(2,1)S(1)}, bf16[16,8192]{1,0:T(8,128)(2,1)S(1)}, u32[]{:S(2)}, u32[]{:S(2)}) collective-permute-start(bf16[16,8192]{1,0:T(8,128)(2,1)S(1)} %collective-permute-done.3.block_ref.refs_7_), channel_id=1, source_target_pairs={{0,1},{1,0},{2,3},{3,2},{4,5},{5,4},{6,7},{7,6},{8,9},{9,8},{10,11... | collective-permute-start | bytes 786440 | tf_op jit(solution)/shard_map/ppermute | solution.py:24
  38.2 7.4 %collective-permute-start.8 = (bf16[16,8192]{1,0:T(8,128)(2,1)S(1)}, bf16[16,8192]{1,0:T(8,128)(2,1)S(1)}, u32[]{:S(2)}, u32[]{:S(2)}) collective-permute-start(bf16[16,8192]{1,0:T(8,128)(2,1)S(1)} %collective-permute-done.2.block_ref.refs_1_), channel_id=1, source_target_pairs={{0,1},{1,0},{2,3},{3,2},{4,5},{5,4},{6,7},{7,6},{8,9},{9,8},{10,11... | collective-permute-start | bytes 786440 | tf_op jit(solution)/shard_map/ppermute | solution.py:24
  41.3 3.0 %collective-permute-start.10 = (bf16[8,8192]{1,0:T(8,128)(2,1)S(1)}, bf16[8,8192]{1,0:T(8,128)(2,1)S(1)}, u32[]{:S(2)}, u32[]{:S(2)}) collective-permute-start(bf16[8,8192]{1,0:T(8,128)(2,1)S(1)} %collective-permute-done.6.refs_4_), channel_id=1, source_target_pairs={{0,1},{1,0},{2,3},{3,2},{4,5},{5,4},{6,7},{7,6},{8,9},{9,8},{10,11... | collective-permute-start | bytes 393224 | tf_op jit(solution)/shard_map/ppermute | solution.py:24
  44.3 1.3 %collective-permute-start.9 = (bf16[8,8192]{1,0:T(8,128)(2,1)S(1)}, bf16[8,8192]{1,0:T(8,128)(2,1)S(1)}, u32[]{:S(2)}, u32[]{:S(2)}) collective-permute-start(bf16[8,8192]{1,0:T(8,128)(2,1)S(1)} %collective-permute-done.5.refs_3_), channel_id=1, source_target_pairs={{0,1},{1,0},{2,3},{3,2},{4,5},{5,4},{6,7},{7,6},{8,9},{9,8},{10,11... | collective-permute-start | bytes 393224 | tf_op jit(solution)/shard_map/ppermute | solution.py:24
  48.3 1.6 %collective-permute-start.14 = (bf16[16,8192]{1,0:T(8,128)(2,1)S(1)}, bf16[16,8192]{1,0:T(8,128)(2,1)S(1)}, u32[]{:S(2)}, u32[]{:S(2)}) collective-permute-start(bf16[16,8192]{1,0:T(8,128)(2,1)S(1)} %get-tuple-element.22), channel_id=1, source_target_pairs={{0,1},{1,0},{2,3},{3,2},{4,5},{5,4},{6,7},{7,6},{8,9},{9,8},{10,11... | collective-permute-start | bytes 786440 | tf_op jit(solution)/shard_map/ppermute | solution.py:24
  48.6 2.5 %collective-permute-start.11 = (bf16[48,8192]{1,0:T(8,128)(2,1)S(1)}, bf16[48,8192]{1,0:T(8,128)(2,1)S(1)}, u32[]{:S(2)}, u32[]{:S(2)}) collective-permute-start(bf16[48,8192]{1,0:T(8,128)(2,1)S(1)} %get-tuple-element.21), channel_id=1, source_target_pairs={{0,1},{1,0},{2,3},{3,2},{4,5},{5,4},{6,7},{7,6},{8,9},{9,8},{10,11... | collective-permute-start | bytes 2359304 | tf_op jit(solution)/shard_map/ppermute | solution.py:24
  50.0 6.4 %collective-permute-start.15 = (bf16[16,8192]{1,0:T(8,128)(2,1)S(1)}, bf16[16,8192]{1,0:T(8,128)(2,1)S(1)}, u32[]{:S(2)}, u32[]{:S(2)}) collective-permute-start(bf16[16,8192]{1,0:T(8,128)(2,1)S(1)} %add_convert_fusion), channel_id=1, source_target_pairs={{0,34},{1,3},{2,0},{3,33},{32,2},{33,35},{34,32},{35,1},{4,38},{5,... | collective-permute-start | bytes 786440 | tf_op jit(solution)/shard_map/ppermute | solution.py:104
  51.3 8.0 %collective-permute-start.12 = (bf16[16,8192]{1,0:T(8,128)(2,1)S(1)}, bf16[16,8192]{1,0:T(8,128)(2,1)S(1)}, u32[]{:S(2)}, u32[]{:S(2)}) collective-permute-start(bf16[16,8192]{1,0:T(8,128)(2,1)S(1)} %slice.45), channel_id=1, source_target_pairs={{0,34},{1,3},{2,0},{3,33},{32,2},{33,35},{34,32},{35,1},{4,38},{5,... | collective-permute-start | bytes 786440 | tf_op jit(solution)/shard_map/ppermute | solution.py:104
  56.5 6.4 %collective-permute-start.16 = (bf16[16,8192]{1,0:T(8,128)(2,1)S(1)}, bf16[16,8192]{1,0:T(8,128)(2,1)S(1)}, u32[]{:S(2)}, u32[]{:S(2)}) collective-permute-start(bf16[16,8192]{1,0:T(8,128)(2,1)S(1)} %fusion), channel_id=1, source_target_pairs={{0,34},{1,3},{2,0},{3,33},{32,2},{33,35},{34,32},{35,1},{4,38},{5,... | collective-permute-start | bytes 786440 | tf_op jit(solution)/shard_map/ppermute | solution.py:104
  59.3 3.7 %collective-permute-start.13 = (bf16[16,8192]{1,0:T(8,128)(2,1)S(1)}, bf16[16,8192]{1,0:T(8,128)(2,1)S(1)}, u32[]{:S(2)}, u32[]{:S(2)}) collective-permute-start(bf16[16,8192]{1,0:T(8,128)(2,1)S(1)} %collective-permute-done.12), channel_id=1, source_target_pairs={{0,1},{1,0},{2,3},{3,2},{4,5},{5,4},{6,7},{7,6},{8,9},{9,8},{10,11... | collective-permute-start | bytes 786440 | tf_op jit(solution)/shard_map/ppermute | solution.py:24
  78.6 5.2 %collective-permute-start.17 = (f32[1,8192]{1,0:T(1,128)S(1)}, f32[1,8192]{1,0:T(1,128)S(1)}, u32[]{:S(2)}, u32[]{:S(2)}) collective-permute-start(f32[1,8192]{1,0:T(1,128)S(1)} %get-tuple-element.24), channel_id=1, source_target_pairs={{0,192},{64,128},{128,64},{192,0},{1,193},{65,129},{129,65},{193,1... | collective-permute-start | bytes 98312 | tf_op jit(solution)/shard_map/ppermute | solution.py:32
  81.5 5.4 %collective-permute-start.18 = (f32[1,8192]{1,0:T(1,128)S(1)}, f32[1,8192]{1,0:T(1,128)S(1)}, u32[]{:S(2)}, u32[]{:S(2)}) collective-permute-start(f32[1,8192]{1,0:T(1,128)S(1)} %get-tuple-element.23), channel_id=1, source_target_pairs={{0,128},{64,192},{128,0},{192,64},{1,129},{65,193},{129,1},{193,65... | collective-permute-start | bytes 98312 | tf_op jit(solution)/shard_map/ppermute | solution.py:36

commit v5 on v4

--- a/solution.py
+++ b/solution.py
@@ -1,5 +1,3 @@
-import functools
-
 import jax
 import jax.numpy as jnp
 from jax import lax
@@ -83,20 +81,19 @@
     )(pairs)
 
 
-def half_kernel(block_ref, token_ref, half_ref, *, start):
-    half_ref[...] = block_ref[pl.ds(start, half_ref.shape[0]), :]
-
-
-def half_of(block, start, token):
-    rows, width = block.shape
-    in_vmem = pl.BlockSpec(memory_space=pltpu.VMEM)
-    return pl.pallas_call(
-        functools.partial(half_kernel, start=start),
-        out_shape=pltpu.VMEM((rows // 2, width), block.dtype),
+def onward_kernel(rows_ref, token_ref, copy_ref):
+    copy_ref[...] = rows_ref[...]
+
+
+def onward(rows, token):
+    in_vmem = pl.BlockSpec(memory_space=pltpu.VMEM)
+    return pl.pallas_call(
+        onward_kernel,
+        out_shape=pltpu.VMEM(rows.shape, rows.dtype),
         in_specs=[in_vmem, pl.BlockSpec(memory_space=pl.ANY)],
         out_specs=in_vmem,
         compiler_params=pltpu.CompilerParams(vmem_limit_bytes=4 << 20),
-    )(block, token)
+    )(rows, token)
 
 
 def along_x(value, hops):
@@ -110,11 +107,10 @@
     block = rows_of_pairs(pairs)
     *weights, token = loaded(weights, block)
     near = along_x(block, 1)
-    back = along_x(block, -1)
-    far_low = along_x(half_of(near, 0, token), 1)
-    far_high = along_x(half_of(back, 8, token), -1)
-    kept = [block, near, swapped(back), far_low, far_high]
-    return kept + [swapped(block), swapped(near), back, swapped(far_low), swapped(far_high)], weights
+    far = along_x(near, 1)
+    back = along_x(onward(block, token), -1)
+    kept = [block, near, swapped(back), far]
+    return kept + [swapped(block), swapped(near), back, swapped(far)], weights
 
 
 def returned_rows(keep, send, send_far):

time: 87.8 us -> 86.8 us (0.989)
  waiting for transfers between devices: 26.2 us -> 25.3 us
    ppermute x7 -> x6, waiting for transfers between devices: 13.7 us -> 12.8 us  [along_x(): return lax.ppermute(value, X + ('c',), pairs)]
    ppermute x7 -> x6, starting transfers between devices: 10.7 us -> 11.6 us  [along_x(): return lax.ppermute(value, X + ('c',), pairs)]
    ppermute x8 -> x7, waiting for transfers between devices: 2.51 us -> 2.55 us  [shifted(): lax.ppermute(value, axes, [(i, (i + hops) % size) for i in range(size)])]
  transfers between devices with their start and end apart: 19 -> 17, of which waited for: 12 -> 11; matrix products, arithmetic and copies ran while one was open for 0% -> 0% of each run, Pallas kernels for 5% -> 5%
where the time goes in v5:
time: 86.8 us; the launch traced here: 86.6 us
  blocking collectives  31.6 us (36%)
  waiting for transfers between devices  25.3 us (29%)
  starting transfers between devices  18.5 us (21%)
  Pallas kernels  8.95 us (10%)
  other arithmetic  1.28 us (1%)
    all_to_all x1, blocking collectives, gathered_blocks(): pairs = lax.all_to_all(copies, 'z', 0, 0, tiled=True)  17.1 us
    all_to_all x1, blocking collectives, returned_rows(): arrived = lax.all_to_all(pieces, 'z', 0, 0, tiled=True)  14.5 us
    ppermute x6, waiting for transfers between devices, along_x(): return lax.ppermute(value, X + ('c',), pairs)  12.8 us
    ppermute x6, starting transfers between devices, along_x(): return lax.ppermute(value, X + ('c',), pairs)  11.6 us
    ppermute x2, waiting for transfers between devices, opposite(): return lax.ppermute(value, 'y', [(i, (i + 2) % 4) for i in range(4)])  5.26 us
    ppermute x2, starting transfers between devices, mirrored(): return lax.ppermute(value, 'y', [(i, 3 - i) for i in range(4)])  4.86 us
    ppermute x2, waiting for transfers between devices, mirrored(): return lax.ppermute(value, 'y', [(i, 3 - i) for i in range(4)])  4.71 us
    pallas_call x1, Pallas kernels, loaded(): pl.pallas_call(load_kernel, out_shape=tuple((pltpu.VMEM(w.shape, w.dtype)...  4.01 us
  transfers between devices with their start and end apart: 17, of which 11 were waited for; matrix products, arithmetic and copies ran while one was open for 0% of the time, Pallas kernels for 5%

profile of v5, /device:TPU:24, one launch (start us, length us, event | category | flops | bytes accessed | tf_op | source)
XLA Modules:
  0.0 86.6 jit_solution(6969440922855654528)
XLA Ops:
  0.7 2.1 %shard_map.109 = (f32[1,8192]{1,0:T(1,128)S(1)}, bf16[1,8192]{1,0:T(2,128)(2,1)S(1)}) custom-call(s32[1,1]{1,0:T(1,128)S(6)} %copy.12.length_ref, bf16[768,512]{1,0:T(8,128)(2,1)} %bitcast.15, bf16[768,512]{1,0:T(8,128)(2,1)} %bitcast.16, bf16[1,8192]{1,0:T(2,128)(2,1)} %bitcast.17, bf16[1,512]{1,0:T(2,128)(2,1)} %bitcast.20, bf16[1,512]{1,0:T(2,128)(2,1)} %bitcast.21, ...), custom_call_target="tpu_custom_call" | custom-call | tf_op jit(solution)/shard_map/pallas_call | solution.py:290
  2.7 2.0 %collective-permute-start = (bf16[1,8192]{1,0:T(2,128)(2,1)S(1)}, bf16[1,8192]{1,0:T(2,128)(2,1)S(1)}, u32[]{:S(2)}, u32[]{:S(2)}) collective-permute-start(bf16[1,8192]{1,0:T(2,128)(2,1)S(1)} %get-tuple-element.15), channel_id=1, source_target_pairs={{0,192},{64,128},{128,64},{192,0},{1,193},{65,129},{129,65},{193,1... | collective-permute-start | bytes 49160 | tf_op jit(solution)/shard_map/ppermute | solution.py:30
  4.8 0.9 collective-permute-start.1
  5.6 2.3 %collective-permute-done.near_ref = bf16[1,8192]{1,0:T(2,128)(2,1)S(1)} collective-permute-done((bf16[1,8192]{1,0:T(2,128)(2,1)S(1)}, bf16[1,8192]{1,0:T(2,128)(2,1)S(1)}, u32[]{:S(2)}, u32[]{:S(2)}) %collective-permute-start) | collective-permute-done | bytes 16416 | tf_op jit(solution)/shard_map/ppermute | solution.py:30
  7.9 2.3 %collective-permute-done.1.far_ref = bf16[1,8192]{1,0:T(2,128)(2,1)S(1)} collective-permute-done((bf16[1,8192]{1,0:T(2,128)(2,1)S(1)}, bf16[1,8192]{1,0:T(2,128)(2,1)S(1)}, u32[]{:S(2)}, u32[]{:S(2)}) %collective-permute-start.1) | collective-permute-done | bytes 16416 | tf_op jit(solution)/shard_map/ppermute | solution.py:34
  10.2 17.1 %all_to_all.10.pairs_ref = bf16[8,2,8192]{2,1,0:T(2,128)(2,1)S(1)} all-to-all(bf16[8,2,8192]{2,1,0:T(2,128)(2,1)S(1)} %shard_map.110), channel_id=1, replica_groups=mesh['y'=4,'xh'=2,'z'=8,'xl'=2,'c'=2] {'z'}, dimensions={0} | all-to-all | bytes 524288 | tf_op jit(solution)/shard_map/all_to_all | solution.py:106
  27.4 0.1 shard_map.111.refs_3_.rows_ref.refs_0_
  27.5 1.6 %collective-permute-start.2 = (bf16[16,8192]{1,0:T(8,128)(2,1)S(1)}, bf16[16,8192]{1,0:T(8,128)(2,1)S(1)}, u32[]{:S(2)}, u32[]{:S(2)}) collective-permute-start(bf16[16,8192]{1,0:T(8,128)(2,1)S(1)} %shard_map.111.refs_3_.rows_ref.refs_0_), channel_id=1, source_target_pairs={{0,2},{1,35},{2,32},{3,1},{32,34},{33,3},{34,0},{35,33},{4,6},{5,3... | collective-permute-start | bytes 786440 | tf_op jit(solution)/shard_map/ppermute | solution.py:101
  29.1 4.0 %shard_map.112 = (bf16[208,8192]{1,0:T(8,128)(2,1)S(1)}, bf16[208,8192]{1,0:T(8,128)(2,1)S(1)}, bf16[208,8192]{1,0:T(8,128)(2,1)S(1)}, f32[8,128]{1,0:T(8,128)S(1)}) custom-call(bf16[208,8192]{1,0:T(8,128)(2,1)} %bitcast.12, bf16[208,8192]{1,0:T(8,128)(2,1)} %bitcast.13, bf16[208,8192]{1,0:T(8,128)(2,1)} %bitcast.14, ...), custom_call_target="tpu_custom_call" | custom-call | tf_op jit(solution)/shard_map/pallas_call | solution.py:149
  33.1 1.8 %collective-permute-start.3 = (bf16[16,8192]{1,0:T(8,128)(2,1)S(1)}, bf16[16,8192]{1,0:T(8,128)(2,1)S(1)}, u32[]{:S(2)}, u32[]{:S(2)}) collective-permute-start(bf16[16,8192]{1,0:T(8,128)(2,1)S(1)} %shard_map.113), channel_id=1, source_target_pairs={{0,34},{1,3},{2,0},{3,33},{32,2},{33,35},{34,32},{35,1},{4,38},{5,... | collective-permute-start | bytes 786440 | tf_op jit(solution)/shard_map/ppermute | solution.py:101
  35.0 0.2 collective-permute-done.2.refs_1_
  35.2 1.6 %collective-permute-start.5 = (bf16[16,8192]{1,0:T(8,128)(2,1)S(1)}, bf16[16,8192]{1,0:T(8,128)(2,1)S(1)}, u32[]{:S(2)}, u32[]{:S(2)}) collective-permute-start(bf16[16,8192]{1,0:T(8,128)(2,1)S(1)} %collective-permute-done.2.refs_1_), channel_id=1, source_target_pairs={{0,2},{1,35},{2,32},{3,1},{32,34},{33,3},{34,0},{35,33},{4,6},{5,3... | collective-permute-start | bytes 786440 | tf_op jit(solution)/shard_map/ppermute | solution.py:101
  36.7 0.0 collective-permute-start.6
  36.8 0.5 collective-permute-start.7
  37.3 2.8 %collective-permute-done.3.refs_6_ = bf16[16,8192]{1,0:T(8,128)(2,1)S(1)} collective-permute-done((bf16[16,8192]{1,0:T(8,128)(2,1)S(1)}, bf16[16,8192]{1,0:T(8,128)(2,1)S(1)}, u32[]{:S(2)}, u32[]{:S(2)}) %collective-permute-start.3) | collective-permute-done | bytes 262176 | tf_op jit(solution)/shard_map/ppermute | solution.py:101
  40.1 0.0 collective-permute-start.4
  40.1 3.0 %collective-permute-done.5.refs_3_ = bf16[16,8192]{1,0:T(8,128)(2,1)S(1)} collective-permute-done((bf16[16,8192]{1,0:T(8,128)(2,1)S(1)}, bf16[16,8192]{1,0:T(8,128)(2,1)S(1)}, u32[]{:S(2)}, u32[]{:S(2)}) %collective-permute-start.5) | collective-permute-done | bytes 262176 | tf_op jit(solution)/shard_map/ppermute | solution.py:101
  43.0 0.0 collective-permute-start.8
  43.0 0.0 collective-permute-done.6.refs_4_
  43.0 0.0 collective-permute-done.4.refs_2_
  43.0 0.0 collective-permute-done.7.refs_5_
  43.0 1.5 %collective-permute-done.8.refs_7_ = bf16[16,8192]{1,0:T(8,128)(2,1)S(1)} collective-permute-done((bf16[16,8192]{1,0:T(8,128)(2,1)S(1)}, bf16[16,8192]{1,0:T(8,128)(2,1)S(1)}, u32[]{:S(2)}, u32[]{:S(2)}) %collective-permute-start.8) | collective-permute-done | bytes 262176 | tf_op jit(solution)/shard_map/ppermute | solution.py:22
  44.6 2.7 %shard_map.114 = (f32[64,8192]{1,0:T(8,128)S(1)}, bf16[48,8192]{1,0:T(8,128)(2,1)S(1)}, bf16[16,8192]{1,0:T(8,128)(2,1)S(1)}) custom-call(bf16[16,8192]{1,0:T(8,128)(2,1)S(1)} %shard_map.111.refs_3_.rows_ref.refs_0_, bf16[16,8192]{1,0:T(8,128)(2,1)S(1)} %collective-permute-done.2.refs_1_, bf16[16,8192]{1,0:T(8,128)(2,1)S(1)} %collective-permute-done.4.refs_2_, ...), custom_call_target="tpu_custom_call" | custom-call | tf_op jit(solution)/shard_map/pallas_call | solution.py:185
  47.2 0.2 collective-permute-start.12
  47.5 0.4 collective-permute-start.9
  47.8 1.0 %collective-permute-done.12 = bf16[16,8192]{1,0:T(8,128)(2,1)S(1)} collective-permute-done((bf16[16,8192]{1,0:T(8,128)(2,1)S(1)}, bf16[16,8192]{1,0:T(8,128)(2,1)S(1)}, u32[]{:S(2)}, u32[]{:S(2)}) %collective-permute-start.12) | collective-permute-done | bytes 262176 | tf_op jit(solution)/shard_map/ppermute | solution.py:22
  48.9 0.1 add_convert_fusion
  48.9 2.1 %collective-permute-start.13 = (bf16[16,8192]{1,0:T(8,128)(2,1)S(1)}, bf16[16,8192]{1,0:T(8,128)(2,1)S(1)}, u32[]{:S(2)}, u32[]{:S(2)}) collective-permute-start(bf16[16,8192]{1,0:T(8,128)(2,1)S(1)} %add_convert_fusion), channel_id=1, source_target_pairs={{0,34},{1,3},{2,0},{3,33},{32,2},{33,35},{34,32},{35,1},{4,38},{5,... | collective-permute-start | bytes 786440 | tf_op jit(solution)/shard_map/ppermute | solution.py:101
  51.0 0.0 collective-permute-done.9
  51.0 0.2 convert_add_fusion
  51.2 1.2 %collective-permute-start.10 = (bf16[16,8192]{1,0:T(8,128)(2,1)S(1)}, bf16[16,8192]{1,0:T(8,128)(2,1)S(1)}, u32[]{:S(2)}, u32[]{:S(2)}) collective-permute-start(bf16[16,8192]{1,0:T(8,128)(2,1)S(1)} %slice.45), channel_id=1, source_target_pairs={{0,34},{1,3},{2,0},{3,33},{32,2},{33,35},{34,32},{35,1},{4,38},{5,... | collective-permute-start | bytes 786440 | tf_op jit(solution)/shard_map/ppermute | solution.py:101
  52.5 2.9 %collective-permute-done.13 = bf16[16,8192]{1,0:T(8,128)(2,1)S(1)} collective-permute-done((bf16[16,8192]{1,0:T(8,128)(2,1)S(1)}, bf16[16,8192]{1,0:T(8,128)(2,1)S(1)}, u32[]{:S(2)}, u32[]{:S(2)}) %collective-permute-start.13) | collective-permute-done | bytes 262176 | tf_op jit(solution)/shard_map/ppermute | solution.py:101
  55.4 3.3 %collective-permute-start.14 = (bf16[16,8192]{1,0:T(8,128)(2,1)S(1)}, bf16[16,8192]{1,0:T(8,128)(2,1)S(1)}, u32[]{:S(2)}, u32[]{:S(2)}) collective-permute-start(bf16[16,8192]{1,0:T(8,128)(2,1)S(1)} %fusion), channel_id=1, source_target_pairs={{0,34},{1,3},{2,0},{3,33},{32,2},{33,35},{34,32},{35,1},{4,38},{5,... | collective-permute-start | bytes 786440 | tf_op jit(solution)/shard_map/ppermute | solution.py:101
  58.7 0.0 collective-permute-done.10
  58.7 0.0 collective-permute-start.11
  58.7 3.9 %collective-permute-done.14 = bf16[16,8192]{1,0:T(8,128)(2,1)S(1)} collective-permute-done((bf16[16,8192]{1,0:T(8,128)(2,1)S(1)}, bf16[16,8192]{1,0:T(8,128)(2,1)S(1)}, u32[]{:S(2)}, u32[]{:S(2)}) %collective-permute-start.14) | collective-permute-done | bytes 262176 | tf_op jit(solution)/shard_map/ppermute | solution.py:101
  62.6 0.0 collective-permute-done.11
  62.6 0.1 fusion.2
  62.7 0.2 reshape.34
  62.9 14.5 %all_to_all.11 = bf16[8,2,8192]{2,1,0:T(2,128)(2,1)S(1)} all-to-all(bf16[8,2,8192]{2,1,0:T(2,128)(2,1)S(1)} %reshape.34), channel_id=1, replica_groups=mesh['y'=4,'xh'=2,'z'=8,'xl'=2,'c'=2] {'z'}, dimensions={0} | all-to-all | bytes 524288 | tf_op jit(solution)/shard_map/all_to_all | solution.py:126
  77.4 0.2 convert_reduce_fusion
  77.6 0.1 fusion.4
  77.7 2.8 %collective-permute-start.15 = (f32[1,8192]{1,0:T(1,128)S(1)}, f32[1,8192]{1,0:T(1,128)S(1)}, u32[]{:S(2)}, u32[]{:S(2)}) collective-permute-start(f32[1,8192]{1,0:T(1,128)S(1)} %get-tuple-element.24), channel_id=1, source_target_pairs={{0,192},{64,128},{128,64},{192,0},{1,193},{65,129},{129,65},{193,1... | collective-permute-start | bytes 98312 | tf_op jit(solution)/shard_map/ppermute | solution.py:30
  80.5 0.0 collective-permute-start.16
  80.5 2.4 %collective-permute-done.15 = f32[1,8192]{1,0:T(1,128)S(1)} collective-permute-done((f32[1,8192]{1,0:T(1,128)S(1)}, f32[1,8192]{1,0:T(1,128)S(1)}, u32[]{:S(2)}, u32[]{:S(2)}) %collective-permute-start.15) | collective-permute-done | bytes 32800 | tf_op jit(solution)/shard_map/ppermute | solution.py:30
  82.9 3.0 %collective-permute-done.16 = f32[1,8192]{1,0:T(1,128)S(1)} collective-permute-done((f32[1,8192]{1,0:T(1,128)S(1)}, f32[1,8192]{1,0:T(1,128)S(1)}, u32[]{:S(2)}, u32[]{:S(2)}) %collective-permute-start.16) | collective-permute-done | bytes 32800 | tf_op jit(solution)/shard_map/ppermute | solution.py:34
  85.9 0.7 fusion.3
  (4 shorter events, 0.1 us)
Async XLA Ops:
  2.7 5.2 %collective-permute-start = (bf16[1,8192]{1,0:T(2,128)(2,1)S(1)}, bf16[1,8192]{1,0:T(2,128)(2,1)S(1)}, u32[]{:S(2)}, u32[]{:S(2)}) collective-permute-start(bf16[1,8192]{1,0:T(2,128)(2,1)S(1)} %get-tuple-element.15), channel_id=1, source_target_pairs={{0,192},{64,128},{128,64},{192,0},{1,193},{65,129},{129,65},{193,1... | collective-permute-start | bytes 49160 | tf_op jit(solution)/shard_map/ppermute | solution.py:30
  4.8 5.4 %collective-permute-start.1 = (bf16[1,8192]{1,0:T(2,128)(2,1)S(1)}, bf16[1,8192]{1,0:T(2,128)(2,1)S(1)}, u32[]{:S(2)}, u32[]{:S(2)}) collective-permute-start(bf16[1,8192]{1,0:T(2,128)(2,1)S(1)} %get-tuple-element.15), channel_id=1, source_target_pairs={{0,128},{64,192},{128,0},{192,64},{1,129},{65,193},{129,1},{193,65... | collective-permute-start | bytes 49160 | tf_op jit(solution)/shard_map/ppermute | solution.py:34
  27.5 7.7 %collective-permute-start.2 = (bf16[16,8192]{1,0:T(8,128)(2,1)S(1)}, bf16[16,8192]{1,0:T(8,128)(2,1)S(1)}, u32[]{:S(2)}, u32[]{:S(2)}) collective-permute-start(bf16[16,8192]{1,0:T(8,128)(2,1)S(1)} %shard_map.111.refs_3_.rows_ref.refs_0_), channel_id=1, source_target_pairs={{0,2},{1,35},{2,32},{3,1},{32,34},{33,3},{34,0},{35,33},{4,6},{5,3... | collective-permute-start | bytes 786440 | tf_op jit(solution)/shard_map/ppermute | solution.py:101
  33.1 6.9 %collective-permute-start.3 = (bf16[16,8192]{1,0:T(8,128)(2,1)S(1)}, bf16[16,8192]{1,0:T(8,128)(2,1)S(1)}, u32[]{:S(2)}, u32[]{:S(2)}) collective-permute-start(bf16[16,8192]{1,0:T(8,128)(2,1)S(1)} %shard_map.113), channel_id=1, source_target_pairs={{0,34},{1,3},{2,0},{3,33},{32,2},{33,35},{34,32},{35,1},{4,38},{5,... | collective-permute-start | bytes 786440 | tf_op jit(solution)/shard_map/ppermute | solution.py:101
  35.2 7.8 %collective-permute-start.5 = (bf16[16,8192]{1,0:T(8,128)(2,1)S(1)}, bf16[16,8192]{1,0:T(8,128)(2,1)S(1)}, u32[]{:S(2)}, u32[]{:S(2)}) collective-permute-start(bf16[16,8192]{1,0:T(8,128)(2,1)S(1)} %collective-permute-done.2.refs_1_), channel_id=1, source_target_pairs={{0,2},{1,35},{2,32},{3,1},{32,34},{33,3},{34,0},{35,33},{4,6},{5,3... | collective-permute-start | bytes 786440 | tf_op jit(solution)/shard_map/ppermute | solution.py:101
  36.7 6.3 %collective-permute-start.6 = (bf16[16,8192]{1,0:T(8,128)(2,1)S(1)}, bf16[16,8192]{1,0:T(8,128)(2,1)S(1)}, u32[]{:S(2)}, u32[]{:S(2)}) collective-permute-start(bf16[16,8192]{1,0:T(8,128)(2,1)S(1)} %shard_map.111.refs_3_.rows_ref.refs_0_), channel_id=1, source_target_pairs={{0,1},{1,0},{2,3},{3,2},{4,5},{5,4},{6,7},{7,6},{8,9},{9,8},{10,11... | collective-permute-start | bytes 786440 | tf_op jit(solution)/shard_map/ppermute | solution.py:22
  36.8 6.3 %collective-permute-start.7 = (bf16[16,8192]{1,0:T(8,128)(2,1)S(1)}, bf16[16,8192]{1,0:T(8,128)(2,1)S(1)}, u32[]{:S(2)}, u32[]{:S(2)}) collective-permute-start(bf16[16,8192]{1,0:T(8,128)(2,1)S(1)} %collective-permute-done.2.refs_1_), channel_id=1, source_target_pairs={{0,1},{1,0},{2,3},{3,2},{4,5},{5,4},{6,7},{7,6},{8,9},{9,8},{10,11... | collective-permute-start | bytes 786440 | tf_op jit(solution)/shard_map/ppermute | solution.py:22
  40.1 3.0 %collective-permute-start.4 = (bf16[16,8192]{1,0:T(8,128)(2,1)S(1)}, bf16[16,8192]{1,0:T(8,128)(2,1)S(1)}, u32[]{:S(2)}, u32[]{:S(2)}) collective-permute-start(bf16[16,8192]{1,0:T(8,128)(2,1)S(1)} %collective-permute-done.3.refs_6_), channel_id=1, source_target_pairs={{0,1},{1,0},{2,3},{3,2},{4,5},{5,4},{6,7},{7,6},{8,9},{9,8},{10,11... | collective-permute-start | bytes 786440 | tf_op jit(solution)/shard_map/ppermute | solution.py:22
  43.0 1.5 %collective-permute-start.8 = (bf16[16,8192]{1,0:T(8,128)(2,1)S(1)}, bf16[16,8192]{1,0:T(8,128)(2,1)S(1)}, u32[]{:S(2)}, u32[]{:S(2)}) collective-permute-start(bf16[16,8192]{1,0:T(8,128)(2,1)S(1)} %collective-permute-done.5.refs_3_), channel_id=1, source_target_pairs={{0,1},{1,0},{2,3},{3,2},{4,5},{5,4},{6,7},{7,6},{8,9},{9,8},{10,11... | collective-permute-start | bytes 786440 | tf_op jit(solution)/shard_map/ppermute | solution.py:22
  47.2 1.6 %collective-permute-start.12 = (bf16[16,8192]{1,0:T(8,128)(2,1)S(1)}, bf16[16,8192]{1,0:T(8,128)(2,1)S(1)}, u32[]{:S(2)}, u32[]{:S(2)}) collective-permute-start(bf16[16,8192]{1,0:T(8,128)(2,1)S(1)} %get-tuple-element.22), channel_id=1, source_target_pairs={{0,1},{1,0},{2,3},{3,2},{4,5},{5,4},{6,7},{7,6},{8,9},{9,8},{10,11... | collective-permute-start | bytes 786440 | tf_op jit(solution)/shard_map/ppermute | solution.py:22
  47.5 3.6 %collective-permute-start.9 = (bf16[48,8192]{1,0:T(8,128)(2,1)S(1)}, bf16[48,8192]{1,0:T(8,128)(2,1)S(1)}, u32[]{:S(2)}, u32[]{:S(2)}) collective-permute-start(bf16[48,8192]{1,0:T(8,128)(2,1)S(1)} %get-tuple-element.21), channel_id=1, source_target_pairs={{0,1},{1,0},{2,3},{3,2},{4,5},{5,4},{6,7},{7,6},{8,9},{9,8},{10,11... | collective-permute-start | bytes 2359304 | tf_op jit(solution)/shard_map/ppermute | solution.py:22
  48.9 6.4 %collective-permute-start.13 = (bf16[16,8192]{1,0:T(8,128)(2,1)S(1)}, bf16[16,8192]{1,0:T(8,128)(2,1)S(1)}, u32[]{:S(2)}, u32[]{:S(2)}) collective-permute-start(bf16[16,8192]{1,0:T(8,128)(2,1)S(1)} %add_convert_fusion), channel_id=1, source_target_pairs={{0,34},{1,3},{2,0},{3,33},{32,2},{33,35},{34,32},{35,1},{4,38},{5,... | collective-permute-start | bytes 786440 | tf_op jit(solution)/shard_map/ppermute | solution.py:101
  51.2 7.5 %collective-permute-start.10 = (bf16[16,8192]{1,0:T(8,128)(2,1)S(1)}, bf16[16,8192]{1,0:T(8,128)(2,1)S(1)}, u32[]{:S(2)}, u32[]{:S(2)}) collective-permute-start(bf16[16,8192]{1,0:T(8,128)(2,1)S(1)} %slice.45), channel_id=1, source_target_pairs={{0,34},{1,3},{2,0},{3,33},{32,2},{33,35},{34,32},{35,1},{4,38},{5,... | collective-permute-start | bytes 786440 | tf_op jit(solution)/shard_map/ppermute | solution.py:101
  55.4 7.2 %collective-permute-start.14 = (bf16[16,8192]{1,0:T(8,128)(2,1)S(1)}, bf16[16,8192]{1,0:T(8,128)(2,1)S(1)}, u32[]{:S(2)}, u32[]{:S(2)}) collective-permute-start(bf16[16,8192]{1,0:T(8,128)(2,1)S(1)} %fusion), channel_id=1, source_target_pairs={{0,34},{1,3},{2,0},{3,33},{32,2},{33,35},{34,32},{35,1},{4,38},{5,... | collective-permute-start | bytes 786440 | tf_op jit(solution)/shard_map/ppermute | solution.py:101
  58.7 3.9 %collective-permute-start.11 = (bf16[16,8192]{1,0:T(8,128)(2,1)S(1)}, bf16[16,8192]{1,0:T(8,128)(2,1)S(1)}, u32[]{:S(2)}, u32[]{:S(2)}) collective-permute-start(bf16[16,8192]{1,0:T(8,128)(2,1)S(1)} %collective-permute-done.10), channel_id=1, source_target_pairs={{0,1},{1,0},{2,3},{3,2},{4,5},{5,4},{6,7},{7,6},{8,9},{9,8},{10,11... | collective-permute-start | bytes 786440 | tf_op jit(solution)/shard_map/ppermute | solution.py:22
  77.7 5.2 %collective-permute-start.15 = (f32[1,8192]{1,0:T(1,128)S(1)}, f32[1,8192]{1,0:T(1,128)S(1)}, u32[]{:S(2)}, u32[]{:S(2)}) collective-permute-start(f32[1,8192]{1,0:T(1,128)S(1)} %get-tuple-element.24), channel_id=1, source_target_pairs={{0,192},{64,128},{128,64},{192,0},{1,193},{65,129},{129,65},{193,1... | collective-permute-start | bytes 98312 | tf_op jit(solution)/shard_map/ppermute | solution.py:30
  80.5 5.4 %collective-permute-start.16 = (f32[1,8192]{1,0:T(1,128)S(1)}, f32[1,8192]{1,0:T(1,128)S(1)}, u32[]{:S(2)}, u32[]{:S(2)}) collective-permute-start(f32[1,8192]{1,0:T(1,128)S(1)} %get-tuple-element.23), channel_id=1, source_target_pairs={{0,128},{64,192},{128,0},{192,64},{1,129},{65,193},{129,1},{193,65... | collective-permute-start | bytes 98312 | tf_op jit(solution)/shard_map/ppermute | solution.py:34

commit v6 on v5

--- a/solution.py
+++ b/solution.py
@@ -131,7 +131,7 @@
 def load_kernel(*refs):
     sources, targets, token_ref, sems = refs[:3], refs[4:7], refs[7], refs[8]
     copies = []
-    parts = 2
+    parts = 13
     for w, (source, target) in enumerate(zip(sources, targets)):
         size = source.shape[0] // parts
         for i in range(parts):
@@ -151,7 +151,7 @@
         out_shape=tuple(pltpu.VMEM(w.shape, w.dtype) for w in weights) + (pltpu.VMEM((8, 128), jnp.float32),),
         in_specs=[pl.BlockSpec(memory_space=pltpu.HBM)] * 3 + [pl.BlockSpec(memory_space=pl.ANY)],
         out_specs=(in_vmem,) * 4,
-        scratch_shapes=[pltpu.SemaphoreType.DMA((6,))],
+        scratch_shapes=[pltpu.SemaphoreType.DMA((39,))],
         compiler_params=pltpu.CompilerParams(vmem_limit_bytes=12 << 20),
     )(*(in_hbm(w) for w in weights), rows)
 

time: 86.8 us -> 86.6 us (level)
  transfers between devices with their start and end apart: 17 -> 17, of which waited for: 11 -> 10; matrix products, arithmetic and copies ran while one was open for 0% -> 0% of each run, Pallas kernels for 5% -> 5%
where the time goes in v6:
time: 86.6 us; the launch traced here: 86.4 us
  blocking collectives  31.6 us (36%)
  waiting for transfers between devices  25 us (29%)
  starting transfers between devices  18.2 us (21%)
  Pallas kernels  9.15 us (11%)
  other arithmetic  1.28 us (1%)
    all_to_all x1, blocking collectives, gathered_blocks(): pairs = lax.all_to_all(copies, 'z', 0, 0, tiled=True)  17.1 us
    all_to_all x1, blocking collectives, returned_rows(): arrived = lax.all_to_all(pieces, 'z', 0, 0, tiled=True)  14.5 us
    ppermute x6, waiting for transfers between devices, along_x(): return lax.ppermute(value, X + ('c',), pairs)  12.5 us
    ppermute x6, starting transfers between devices, along_x(): return lax.ppermute(value, X + ('c',), pairs)  11.4 us
    ppermute x2, waiting for transfers between devices, opposite(): return lax.ppermute(value, 'y', [(i, (i + 2) % 4) for i in range(4)])  5.26 us
    ppermute x2, starting transfers between devices, mirrored(): return lax.ppermute(value, 'y', [(i, 3 - i) for i in range(4)])  4.86 us
    ppermute x2, waiting for transfers between devices, mirrored(): return lax.ppermute(value, 'y', [(i, 3 - i) for i in range(4)])  4.68 us
    pallas_call x1, Pallas kernels, loaded(): pl.pallas_call(load_kernel, out_shape=tuple((pltpu.VMEM(w.shape, w.dtype)...  4.22 us
  transfers between devices with their start and end apart: 17, of which 10 were waited for; matrix products, arithmetic and copies ran while one was open for 0% of the time, Pallas kernels for 5%

profile of v6, /device:TPU:24, one launch (start us, length us, event | category | flops | bytes accessed | tf_op | source)
XLA Modules:
  0.0 86.4 jit_solution(9107593033504905191)
XLA Ops:
  0.7 2.1 %shard_map.109 = (f32[1,8192]{1,0:T(1,128)S(1)}, bf16[1,8192]{1,0:T(2,128)(2,1)S(1)}) custom-call(s32[1,1]{1,0:T(1,128)S(6)} %copy.12.length_ref, bf16[768,512]{1,0:T(8,128)(2,1)} %bitcast.15, bf16[768,512]{1,0:T(8,128)(2,1)} %bitcast.16, bf16[1,8192]{1,0:T(2,128)(2,1)} %bitcast.17, bf16[1,512]{1,0:T(2,128)(2,1)} %bitcast.20, bf16[1,512]{1,0:T(2,128)(2,1)} %bitcast.21, ...), custom_call_target="tpu_custom_call" | custom-call | tf_op jit(solution)/shard_map/pallas_call | solution.py:290
  2.7 2.0 %collective-permute-start = (bf16[1,8192]{1,0:T(2,128)(2,1)S(1)}, bf16[1,8192]{1,0:T(2,128)(2,1)S(1)}, u32[]{:S(2)}, u32[]{:S(2)}) collective-permute-start(bf16[1,8192]{1,0:T(2,128)(2,1)S(1)} %get-tuple-element.15), channel_id=1, source_target_pairs={{0,192},{64,128},{128,64},{192,0},{1,193},{65,129},{129,65},{193,1... | collective-permute-start | bytes 49160 | tf_op jit(solution)/shard_map/ppermute | solution.py:30
  4.8 0.9 collective-permute-start.1
  5.6 2.3 %collective-permute-done.near_ref = bf16[1,8192]{1,0:T(2,128)(2,1)S(1)} collective-permute-done((bf16[1,8192]{1,0:T(2,128)(2,1)S(1)}, bf16[1,8192]{1,0:T(2,128)(2,1)S(1)}, u32[]{:S(2)}, u32[]{:S(2)}) %collective-permute-start) | collective-permute-done | bytes 16416 | tf_op jit(solution)/shard_map/ppermute | solution.py:30
  7.9 2.3 %collective-permute-done.1.far_ref = bf16[1,8192]{1,0:T(2,128)(2,1)S(1)} collective-permute-done((bf16[1,8192]{1,0:T(2,128)(2,1)S(1)}, bf16[1,8192]{1,0:T(2,128)(2,1)S(1)}, u32[]{:S(2)}, u32[]{:S(2)}) %collective-permute-start.1) | collective-permute-done | bytes 16416 | tf_op jit(solution)/shard_map/ppermute | solution.py:34
  10.2 17.1 %all_to_all.10.pairs_ref = bf16[8,2,8192]{2,1,0:T(2,128)(2,1)S(1)} all-to-all(bf16[8,2,8192]{2,1,0:T(2,128)(2,1)S(1)} %shard_map.110), channel_id=1, replica_groups=mesh['y'=4,'xh'=2,'z'=8,'xl'=2,'c'=2] {'z'}, dimensions={0} | all-to-all | bytes 524288 | tf_op jit(solution)/shard_map/all_to_all | solution.py:106
  27.4 0.1 shard_map.111.refs_3_.rows_ref.refs_0_
  27.5 1.6 %collective-permute-start.2 = (bf16[16,8192]{1,0:T(8,128)(2,1)S(1)}, bf16[16,8192]{1,0:T(8,128)(2,1)S(1)}, u32[]{:S(2)}, u32[]{:S(2)}) collective-permute-start(bf16[16,8192]{1,0:T(8,128)(2,1)S(1)} %shard_map.111.refs_3_.rows_ref.refs_0_), channel_id=1, source_target_pairs={{0,2},{1,35},{2,32},{3,1},{32,34},{33,3},{34,0},{35,33},{4,6},{5,3... | collective-permute-start | bytes 786440 | tf_op jit(solution)/shard_map/ppermute | solution.py:101
  29.1 4.2 %shard_map.112 = (bf16[208,8192]{1,0:T(8,128)(2,1)S(1)}, bf16[208,8192]{1,0:T(8,128)(2,1)S(1)}, bf16[208,8192]{1,0:T(8,128)(2,1)S(1)}, f32[8,128]{1,0:T(8,128)S(1)}) custom-call(bf16[208,8192]{1,0:T(8,128)(2,1)} %bitcast.12, bf16[208,8192]{1,0:T(8,128)(2,1)} %bitcast.13, bf16[208,8192]{1,0:T(8,128)(2,1)} %bitcast.14, ...), custom_call_target="tpu_custom_call" | custom-call | tf_op jit(solution)/shard_map/pallas_call | solution.py:149
  33.3 1.8 %collective-permute-start.3 = (bf16[16,8192]{1,0:T(8,128)(2,1)S(1)}, bf16[16,8192]{1,0:T(8,128)(2,1)S(1)}, u32[]{:S(2)}, u32[]{:S(2)}) collective-permute-start(bf16[16,8192]{1,0:T(8,128)(2,1)S(1)} %shard_map.113), channel_id=1, source_target_pairs={{0,34},{1,3},{2,0},{3,33},{32,2},{33,35},{34,32},{35,1},{4,38},{5,... | collective-permute-start | bytes 786440 | tf_op jit(solution)/shard_map/ppermute | solution.py:101
  35.2 0.0 collective-permute-done.2.refs_1_
  35.2 1.3 %collective-permute-start.5 = (bf16[16,8192]{1,0:T(8,128)(2,1)S(1)}, bf16[16,8192]{1,0:T(8,128)(2,1)S(1)}, u32[]{:S(2)}, u32[]{:S(2)}) collective-permute-start(bf16[16,8192]{1,0:T(8,128)(2,1)S(1)} %collective-permute-done.2.refs_1_), channel_id=1, source_target_pairs={{0,2},{1,35},{2,32},{3,1},{32,34},{33,3},{34,0},{35,33},{4,6},{5,3... | collective-permute-start | bytes 786440 | tf_op jit(solution)/shard_map/ppermute | solution.py:101
  36.5 0.0 collective-permute-start.6
  36.5 0.5 collective-permute-start.7
  37.0 3.2 %collective-permute-done.3.refs_6_ = bf16[16,8192]{1,0:T(8,128)(2,1)S(1)} collective-permute-done((bf16[16,8192]{1,0:T(8,128)(2,1)S(1)}, bf16[16,8192]{1,0:T(8,128)(2,1)S(1)}, u32[]{:S(2)}, u32[]{:S(2)}) %collective-permute-start.3) | collective-permute-done | bytes 262176 | tf_op jit(solution)/shard_map/ppermute | solution.py:101
  40.3 0.0 collective-permute-start.4
  40.3 2.5 %collective-permute-done.5.refs_3_ = bf16[16,8192]{1,0:T(8,128)(2,1)S(1)} collective-permute-done((bf16[16,8192]{1,0:T(8,128)(2,1)S(1)}, bf16[16,8192]{1,0:T(8,128)(2,1)S(1)}, u32[]{:S(2)}, u32[]{:S(2)}) %collective-permute-start.5) | collective-permute-done | bytes 262176 | tf_op jit(solution)/shard_map/ppermute | solution.py:101
  42.8 0.0 collective-permute-start.8
  42.8 0.0 collective-permute-done.6.refs_4_
  42.8 0.0 collective-permute-done.4.refs_2_
  42.8 0.0 collective-permute-done.7.refs_5_
  42.8 1.5 %collective-permute-done.8.refs_7_ = bf16[16,8192]{1,0:T(8,128)(2,1)S(1)} collective-permute-done((bf16[16,8192]{1,0:T(8,128)(2,1)S(1)}, bf16[16,8192]{1,0:T(8,128)(2,1)S(1)}, u32[]{:S(2)}, u32[]{:S(2)}) %collective-permute-start.8) | collective-permute-done | bytes 262176 | tf_op jit(solution)/shard_map/ppermute | solution.py:22
  44.3 2.7 %shard_map.114 = (f32[64,8192]{1,0:T(8,128)S(1)}, bf16[48,8192]{1,0:T(8,128)(2,1)S(1)}, bf16[16,8192]{1,0:T(8,128)(2,1)S(1)}) custom-call(bf16[16,8192]{1,0:T(8,128)(2,1)S(1)} %shard_map.111.refs_3_.rows_ref.refs_0_, bf16[16,8192]{1,0:T(8,128)(2,1)S(1)} %collective-permute-done.2.refs_1_, bf16[16,8192]{1,0:T(8,128)(2,1)S(1)} %collective-permute-done.4.refs_2_, ...), custom_call_target="tpu_custom_call" | custom-call | tf_op jit(solution)/shard_map/pallas_call | solution.py:185
  47.0 0.2 collective-permute-start.12
  47.2 0.4 collective-permute-start.9
  47.6 1.0 %collective-permute-done.12 = bf16[16,8192]{1,0:T(8,128)(2,1)S(1)} collective-permute-done((bf16[16,8192]{1,0:T(8,128)(2,1)S(1)}, bf16[16,8192]{1,0:T(8,128)(2,1)S(1)}, u32[]{:S(2)}, u32[]{:S(2)}) %collective-permute-start.12) | collective-permute-done | bytes 262176 | tf_op jit(solution)/shard_map/ppermute | solution.py:22
  48.6 0.1 add_convert_fusion
  48.7 2.1 %collective-permute-start.13 = (bf16[16,8192]{1,0:T(8,128)(2,1)S(1)}, bf16[16,8192]{1,0:T(8,128)(2,1)S(1)}, u32[]{:S(2)}, u32[]{:S(2)}) collective-permute-start(bf16[16,8192]{1,0:T(8,128)(2,1)S(1)} %add_convert_fusion), channel_id=1, source_target_pairs={{0,34},{1,3},{2,0},{3,33},{32,2},{33,35},{34,32},{35,1},{4,38},{5,... | collective-permute-start | bytes 786440 | tf_op jit(solution)/shard_map/ppermute | solution.py:101
  50.8 0.0 collective-permute-done.9
  50.8 0.2 convert_add_fusion
  51.0 1.2 %collective-permute-start.10 = (bf16[16,8192]{1,0:T(8,128)(2,1)S(1)}, bf16[16,8192]{1,0:T(8,128)(2,1)S(1)}, u32[]{:S(2)}, u32[]{:S(2)}) collective-permute-start(bf16[16,8192]{1,0:T(8,128)(2,1)S(1)} %slice.45), channel_id=1, source_target_pairs={{0,34},{1,3},{2,0},{3,33},{32,2},{33,35},{34,32},{35,1},{4,38},{5,... | collective-permute-start | bytes 786440 | tf_op jit(solution)/shard_map/ppermute | solution.py:101
  52.2 2.9 %collective-permute-done.13 = bf16[16,8192]{1,0:T(8,128)(2,1)S(1)} collective-permute-done((bf16[16,8192]{1,0:T(8,128)(2,1)S(1)}, bf16[16,8192]{1,0:T(8,128)(2,1)S(1)}, u32[]{:S(2)}, u32[]{:S(2)}) %collective-permute-start.13) | collective-permute-done | bytes 262176 | tf_op jit(solution)/shard_map/ppermute | solution.py:101
  55.2 3.3 %collective-permute-start.14 = (bf16[16,8192]{1,0:T(8,128)(2,1)S(1)}, bf16[16,8192]{1,0:T(8,128)(2,1)S(1)}, u32[]{:S(2)}, u32[]{:S(2)}) collective-permute-start(bf16[16,8192]{1,0:T(8,128)(2,1)S(1)} %fusion), channel_id=1, source_target_pairs={{0,34},{1,3},{2,0},{3,33},{32,2},{33,35},{34,32},{35,1},{4,38},{5,... | collective-permute-start | bytes 786440 | tf_op jit(solution)/shard_map/ppermute | solution.py:101
  58.5 0.0 collective-permute-done.10
  58.5 0.0 collective-permute-start.11
  58.5 3.9 %collective-permute-done.14 = bf16[16,8192]{1,0:T(8,128)(2,1)S(1)} collective-permute-done((bf16[16,8192]{1,0:T(8,128)(2,1)S(1)}, bf16[16,8192]{1,0:T(8,128)(2,1)S(1)}, u32[]{:S(2)}, u32[]{:S(2)}) %collective-permute-start.14) | collective-permute-done | bytes 262176 | tf_op jit(solution)/shard_map/ppermute | solution.py:101
  62.4 0.0 collective-permute-done.11
  62.4 0.1 fusion.2
  62.5 0.2 reshape.34
  62.7 14.5 %all_to_all.11 = bf16[8,2,8192]{2,1,0:T(2,128)(2,1)S(1)} all-to-all(bf16[8,2,8192]{2,1,0:T(2,128)(2,1)S(1)} %reshape.34), channel_id=1, replica_groups=mesh['y'=4,'xh'=2,'z'=8,'xl'=2,'c'=2] {'z'}, dimensions={0} | all-to-all | bytes 524288 | tf_op jit(solution)/shard_map/all_to_all | solution.py:126
  77.2 0.2 convert_reduce_fusion
  77.4 0.1 fusion.4
  77.5 2.8 %collective-permute-start.15 = (f32[1,8192]{1,0:T(1,128)S(1)}, f32[1,8192]{1,0:T(1,128)S(1)}, u32[]{:S(2)}, u32[]{:S(2)}) collective-permute-start(f32[1,8192]{1,0:T(1,128)S(1)} %get-tuple-element.24), channel_id=1, source_target_pairs={{0,192},{64,128},{128,64},{192,0},{1,193},{65,129},{129,65},{193,1... | collective-permute-start | bytes 98312 | tf_op jit(solution)/shard_map/ppermute | solution.py:30
  80.3 0.0 collective-permute-start.16
  80.3 2.4 %collective-permute-done.15 = f32[1,8192]{1,0:T(1,128)S(1)} collective-permute-done((f32[1,8192]{1,0:T(1,128)S(1)}, f32[1,8192]{1,0:T(1,128)S(1)}, u32[]{:S(2)}, u32[]{:S(2)}) %collective-permute-start.15) | collective-permute-done | bytes 32800 | tf_op jit(solution)/shard_map/ppermute | solution.py:30
  82.7 3.0 %collective-permute-done.16 = f32[1,8192]{1,0:T(1,128)S(1)} collective-permute-done((f32[1,8192]{1,0:T(1,128)S(1)}, f32[1,8192]{1,0:T(1,128)S(1)}, u32[]{:S(2)}, u32[]{:S(2)}) %collective-permute-start.16) | collective-permute-done | bytes 32800 | tf_op jit(solution)/shard_map/ppermute | solution.py:34
  85.7 0.7 fusion.3
  (4 shorter events, 0.1 us)
Async XLA Ops:
  2.7 5.2 %collective-permute-start = (bf16[1,8192]{1,0:T(2,128)(2,1)S(1)}, bf16[1,8192]{1,0:T(2,128)(2,1)S(1)}, u32[]{:S(2)}, u32[]{:S(2)}) collective-permute-start(bf16[1,8192]{1,0:T(2,128)(2,1)S(1)} %get-tuple-element.15), channel_id=1, source_target_pairs={{0,192},{64,128},{128,64},{192,0},{1,193},{65,129},{129,65},{193,1... | collective-permute-start | bytes 49160 | tf_op jit(solution)/shard_map/ppermute | solution.py:30
  4.8 5.4 %collective-permute-start.1 = (bf16[1,8192]{1,0:T(2,128)(2,1)S(1)}, bf16[1,8192]{1,0:T(2,128)(2,1)S(1)}, u32[]{:S(2)}, u32[]{:S(2)}) collective-permute-start(bf16[1,8192]{1,0:T(2,128)(2,1)S(1)} %get-tuple-element.15), channel_id=1, source_target_pairs={{0,128},{64,192},{128,0},{192,64},{1,129},{65,193},{129,1},{193,65... | collective-permute-start | bytes 49160 | tf_op jit(solution)/shard_map/ppermute | solution.py:34
  27.5 7.7 %collective-permute-start.2 = (bf16[16,8192]{1,0:T(8,128)(2,1)S(1)}, bf16[16,8192]{1,0:T(8,128)(2,1)S(1)}, u32[]{:S(2)}, u32[]{:S(2)}) collective-permute-start(bf16[16,8192]{1,0:T(8,128)(2,1)S(1)} %shard_map.111.refs_3_.rows_ref.refs_0_), channel_id=1, source_target_pairs={{0,2},{1,35},{2,32},{3,1},{32,34},{33,3},{34,0},{35,33},{4,6},{5,3... | collective-permute-start | bytes 786440 | tf_op jit(solution)/shard_map/ppermute | solution.py:101
  33.3 6.9 %collective-permute-start.3 = (bf16[16,8192]{1,0:T(8,128)(2,1)S(1)}, bf16[16,8192]{1,0:T(8,128)(2,1)S(1)}, u32[]{:S(2)}, u32[]{:S(2)}) collective-permute-start(bf16[16,8192]{1,0:T(8,128)(2,1)S(1)} %shard_map.113), channel_id=1, source_target_pairs={{0,34},{1,3},{2,0},{3,33},{32,2},{33,35},{34,32},{35,1},{4,38},{5,... | collective-permute-start | bytes 786440 | tf_op jit(solution)/shard_map/ppermute | solution.py:101
  35.2 7.6 %collective-permute-start.5 = (bf16[16,8192]{1,0:T(8,128)(2,1)S(1)}, bf16[16,8192]{1,0:T(8,128)(2,1)S(1)}, u32[]{:S(2)}, u32[]{:S(2)}) collective-permute-start(bf16[16,8192]{1,0:T(8,128)(2,1)S(1)} %collective-permute-done.2.refs_1_), channel_id=1, source_target_pairs={{0,2},{1,35},{2,32},{3,1},{32,34},{33,3},{34,0},{35,33},{4,6},{5,3... | collective-permute-start | bytes 786440 | tf_op jit(solution)/shard_map/ppermute | solution.py:101
  36.5 6.3 %collective-permute-start.6 = (bf16[16,8192]{1,0:T(8,128)(2,1)S(1)}, bf16[16,8192]{1,0:T(8,128)(2,1)S(1)}, u32[]{:S(2)}, u32[]{:S(2)}) collective-permute-start(bf16[16,8192]{1,0:T(8,128)(2,1)S(1)} %shard_map.111.refs_3_.rows_ref.refs_0_), channel_id=1, source_target_pairs={{0,1},{1,0},{2,3},{3,2},{4,5},{5,4},{6,7},{7,6},{8,9},{9,8},{10,11... | collective-permute-start | bytes 786440 | tf_op jit(solution)/shard_map/ppermute | solution.py:22
  36.5 6.3 %collective-permute-start.7 = (bf16[16,8192]{1,0:T(8,128)(2,1)S(1)}, bf16[16,8192]{1,0:T(8,128)(2,1)S(1)}, u32[]{:S(2)}, u32[]{:S(2)}) collective-permute-start(bf16[16,8192]{1,0:T(8,128)(2,1)S(1)} %collective-permute-done.2.refs_1_), channel_id=1, source_target_pairs={{0,1},{1,0},{2,3},{3,2},{4,5},{5,4},{6,7},{7,6},{8,9},{9,8},{10,11... | collective-permute-start | bytes 786440 | tf_op jit(solution)/shard_map/ppermute | solution.py:22
  40.3 2.5 %collective-permute-start.4 = (bf16[16,8192]{1,0:T(8,128)(2,1)S(1)}, bf16[16,8192]{1,0:T(8,128)(2,1)S(1)}, u32[]{:S(2)}, u32[]{:S(2)}) collective-permute-start(bf16[16,8192]{1,0:T(8,128)(2,1)S(1)} %collective-permute-done.3.refs_6_), channel_id=1, source_target_pairs={{0,1},{1,0},{2,3},{3,2},{4,5},{5,4},{6,7},{7,6},{8,9},{9,8},{10,11... | collective-permute-start | bytes 786440 | tf_op jit(solution)/shard_map/ppermute | solution.py:22
  42.8 1.5 %collective-permute-start.8 = (bf16[16,8192]{1,0:T(8,128)(2,1)S(1)}, bf16[16,8192]{1,0:T(8,128)(2,1)S(1)}, u32[]{:S(2)}, u32[]{:S(2)}) collective-permute-start(bf16[16,8192]{1,0:T(8,128)(2,1)S(1)} %collective-permute-done.5.refs_3_), channel_id=1, source_target_pairs={{0,1},{1,0},{2,3},{3,2},{4,5},{5,4},{6,7},{7,6},{8,9},{9,8},{10,11... | collective-permute-start | bytes 786440 | tf_op jit(solution)/shard_map/ppermute | solution.py:22
  47.0 1.6 %collective-permute-start.12 = (bf16[16,8192]{1,0:T(8,128)(2,1)S(1)}, bf16[16,8192]{1,0:T(8,128)(2,1)S(1)}, u32[]{:S(2)}, u32[]{:S(2)}) collective-permute-start(bf16[16,8192]{1,0:T(8,128)(2,1)S(1)} %get-tuple-element.22), channel_id=1, source_target_pairs={{0,1},{1,0},{2,3},{3,2},{4,5},{5,4},{6,7},{7,6},{8,9},{9,8},{10,11... | collective-permute-start | bytes 786440 | tf_op jit(solution)/shard_map/ppermute | solution.py:22
  47.2 3.6 %collective-permute-start.9 = (bf16[48,8192]{1,0:T(8,128)(2,1)S(1)}, bf16[48,8192]{1,0:T(8,128)(2,1)S(1)}, u32[]{:S(2)}, u32[]{:S(2)}) collective-permute-start(bf16[48,8192]{1,0:T(8,128)(2,1)S(1)} %get-tuple-element.21), channel_id=1, source_target_pairs={{0,1},{1,0},{2,3},{3,2},{4,5},{5,4},{6,7},{7,6},{8,9},{9,8},{10,11... | collective-permute-start | bytes 2359304 | tf_op jit(solution)/shard_map/ppermute | solution.py:22
  48.7 6.4 %collective-permute-start.13 = (bf16[16,8192]{1,0:T(8,128)(2,1)S(1)}, bf16[16,8192]{1,0:T(8,128)(2,1)S(1)}, u32[]{:S(2)}, u32[]{:S(2)}) collective-permute-start(bf16[16,8192]{1,0:T(8,128)(2,1)S(1)} %add_convert_fusion), channel_id=1, source_target_pairs={{0,34},{1,3},{2,0},{3,33},{32,2},{33,35},{34,32},{35,1},{4,38},{5,... | collective-permute-start | bytes 786440 | tf_op jit(solution)/shard_map/ppermute | solution.py:101
  51.0 7.5 %collective-permute-start.10 = (bf16[16,8192]{1,0:T(8,128)(2,1)S(1)}, bf16[16,8192]{1,0:T(8,128)(2,1)S(1)}, u32[]{:S(2)}, u32[]{:S(2)}) collective-permute-start(bf16[16,8192]{1,0:T(8,128)(2,1)S(1)} %slice.45), channel_id=1, source_target_pairs={{0,34},{1,3},{2,0},{3,33},{32,2},{33,35},{34,32},{35,1},{4,38},{5,... | collective-permute-start | bytes 786440 | tf_op jit(solution)/shard_map/ppermute | solution.py:101
  55.2 7.2 %collective-permute-start.14 = (bf16[16,8192]{1,0:T(8,128)(2,1)S(1)}, bf16[16,8192]{1,0:T(8,128)(2,1)S(1)}, u32[]{:S(2)}, u32[]{:S(2)}) collective-permute-start(bf16[16,8192]{1,0:T(8,128)(2,1)S(1)} %fusion), channel_id=1, source_target_pairs={{0,34},{1,3},{2,0},{3,33},{32,2},{33,35},{34,32},{35,1},{4,38},{5,... | collective-permute-start | bytes 786440 | tf_op jit(solution)/shard_map/ppermute | solution.py:101
  58.5 3.9 %collective-permute-start.11 = (bf16[16,8192]{1,0:T(8,128)(2,1)S(1)}, bf16[16,8192]{1,0:T(8,128)(2,1)S(1)}, u32[]{:S(2)}, u32[]{:S(2)}) collective-permute-start(bf16[16,8192]{1,0:T(8,128)(2,1)S(1)} %collective-permute-done.10), channel_id=1, source_target_pairs={{0,1},{1,0},{2,3},{3,2},{4,5},{5,4},{6,7},{7,6},{8,9},{9,8},{10,11... | collective-permute-start | bytes 786440 | tf_op jit(solution)/shard_map/ppermute | solution.py:22
  77.5 5.2 %collective-permute-start.15 = (f32[1,8192]{1,0:T(1,128)S(1)}, f32[1,8192]{1,0:T(1,128)S(1)}, u32[]{:S(2)}, u32[]{:S(2)}) collective-permute-start(f32[1,8192]{1,0:T(1,128)S(1)} %get-tuple-element.24), channel_id=1, source_target_pairs={{0,192},{64,128},{128,64},{192,0},{1,193},{65,129},{129,65},{193,1... | collective-permute-start | bytes 98312 | tf_op jit(solution)/shard_map/ppermute | solution.py:30
  80.3 5.4 %collective-permute-start.16 = (f32[1,8192]{1,0:T(1,128)S(1)}, f32[1,8192]{1,0:T(1,128)S(1)}, u32[]{:S(2)}, u32[]{:S(2)}) collective-permute-start(f32[1,8192]{1,0:T(1,128)S(1)} %get-tuple-element.23), channel_id=1, source_target_pairs={{0,128},{64,192},{128,0},{192,64},{1,129},{65,193},{129,1},{193,65... | collective-permute-start | bytes 98312 | tf_op jit(solution)/shard_map/ppermute | solution.py:34
